TPU v7x, 32 devices: a whole 2x2x4 slice. The times are simulated.
32 devices in a mesh: gx: 4 (over y, x), gy: 4 (over z), gz: 2 (over core).
Axes of the slice: x: 2, y: 2, z: 4, core: 2. Of those that a mesh axis runs over, the one named last changes fastest.
Arguments:
- checkpoint: float32 [19, 8, 64, 256], P(None, 'gx', 'gy', 'gz'), may hold values from 0 to 1, as said below
- resistance: float32 [8, 64, 256], P('gx', 'gy', 'gz'), may hold values from 0.01 to 1
- solid: int32 [8, 64, 256], P('gx', 'gy', 'gz'), may hold values 0 or 1
- adjoint_final: float32 [19, 8, 64, 256], P(None, 'gx', 'gy', 'gz'), may hold values from -6 to 6
Outputs:
- adjoint_start: float32 [19, 8, 64, 256], P(None, 'gx', 'gy', 'gz')
- sensitivity: float32 [8, 64, 256], P('gx', 'gy', 'gz')
Inputs may be any that keep to these rules, and one draw needn't show every extreme that they name: `checkpoint`: every population is positive, near w_i times a density of order one.
All inputs are finite; a program needn't handle non-finite values. No bound on the sum of `solid` on one device may be relied on, other than what follows from the above.
Results may differ from a plain program's by a relative error of at most 0.0003.
Values sent between devices are 32-bit elements; how exact they have to be, the bound alone decides.
No kernel may reach another device: no remote copies, remote signals or barrier semaphores. Data moves between devices by JAX's collectives and lax.ppermute only.
A program may use at most 64 MiB of HBM per device.

v0:
```python
import functools

import jax
import jax.numpy as jnp
from jax import lax
from jax.experimental import pallas as pl
from jax.experimental.pallas import tpu as pltpu
from jax.sharding import PartitionSpec as P

STEPS = 4


VELOCITIES = (
    (0, 0, 0),
    (1, 0, 0),
    (-1, 0, 0),
    (0, 1, 0),
    (0, -1, 0),
    (0, 0, 1),
    (0, 0, -1),
    (1, 1, 0),
    (-1, -1, 0),
    (1, -1, 0),
    (-1, 1, 0),
    (1, 0, 1),
    (-1, 0, -1),
    (1, 0, -1),
    (-1, 0, 1),
    (0, 1, 1),
    (0, -1, -1),
    (0, 1, -1),
    (0, -1, 1),
)
WEIGHTS = (1.0 / 3.0,) + (1.0 / 18.0,) * 6 + (1.0 / 36.0,) * 12
OPPOSITE = tuple((VELOCITIES.index((-entry[0], -entry[1], -entry[2])) for entry in VELOCITIES))
RELAXATION = 0.8
BODY_FORCE = 0.01

Q = len(VELOCITIES)
KEEP = 1.0 - 1.0 / RELAXATION
PUSH = RELAXATION * BODY_FORCE
VMEM_LIMIT = 16 * 1024 * 1024

GROUP = 4
ROWS = 4
LAYERS = 2
HALO = 3
RES, SOL, ADJ = Q, Q + 1, Q + 2
FIELDS = Q + 2 + Q

FORWARD_UP = (
    [(3, i, -1) for i in range(Q)]
    + [(2, i, -2) for i in range(Q) if VELOCITIES[i][1] >= 0]
    + [(1, i, -3) for i in range(Q) if VELOCITIES[i][1] > 0]
    + [(3, RES, -1), (3, SOL, -1), (2, RES, -2), (2, SOL, -2)]
    + [(3, ADJ + i, -1) for i in range(Q) if VELOCITIES[i][1] < 0]
)
FORWARD_DOWN = (
    [(0, i, 4) for i in range(Q)]
    + [(1, i, 5) for i in range(Q) if VELOCITIES[i][1] <= 0]
    + [(2, i, 6) for i in range(Q) if VELOCITIES[i][1] < 0]
    + [(0, RES, 4), (0, SOL, 4), (1, RES, 5), (1, SOL, 5)]
    + [(0, ADJ + i, 4) for i in range(Q) if VELOCITIES[i][1] > 0]
)
BACKWARD_UP = (
    [(3, i, -1) for i in range(Q)]
    + [(2, i, -2) for i in range(Q) if VELOCITIES[i][1] <= 0]
    + [(1, i, -3) for i in range(Q) if VELOCITIES[i][1] < 0]
    + [(2, Q + j, -2) for j in range(4)]
)
BACKWARD_DOWN = (
    [(0, i, 4) for i in range(Q)]
    + [(1, i, 5) for i in range(Q) if VELOCITIES[i][1] >= 0]
    + [(2, i, 6) for i in range(Q) if VELOCITIES[i][1] > 0]
    + [(1, Q + j, 5) for j in range(4)]
)


def moments(f):
    plus = [f[i] + f[i + 1] for i in range(1, Q, 2)]
    less = [f[i] - f[i + 1] for i in range(1, Q, 2)]
    density = f[0] + ((plus[0] + plus[1]) + (plus[2] + plus[3])) + ((plus[4] + plus[5]) + (plus[6] + (plus[7] + plus[8])))
    first = less[0] + ((less[3] + less[4]) + (less[5] + less[6]))
    second = less[1] + ((less[3] - less[4]) + (less[7] + less[8]))
    third = less[2] + ((less[5] - less[6]) + (less[7] - less[8]))
    inverse = 1.0 / density
    return density, first * inverse, second * inverse, third * inverse


def along(i, x, y, z):
    total = None
    for sign, part in zip(VELOCITIES[i], (x, y, z)):
        if sign == 0:
            continue
        if total is None:
            total = part if sign > 0 else -part
        else:
            total = total + part if sign > 0 else total - part
    return total


def collide_lists(f, density, vx, vy, vz, resistance, solid):
    damp = 1.0 - RELAXATION * resistance
    ux, uy, uz = damp * vx + PUSH, damp * vy, damp * vz
    base = 1.0 - 1.5 * (ux * ux + uy * uy + uz * uz)
    scaled = {w: density * (w / RELAXATION) for w in sorted(set(WEIGHTS))}
    out = [jnp.where(solid, f[0], KEEP * f[0] + scaled[WEIGHTS[0]] * base)]
    for i in range(1, Q, 2):
        projected = along(i, ux, uy, uz)
        weight = scaled[WEIGHTS[i]]
        even = weight * (base + 4.5 * (projected * projected))
        odd = weight * (3.0 * projected)
        out.append(jnp.where(solid, f[i + 1], KEEP * f[i] + (even + odd)))
        out.append(jnp.where(solid, f[i], KEEP * f[i + 1] + (even - odd)))
    return out


def adjoint_lists(mu, density, vx, vy, vz, resistance, solid):
    damp = 1.0 - RELAXATION * resistance
    ux, uy, uz = damp * vx + PUSH, damp * vy, damp * vz
    plus = [mu[i] + mu[i + 1] for i in range(1, Q, 2)]
    less = [mu[i] - mu[i + 1] for i in range(1, Q, 2)]
    rest, axis, diagonal = (w / RELAXATION for w in (WEIGHTS[0], WEIGHTS[1], WEIGHTS[7]))
    xy, xz, yz = plus[3] + plus[4], plus[5] + plus[6], plus[7] + plus[8]
    zeroth = rest * mu[0] + axis * ((plus[0] + plus[1]) + plus[2]) + diagonal * ((xy + xz) + yz)
    nx = axis * less[0] + diagonal * ((less[3] + less[4]) + (less[5] + less[6]))
    ny = axis * less[1] + diagonal * ((less[3] - less[4]) + (less[7] + less[8]))
    nz = axis * less[2] + diagonal * ((less[5] - less[6]) + (less[7] - less[8]))
    nxx = axis * plus[0] + diagonal * (xy + xz)
    nyy = axis * plus[1] + diagonal * (xy + yz)
    nzz = axis * plus[2] + diagonal * (xz + yz)
    nxy = diagonal * (plus[3] - plus[4])
    nxz = diagonal * (plus[5] - plus[6])
    nyz = diagonal * (plus[7] - plus[8])
    tx = nxx * ux + nxy * uy + nxz * uz
    ty = nxy * ux + nyy * uy + nyz * uz
    tz = nxz * ux + nyz * uy + nzz * uz
    hx = 3.0 * (nx - ux * zeroth) + 9.0 * tx
    hy = 3.0 * (ny - uy * zeroth) + 9.0 * ty
    hz = 3.0 * (nz - uz * zeroth) + 9.0 * tz
    pulled = vx * hx + vy * hy + vz * hz
    square = ux * ux + uy * uy + uz * uz
    scalar = (
        zeroth * (1.0 - 1.5 * square)
        + 3.0 * (nx * ux + ny * uy + nz * uz)
        + 4.5 * (tx * ux + ty * uy + tz * uz)
        - damp * pulled
    )
    qx, qy, qz = damp * hx, damp * hy, damp * hz
    out = [jnp.where(solid, mu[0], KEEP * mu[0] + scalar)]
    for i in range(1, Q, 2):
        slope = along(i, qx, qy, qz)
        out.append(jnp.where(solid, mu[i + 1], KEEP * mu[i] + (scalar + slope)))
        out.append(jnp.where(solid, mu[i], KEEP * mu[i + 1] + (scalar - slope)))
    design = jnp.where(solid, 0.0, (-RELAXATION) * density * pulled)
    return out, design


def shifted(value, i, sign):
    first, _, third = VELOCITIES[i]
    if first:
        value = pltpu.roll(value, (sign * first) % value.shape[0], axis=0)
    if third:
        value = pltpu.roll(value, (sign * third) % value.shape[1], axis=1)
    return value


def block_of(number):
    gray = number ^ (number >> 1)
    odd = lax.axis_index("gy") % 2
    return gray + odd * (GROUP - 1 - 2 * gray)


def send_kernel(f_ref, r_ref, s_ref, a_ref, *refs):
    outs, blocks = refs[:GROUP], refs[GROUP]
    for half in range(2):
        rows = pl.ds(8 * half, 8)
        tiles = []
        for layer in range(LAYERS):
            f = [f_ref[i, layer, rows, :] for i in range(Q)]
            resistance, kind = r_ref[layer, rows, :], s_ref[layer, rows, :]
            out = collide_lists(f, *moments(f), resistance, kind == 1)
            out += [resistance, kind.astype(jnp.float32)]
            out += [a_ref[i, layer, rows, :] for i in range(Q)]
            tiles.append(out)
        for field in range(FIELDS):
            first, second = tiles[0][field], tiles[1][field]
            blocks[2 * half, field] = jnp.concatenate([first[:4], second[:4]], axis=0)
            blocks[2 * half + 1, field] = jnp.concatenate([first[4:], second[4:]], axis=0)
    here = lax.axis_index("gx")
    for k in range(GROUP):
        outs[k][...] = blocks[block_of(here ^ k)]


def turn_kernel(*refs):
    ins, (own, up, down, flat) = refs[:GROUP], refs[GROUP:]
    here = lax.axis_index("gx")
    for k in range(GROUP):
        start = 8 * (here ^ k)
        for field in range(FIELDS):
            flat[field, pl.ds(pl.multiple_of(start, 8), 8), :] = ins[k][field]
    for field in range(FIELDS):
        for row in range(ROWS):
            own[row, field] = flat[field, pl.ds(row, 8, stride=ROWS), :]
    for number, (row, field, _) in enumerate(FORWARD_UP):
        up[number] = own[row, field]
    for number, (row, field, _) in enumerate(FORWARD_DOWN):
        down[number] = own[row, field]


def forward_kernel(own_a, own_b, lo_a, lo_b, hi_a, hi_b, lam_ref, sens_ref, mom1, mom2, rs_ref, up, down, p0, p1, p2, a4):
    for side, own, lo, hi in ((0, own_a, lo_a, hi_a), (1, own_b, lo_b, hi_b)):
        lanes = slice(128 * side, 128 * side + 128)
        for row in range(ROWS):
            for i in range(Q):
                p0[row + 3, i, :, lanes] = own[row, i]
                a4[row + 1, i, :, lanes] = own[row, ADJ + i]
            for j in range(2):
                rs_ref[row + 2, j, :, lanes] = own[row, RES + j]
        for table, part in ((FORWARD_UP, lo), (FORWARD_DOWN, hi)):
            for number, (_, field, row) in enumerate(table):
                if field < Q:
                    p0[row + 3, field, :, lanes] = part[number]
                elif field < ADJ:
                    rs_ref[row + 2, field - RES, :, lanes] = part[number]
                else:
                    a4[row + 1, field - ADJ, :, lanes] = part[number]

    def pull(source, row):
        return [shifted(source[row + 1 - VELOCITIES[i][1], i], i, 1) for i in range(Q)]

    def first(row, _):
        f = pull(p0, row)
        moment = moments(f)
        for j in range(4):
            mom1[row, j] = moment[j]
        out = collide_lists(f, *moment, rs_ref[row, 0], rs_ref[row, 1] == 1.0)
        for i in range(Q):
            p1[row, i] = out[i]
        return 0

    lax.fori_loop(0, ROWS + 4, first, 0)

    def second(row, _):
        f = pull(p1, row)
        moment = moments(f)
        for j in range(4):
            mom2[row + 1, j] = moment[j]
        out = collide_lists(f, *moment, rs_ref[row + 1, 0], rs_ref[row + 1, 1] == 1.0)
        for i in range(Q):
            p2[row, i] = out[i]
        return 0

    lax.fori_loop(0, ROWS + 2, second, 0)

    def third(row, _):
        moment = moments(pull(p2, row))
        mu = [shifted(a4[row + 1 + VELOCITIES[i][1], i], i, -1) for i in range(Q)]
        out, design = adjoint_lists(mu, *moment, rs_ref[row + 2, 0], rs_ref[row + 2, 1] == 1.0)
        for i in range(Q):
            lam_ref[row, i] = out[i]
        sens_ref[row] = design[:, :128]
        return 0

    lax.fori_loop(0, ROWS, third, 0)
    for table, part in ((BACKWARD_UP, up), (BACKWARD_DOWN, down)):
        for number, (row, field, _) in enumerate(table):
            source = lam_ref[row, field, :, :128] if field < Q else mom2[row + 2, field - Q, :, :128]
            part[number] = source
    for row in (0, ROWS + 3):
        for j in range(4):
            mom2[row, j] = jnp.zeros((8, 256), jnp.float32)


def backward_kernel(lam_ref, sens_ref, mom1, mom2, rs_ref, lo_a, lo_b, hi_a, hi_b, *refs):
    outs, (l3, l2, l1, m2, flat) = refs[:GROUP], refs[GROUP:]
    for row in range(ROWS):
        for i in range(Q):
            l3[row + 3, i] = lam_ref[row, i]
    for row in range(ROWS + 4):
        for j in range(4):
            m2[row, j] = mom2[row, j]
    for side, lo, hi in ((0, lo_a, hi_a), (1, lo_b, hi_b)):
        lanes = slice(128 * side, 128 * side + 128)
        for table, part in ((BACKWARD_UP, lo), (BACKWARD_DOWN, hi)):
            for number, (_, field, row) in enumerate(table):
                if field < Q:
                    l3[row + 3, field, :, lanes] = part[number]
                else:
                    m2[row + 2, field - Q, :, lanes] = part[number]

    def pull(source, row):
        return [shifted(source[row + 1 + VELOCITIES[i][1], i], i, -1) for i in range(Q)]

    designs = flat.at[Q]

    def second(row, _):
        mu = pull(l3, row)
        out, design = adjoint_lists(mu, *[m2[row, j] for j in range(4)], rs_ref[row, 0], rs_ref[row, 1] == 1.0)
        for i in range(Q):
            l2[row, i] = out[i]
        l1[row, 0] = design
        return 0

    lax.fori_loop(0, ROWS + 4, second, 0)
    total = [sens_ref[row] + l1[row + 2, 0, :, :128] for row in range(ROWS)]

    def first(row, _):
        mu = pull(l2, row)
        out, design = adjoint_lists(
            mu, *[mom1[row + 1, j] for j in range(4)], rs_ref[row + 1, 0], rs_ref[row + 1, 1] == 1.0
        )
        for i in range(Q):
            l1[row, i] = out[i]
        m2[row, 0] = design
        return 0

    lax.fori_loop(0, ROWS + 2, first, 0)
    for row in range(ROWS):
        designs[pl.ds(row, 8, stride=ROWS), :] = total[row] + m2[row + 1, 0, :, :128]
        mu = pull(l1, row)
        for i in range(Q):
            flat[i, pl.ds(row, 8, stride=ROWS), :] = mu[i][:, :128]
    here = lax.axis_index("gx")
    for k in range(GROUP):
        start = 8 * (here ^ k)
        for i in range(Q + 1):
            outs[k][i] = flat[i, pl.ds(pl.multiple_of(start, 8), 8), :]


def finish_kernel(f_ref, r_ref, s_ref, *refs):
    ins, (lam_ref, sens_ref, blocks) = refs[:GROUP], refs[GROUP:]
    here = lax.axis_index("gx")
    for k in range(GROUP):
        blocks[block_of(here ^ k)] = ins[k][...]
    for half in range(2):
        rows = pl.ds(8 * half, 8)
        for layer in range(LAYERS):
            part = slice(4 * layer, 4 * layer + 4)
            tile = [
                jnp.concatenate([blocks[2 * half, i, part, :], blocks[2 * half + 1, i, part, :]], axis=0)
                for i in range(Q + 1)
            ]
            f = [f_ref[i, layer, rows, :] for i in range(Q)]
            out, design = adjoint_lists(tile[:Q], *moments(f), r_ref[layer, rows, :], s_ref[layer, rows, :] == 1)
            for i in range(Q):
                lam_ref[i, layer, rows, :] = out[i]
            sens_ref[layer, rows, :] = tile[Q] + design


def call(kernel, outs, scratch, *args):
    vmem = pl.BlockSpec(memory_space=pltpu.VMEM)
    return pl.pallas_call(
        kernel,
        out_shape=[jax.ShapeDtypeStruct(shape, jnp.float32) for shape in outs],
        in_specs=[vmem] * len(args),
        out_specs=[vmem] * len(outs),
        scratch_shapes=[pltpu.VMEM(shape, jnp.float32) for shape in scratch],
        compiler_params=pltpu.CompilerParams(vmem_limit_bytes=VMEM_LIMIT),
    )(*args)


def ring_pairs(planes, step):
    gray = [number ^ (number >> 1) for number in range(GROUP)]
    order = []
    for plane in range(planes):
        inside = sorted(range(GROUP), key=lambda number: gray[number])
        order += [(number, plane) for number in (inside if plane % 2 == 0 else inside[::-1])]
    pairs = []
    for at, (number, plane) in enumerate(order):
        other, beyond = order[(at + step) % len(order)]
        pairs.append((number * planes + plane, other * planes + beyond))
    return pairs


def fast_body(checkpoint, resistance, solid, adjoint_final):
    planes = lax.axis_size("gy")

    def trade(pieces):
        moved = [pieces[0]]
        for k in range(1, GROUP):
            moved.append(lax.ppermute(pieces[k], "gx", [(i, i ^ k) for i in range(GROUP)]))
        return moved

    def swap(value):
        return lax.ppermute(value, "gz", [(0, 1), (1, 0)])

    def ring(up, down):
        lo = lax.ppermute(up, ("gx", "gy"), ring_pairs(planes, 1))
        hi = lax.ppermute(down, ("gx", "gy"), ring_pairs(planes, -1))
        return lo, hi

    pieces = call(
        send_kernel, [(FIELDS, 8, 128)] * GROUP, [(GROUP, FIELDS, 8, 128)], checkpoint, resistance, solid, adjoint_final
    )
    pieces = trade(pieces)
    own, up, down = call(
        turn_kernel,
        [(ROWS, FIELDS, 8, 128), (len(FORWARD_UP), 8, 128), (len(FORWARD_DOWN), 8, 128)],
        [(FIELDS, 8 * ROWS, 128)],
        *pieces,
    )
    own_b = swap(own)
    lo, hi = ring(up, down)
    lo_b, hi_b = swap(lo), swap(hi)
    lam, sens, mom1, mom2, rs, up, down = call(
        forward_kernel,
        [
            (ROWS, Q, 8, 256),
            (ROWS, 8, 128),
            (ROWS + 4, 4, 8, 256),
            (ROWS + 4, 4, 8, 256),
            (ROWS + 4, 2, 8, 256),
            (len(BACKWARD_UP), 8, 128),
            (len(BACKWARD_DOWN), 8, 128),
        ],
        [(ROWS + 6, Q, 8, 256), (ROWS + 4, Q, 8, 256), (ROWS + 2, Q, 8, 256), (ROWS + 2, Q, 8, 256)],
        own,
        own_b,
        lo,
        lo_b,
        hi,
        hi_b,
    )
    lo, hi = ring(up, down)
    lo_b, hi_b = swap(lo), swap(hi)
    pieces = call(
        backward_kernel,
        [(Q + 1, 8, 128)] * GROUP,
        [
            (ROWS + 6, Q, 8, 256),
            (ROWS + 4, Q, 8, 256),
            (ROWS + 4, Q, 8, 256),
            (ROWS + 4, 4, 8, 256),
            (Q + 1, 8 * ROWS, 128),
        ],
        lam,
        sens,
        mom1,
        mom2,
        rs,
        lo,
        lo_b,
        hi,
        hi_b,
    )
    pieces = trade(pieces)
    return tuple(
        call(
            finish_kernel,
            [checkpoint.shape, resistance.shape],
            [(GROUP, Q + 1, 8, 128)],
            checkpoint,
            resistance,
            solid,
            *pieces,
        )
    )


def padded_2(shard, sides, width):
    for axis, dim in sides:
        count, length = (lax.axis_size(axis), shard.shape[dim])
        up = [(i, (i + 1) % count) for i in range(count)]
        down = [(j, i) for i, j in up]
        last = lax.slice_in_dim(shard, length - width, length, axis=dim)
        leading = lax.slice_in_dim(shard, 0, width, axis=dim)
        before = lax.ppermute(last, axis, up)
        after = lax.ppermute(leading, axis, down)
        shard = jnp.concatenate([before, shard, after], axis=dim)
    return shard


def collide(populations, resistance, solid):
    lattice = jnp.array(VELOCITIES, jnp.float32)
    weights = jnp.array(WEIGHTS, jnp.float32).reshape(-1, 1, 1, 1)
    density = jnp.sum(populations, axis=0)
    momentum = jnp.tensordot(lattice, populations, axes=([0], [0]), precision=lax.Precision.HIGHEST)
    nothing = jnp.zeros_like(density)
    push = jnp.stack([BODY_FORCE * density, nothing, nothing]) - resistance[None] * momentum
    velocity = (momentum + RELAXATION * push) / density[None]
    projected = jnp.tensordot(lattice, velocity, axes=([1], [0]), precision=lax.Precision.HIGHEST)
    speed_squared = jnp.sum(velocity * velocity, axis=0)
    equilibrium = (
        weights
        * density[None]
        * (1.0 + 3.0 * projected + 4.5 * projected * projected - 1.5 * speed_squared[None])
    )
    relaxed = populations - (populations - equilibrium) / RELAXATION
    reflected = jnp.stack([populations[other] for other in OPPOSITE])
    return jnp.where(solid[None] == 1, reflected, relaxed)


def transport(field, sign):
    padded = padded_2(field, (("gx", 1), ("gy", 2), ("gz", 3)), 1)
    first, second, third = (field.shape[1], field.shape[2], field.shape[3])
    pieces = []
    for number, entry in enumerate(VELOCITIES):
        start_a = 1 - sign * entry[0]
        start_b = 1 - sign * entry[1]
        start_c = 1 - sign * entry[2]
        pieces.append(
            padded[
                number,
                start_a : start_a + first,
                start_b : start_b + second,
                start_c : start_c + third,
            ]
        )
    return jnp.stack(pieces)


def general_body(checkpoint, resistance, solid, adjoint_final):
    states = [checkpoint]
    current = checkpoint
    for step in range(STEPS - 1):
        current = transport(collide(current, resistance, solid), 1)
        states.append(current)
    adjoint = adjoint_final
    sensitivity = jnp.zeros_like(resistance)
    for step in reversed(range(STEPS)):
        pulled = transport(adjoint, -1)

        def local_collide(populations, design):
            return collide(populations, design, solid)

        result, backward = jax.vjp(local_collide, states[step], resistance)
        adjoint, design_part = backward(pulled)
        sensitivity = sensitivity + design_part
    return (adjoint, sensitivity)


def body(checkpoint, resistance, solid, adjoint_final):
    fits = (
        lax.axis_size("gx") == GROUP
        and lax.axis_size("gz") == 2
        and resistance.shape == (LAYERS, GROUP * ROWS, 128)
    )
    chosen = fast_body if fits else general_body
    return chosen(checkpoint, resistance, solid, adjoint_final)


def solution(mesh):
    in_specs = (
        P(None, "gx", "gy", "gz"),
        P("gx", "gy", "gz"),
        P("gx", "gy", "gz"),
        P(None, "gx", "gy", "gz"),
    )
    out_specs = (P(None, "gx", "gy", "gz"), P("gx", "gy", "gz"))
    return jax.shard_map(body, mesh=mesh, in_specs=in_specs, out_specs=out_specs, check_vma=False)
```

profile of v0, /device:TPU:18, one launch (start us, length us, event | category | flops | bytes accessed | tf_op | source)
XLA Modules:
  0.0 52.6 jit_solution(13076837669721743198)
XLA Ops:
  0.6 0.0 copy-start
  0.6 1.0 %copy-done = f32[19,2,16,128]{3,2,1,0:T(8,128)S(1)} copy-done((f32[19,2,16,128]{3,2,1,0:T(8,128)S(1)}, f32[19,2,16,128]{3,2,1,0:T(8,128)}, u32[]{:S(2)}) %copy-start) | copy-done | bytes 311320
  1.6 0.0 copy-start.2
  1.6 1.0 %copy-done.2 = f32[19,2,16,128]{3,2,1,0:T(8,128)S(1)} copy-done((f32[19,2,16,128]{3,2,1,0:T(8,128)S(1)}, f32[19,2,16,128]{3,2,1,0:T(8,128)}, u32[]{:S(2)}) %copy-start.2) | copy-done | bytes 311320
  2.6 0.0 copy-start.3
  2.6 0.7 %copy-done.3 = f32[2,16,128]{2,1,0:T(8,128)S(1)} copy-done((f32[2,16,128]{2,1,0:T(8,128)S(1)}, f32[2,16,128]{2,1,0:T(8,128)}, u32[]{:S(2)}) %copy-start.3) | copy-done | bytes 16408
  3.3 0.0 copy-start.5
  3.3 0.7 %copy-done.5 = s32[2,16,128]{2,1,0:T(8,128)S(1)} copy-done((s32[2,16,128]{2,1,0:T(8,128)S(1)}, s32[2,16,128]{2,1,0:T(8,128)}, u32[]{:S(2)}) %copy-start.5) | copy-done | bytes 16408
  4.0 0.2 shard_map.59
  4.2 0.6 %collective-permute-start = (f32[40,8,128]{2,1,0:T(8,128)S(1)}, f32[40,8,128]{2,1,0:T(8,128)S(1)}, u32[]{:S(2)}, u32[]{:S(2)}) collective-permute-start(f32[40,8,128]{2,1,0:T(8,128)S(1)} %get-tuple-element.21), channel_id=1, source_target_pairs={{0,8},{8,0},{16,24},{24,16},{1,9},{9,1},{17,25},{25,17},{2,10},{10... | collective-permute-start | bytes 491528 | tf_op jit(solution)/shard_map/ppermute | solution.py:382
  4.8 1.5 %collective-permute-start.1 = (f32[40,8,128]{2,1,0:T(8,128)S(1)}, f32[40,8,128]{2,1,0:T(8,128)S(1)}, u32[]{:S(2)}, u32[]{:S(2)}) collective-permute-start(f32[40,8,128]{2,1,0:T(8,128)S(1)} %get-tuple-element.22), channel_id=1, source_target_pairs={{0,16},{8,24},{16,0},{24,8},{1,17},{9,25},{17,1},{25,9},{2,18},{10... | collective-permute-start | bytes 491528 | tf_op jit(solution)/shard_map/ppermute | solution.py:382
  6.3 1.4 %collective-permute-start.2 = (f32[40,8,128]{2,1,0:T(8,128)S(1)}, f32[40,8,128]{2,1,0:T(8,128)S(1)}, u32[]{:S(2)}, u32[]{:S(2)}) collective-permute-start(f32[40,8,128]{2,1,0:T(8,128)S(1)} %get-tuple-element.23), channel_id=1, source_target_pairs={{0,24},{8,16},{16,8},{24,0},{1,25},{9,17},{17,9},{25,1},{2,26},{10... | collective-permute-start | bytes 491528 | tf_op jit(solution)/shard_map/ppermute | solution.py:382
  7.8 3.6 %collective-permute-done.refs_1_ = f32[40,8,128]{2,1,0:T(8,128)S(1)} collective-permute-done((f32[40,8,128]{2,1,0:T(8,128)S(1)}, f32[40,8,128]{2,1,0:T(8,128)S(1)}, u32[]{:S(2)}, u32[]{:S(2)}) %collective-permute-start) | collective-permute-done | bytes 163872 | tf_op jit(solution)/shard_map/ppermute | solution.py:382
  11.4 1.7 %collective-permute-done.1.refs_2_ = f32[40,8,128]{2,1,0:T(8,128)S(1)} collective-permute-done((f32[40,8,128]{2,1,0:T(8,128)S(1)}, f32[40,8,128]{2,1,0:T(8,128)S(1)}, u32[]{:S(2)}, u32[]{:S(2)}) %collective-permute-start.1) | collective-permute-done | bytes 163872 | tf_op jit(solution)/shard_map/ppermute | solution.py:382
  13.1 1.6 %collective-permute-done.2.refs_3_ = f32[40,8,128]{2,1,0:T(8,128)S(1)} collective-permute-done((f32[40,8,128]{2,1,0:T(8,128)S(1)}, f32[40,8,128]{2,1,0:T(8,128)S(1)}, u32[]{:S(2)}, u32[]{:S(2)}) %collective-permute-start.2) | collective-permute-done | bytes 163872 | tf_op jit(solution)/shard_map/ppermute | solution.py:382
  14.7 0.2 shard_map.60
  14.9 0.1 collective-permute-start.3
  15.0 0.9 %collective-permute-start.4 = (f32[47,8,128]{2,1,0:T(8,128)S(1)}, f32[47,8,128]{2,1,0:T(8,128)S(1)}, u32[]{:S(2)}, u32[]{:S(2)}) collective-permute-start(f32[47,8,128]{2,1,0:T(8,128)S(1)} %get-tuple-element.25), channel_id=1, source_target_pairs={{0,8},{8,24},{24,16},{16,18},{18,26},{26,10},{10,2},{2,4},{4,12},{... | collective-permute-start | bytes 577544 | tf_op jit(solution)/shard_map/ppermute | solution.py:389
  15.8 1.2 %collective-permute-start.6 = (f32[47,8,128]{2,1,0:T(8,128)S(1)}, f32[47,8,128]{2,1,0:T(8,128)S(1)}, u32[]{:S(2)}, u32[]{:S(2)}) collective-permute-start(f32[47,8,128]{2,1,0:T(8,128)S(1)} %get-tuple-element.26), channel_id=1, source_target_pairs={{0,6},{8,0},{24,8},{16,24},{18,16},{26,18},{10,26},{2,10},{4,2},{1... | collective-permute-start | bytes 577544 | tf_op jit(solution)/shard_map/ppermute | solution.py:390
  17.0 5.1 %collective-permute-done.4.lo_a = f32[47,8,128]{2,1,0:T(8,128)S(1)} collective-permute-done((f32[47,8,128]{2,1,0:T(8,128)S(1)}, f32[47,8,128]{2,1,0:T(8,128)S(1)}, u32[]{:S(2)}, u32[]{:S(2)}) %collective-permute-start.4) | collective-permute-done | bytes 192544 | tf_op jit(solution)/shard_map/ppermute | solution.py:389
  22.2 0.0 collective-permute-start.5
  22.2 0.5 %collective-permute-done.6.hi_a = f32[47,8,128]{2,1,0:T(8,128)S(1)} collective-permute-done((f32[47,8,128]{2,1,0:T(8,128)S(1)}, f32[47,8,128]{2,1,0:T(8,128)S(1)}, u32[]{:S(2)}, u32[]{:S(2)}) %collective-permute-start.6) | collective-permute-done | bytes 192544 | tf_op jit(solution)/shard_map/ppermute | solution.py:390
  22.7 0.0 collective-permute-start.7
  22.7 0.9 %collective-permute-done.5.lo_b = f32[47,8,128]{2,1,0:T(8,128)S(1)} collective-permute-done((f32[47,8,128]{2,1,0:T(8,128)S(1)}, f32[47,8,128]{2,1,0:T(8,128)S(1)}, u32[]{:S(2)}, u32[]{:S(2)}) %collective-permute-start.5) | collective-permute-done | bytes 192544 | tf_op jit(solution)/shard_map/ppermute | solution.py:386
  23.6 0.5 %collective-permute-done.7.hi_b = f32[47,8,128]{2,1,0:T(8,128)S(1)} collective-permute-done((f32[47,8,128]{2,1,0:T(8,128)S(1)}, f32[47,8,128]{2,1,0:T(8,128)S(1)}, u32[]{:S(2)}, u32[]{:S(2)}) %collective-permute-start.7) | collective-permute-done | bytes 192544 | tf_op jit(solution)/shard_map/ppermute | solution.py:386
  24.2 0.0 collective-permute-done.3.own_b
  24.2 2.8 %shard_map.61 = (f32[4,19,8,256]{3,2,1,0:T(8,128)S(1)}, f32[4,8,128]{2,1,0:T(8,128)S(1)}, f32[8,4,8,256]{3,2,1,0:T(8,128)S(1)}, f32[8,4,8,256]{3,2,1,0:T(8,128)S...) custom-call(f32[4,40,8,128]{3,2,1,0:T(8,128)S(1)} %get-tuple-element.24.own_a, ...), custom_call_target="tpu_custom_call" | custom-call | tf_op jit(solution)/shard_map/pallas_call | solution.py:353
  27.0 1.5 %collective-permute-start.8 = (f32[42,8,128]{2,1,0:T(8,128)S(1)}, f32[42,8,128]{2,1,0:T(8,128)S(1)}, u32[]{:S(2)}, u32[]{:S(2)}) collective-permute-start(f32[42,8,128]{2,1,0:T(8,128)S(1)} %get-tuple-element.32), channel_id=1, source_target_pairs={{0,8},{8,24},{24,16},{16,18},{18,26},{26,10},{10,2},{2,4},{4,12},{... | collective-permute-start | bytes 516104 | tf_op jit(solution)/shard_map/ppermute | solution.py:389
  28.5 3.2 %collective-permute-start.10 = (f32[42,8,128]{2,1,0:T(8,128)S(1)}, f32[42,8,128]{2,1,0:T(8,128)S(1)}, u32[]{:S(2)}, u32[]{:S(2)}) collective-permute-start(f32[42,8,128]{2,1,0:T(8,128)S(1)} %get-tuple-element.33), channel_id=1, source_target_pairs={{0,6},{8,0},{24,8},{16,24},{18,16},{26,18},{10,26},{2,10},{4,2},{1... | collective-permute-start | bytes 516104 | tf_op jit(solution)/shard_map/ppermute | solution.py:390
  31.8 4.7 %collective-permute-done.8.lo_a = f32[42,8,128]{2,1,0:T(8,128)S(1)} collective-permute-done((f32[42,8,128]{2,1,0:T(8,128)S(1)}, f32[42,8,128]{2,1,0:T(8,128)S(1)}, u32[]{:S(2)}, u32[]{:S(2)}) %collective-permute-start.8) | collective-permute-done | bytes 172064 | tf_op jit(solution)/shard_map/ppermute | solution.py:389
  36.5 0.0 collective-permute-start.9
  36.5 0.0 collective-permute-done.10.hi_a
  36.5 0.5 collective-permute-start.11
  37.0 0.9 %collective-permute-done.9.lo_b = f32[42,8,128]{2,1,0:T(8,128)S(1)} collective-permute-done((f32[42,8,128]{2,1,0:T(8,128)S(1)}, f32[42,8,128]{2,1,0:T(8,128)S(1)}, u32[]{:S(2)}, u32[]{:S(2)}) %collective-permute-start.9) | collective-permute-done | bytes 172064 | tf_op jit(solution)/shard_map/ppermute | solution.py:386
  37.9 0.2 collective-permute-done.11.hi_b
  38.1 0.0 copy-start.1
  38.1 0.0 copy-start.4
  38.1 2.2 %shard_map.62 = (f32[20,8,128]{2,1,0:T(8,128)S(1)}, f32[20,8,128]{2,1,0:T(8,128)S(1)}, f32[20,8,128]{2,1,0:T(8,128)S(1)}, f32[20,8,128]{2,1,0:T(8,128)S(1)}) custom-call(f32[4,19,8,256]{3,2,1,0:T(8,128)S(1)} %get-tuple-element.27.lam_ref, f32[4,8,128]{2,1,0:T(8,128)S(1)} %get-tuple-element.28.sens_ref, f32[8,4,8,256]{3,2,1,0:T(8,128)S(1)} %get-tuple-element.29.mom1, ...), custom_call_target="tpu_custom_call" | custom-call | tf_op jit(solution)/shard_map/pallas_call | solution.py:353
  40.3 5.2 %collective-permute-start.12 = (f32[20,8,128]{2,1,0:T(8,128)S(1)}, f32[20,8,128]{2,1,0:T(8,128)S(1)}, u32[]{:S(2)}, u32[]{:S(2)}) collective-permute-start(f32[20,8,128]{2,1,0:T(8,128)S(1)} %get-tuple-element.35), channel_id=1, source_target_pairs={{0,8},{8,0},{16,24},{24,16},{1,9},{9,1},{17,25},{25,17},{2,10},{10... | collective-permute-start | bytes 245768 | tf_op jit(solution)/shard_map/ppermute | solution.py:382
  45.5 0.0 collective-permute-start.13
  45.5 1.5 %collective-permute-start.14 = (f32[20,8,128]{2,1,0:T(8,128)S(1)}, f32[20,8,128]{2,1,0:T(8,128)S(1)}, u32[]{:S(2)}, u32[]{:S(2)}) collective-permute-start(f32[20,8,128]{2,1,0:T(8,128)S(1)} %get-tuple-element.37), channel_id=1, source_target_pairs={{0,24},{8,16},{16,8},{24,0},{1,25},{9,17},{17,9},{25,1},{2,26},{10... | collective-permute-start | bytes 245768 | tf_op jit(solution)/shard_map/ppermute | solution.py:382
  47.0 1.3 %collective-permute-done.12.refs_1_ = f32[20,8,128]{2,1,0:T(8,128)S(1)} collective-permute-done((f32[20,8,128]{2,1,0:T(8,128)S(1)}, f32[20,8,128]{2,1,0:T(8,128)S(1)}, u32[]{:S(2)}, u32[]{:S(2)}) %collective-permute-start.12) | collective-permute-done | bytes 81952 | tf_op jit(solution)/shard_map/ppermute | solution.py:382
  48.4 3.2 %collective-permute-done.13.refs_2_ = f32[20,8,128]{2,1,0:T(8,128)S(1)} collective-permute-done((f32[20,8,128]{2,1,0:T(8,128)S(1)}, f32[20,8,128]{2,1,0:T(8,128)S(1)}, u32[]{:S(2)}, u32[]{:S(2)}) %collective-permute-start.13) | collective-permute-done | bytes 81952 | tf_op jit(solution)/shard_map/ppermute | solution.py:382
  51.6 0.0 collective-permute-done.14.refs_3_
  51.6 0.0 copy-done.1
  51.6 0.0 copy-done.4
  51.6 0.0 copy-done.6
  51.6 0.9 %shard_map.63 = (f32[19,2,16,128]{3,2,1,0:T(8,128)}, f32[2,16,128]{2,1,0:T(8,128)}) custom-call(f32[19,2,16,128]{3,2,1,0:T(8,128)S(1)} %copy-done.1, f32[2,16,128]{2,1,0:T(8,128)S(1)} %copy-done.4, s32[2,16,128]{2,1,0:T(8,128)S(1)} %copy-done.6, f32[20,8,128]{2,1,0:T(8,128)S(1)} %get-tuple-element.34.refs_0_, ...), custom_call_target="tpu_custom_call" | custom-call | tf_op jit(solution)/shard_map/pallas_call | solution.py:353
  (1 shorter events, 0.0 us)
Async XLA Ops:
  0.6 1.0 %copy-start = (f32[19,2,16,128]{3,2,1,0:T(8,128)S(1)}, f32[19,2,16,128]{3,2,1,0:T(8,128)}, u32[]{:S(2)}) copy-start(f32[19,2,16,128]{3,2,1,0:T(8,128)} %f_ref.3) | copy-start | bytes 933892
  1.6 1.0 %copy-start.2 = (f32[19,2,16,128]{3,2,1,0:T(8,128)S(1)}, f32[19,2,16,128]{3,2,1,0:T(8,128)}, u32[]{:S(2)}) copy-start(f32[19,2,16,128]{3,2,1,0:T(8,128)} %a_ref.1) | copy-start | bytes 933892
  2.6 0.7 %copy-start.3 = (f32[2,16,128]{2,1,0:T(8,128)S(1)}, f32[2,16,128]{2,1,0:T(8,128)}, u32[]{:S(2)}) copy-start(f32[2,16,128]{2,1,0:T(8,128)} %r_ref.3) | copy-start | bytes 49156
  3.3 0.7 %copy-start.5 = (s32[2,16,128]{2,1,0:T(8,128)S(1)}, s32[2,16,128]{2,1,0:T(8,128)}, u32[]{:S(2)}) copy-start(s32[2,16,128]{2,1,0:T(8,128)} %s_ref.3) | copy-start | bytes 49156
  4.2 7.2 %collective-permute-start = (f32[40,8,128]{2,1,0:T(8,128)S(1)}, f32[40,8,128]{2,1,0:T(8,128)S(1)}, u32[]{:S(2)}, u32[]{:S(2)}) collective-permute-start(f32[40,8,128]{2,1,0:T(8,128)S(1)} %get-tuple-element.21), channel_id=1, source_target_pairs={{0,8},{8,0},{16,24},{24,16},{1,9},{9,1},{17,25},{25,17},{2,10},{10... | collective-permute-start | bytes 491528 | tf_op jit(solution)/shard_map/ppermute | solution.py:382
  4.8 8.2 %collective-permute-start.1 = (f32[40,8,128]{2,1,0:T(8,128)S(1)}, f32[40,8,128]{2,1,0:T(8,128)S(1)}, u32[]{:S(2)}, u32[]{:S(2)}) collective-permute-start(f32[40,8,128]{2,1,0:T(8,128)S(1)} %get-tuple-element.22), channel_id=1, source_target_pairs={{0,16},{8,24},{16,0},{24,8},{1,17},{9,25},{17,1},{25,9},{2,18},{10... | collective-permute-start | bytes 491528 | tf_op jit(solution)/shard_map/ppermute | solution.py:382
  6.3 8.4 %collective-permute-start.2 = (f32[40,8,128]{2,1,0:T(8,128)S(1)}, f32[40,8,128]{2,1,0:T(8,128)S(1)}, u32[]{:S(2)}, u32[]{:S(2)}) collective-permute-start(f32[40,8,128]{2,1,0:T(8,128)S(1)} %get-tuple-element.23), channel_id=1, source_target_pairs={{0,24},{8,16},{16,8},{24,0},{1,25},{9,17},{17,9},{25,1},{2,26},{10... | collective-permute-start | bytes 491528 | tf_op jit(solution)/shard_map/ppermute | solution.py:382
  14.9 9.3 %collective-permute-start.3 = (f32[4,40,8,128]{3,2,1,0:T(8,128)S(1)}, f32[4,40,8,128]{3,2,1,0:T(8,128)S(1)}, u32[]{:S(2)}, u32[]{:S(2)}) collective-permute-start(f32[4,40,8,128]{3,2,1,0:T(8,128)S(1)} %get-tuple-element.24.own_a), channel_id=1, source_target_pairs={{0,1},{1,0},{2,3},{3,2},{4,5},{5,4},{6,7},{7,6},{8,9},{9,8},{10,11... | collective-permute-start | bytes 1966088 | tf_op jit(solution)/shard_map/ppermute | solution.py:386
  15.0 7.2 %collective-permute-start.4 = (f32[47,8,128]{2,1,0:T(8,128)S(1)}, f32[47,8,128]{2,1,0:T(8,128)S(1)}, u32[]{:S(2)}, u32[]{:S(2)}) collective-permute-start(f32[47,8,128]{2,1,0:T(8,128)S(1)} %get-tuple-element.25), channel_id=1, source_target_pairs={{0,8},{8,24},{24,16},{16,18},{18,26},{26,10},{10,2},{2,4},{4,12},{... | collective-permute-start | bytes 577544 | tf_op jit(solution)/shard_map/ppermute | solution.py:389
  15.8 6.9 %collective-permute-start.6 = (f32[47,8,128]{2,1,0:T(8,128)S(1)}, f32[47,8,128]{2,1,0:T(8,128)S(1)}, u32[]{:S(2)}, u32[]{:S(2)}) collective-permute-start(f32[47,8,128]{2,1,0:T(8,128)S(1)} %get-tuple-element.26), channel_id=1, source_target_pairs={{0,6},{8,0},{24,8},{16,24},{18,16},{26,18},{10,26},{2,10},{4,2},{1... | collective-permute-start | bytes 577544 | tf_op jit(solution)/shard_map/ppermute | solution.py:390
  22.2 1.4 %collective-permute-start.5 = (f32[47,8,128]{2,1,0:T(8,128)S(1)}, f32[47,8,128]{2,1,0:T(8,128)S(1)}, u32[]{:S(2)}, u32[]{:S(2)}) collective-permute-start(f32[47,8,128]{2,1,0:T(8,128)S(1)} %collective-permute-done.4.lo_a), channel_id=1, source_target_pairs={{0,1},{1,0},{2,3},{3,2},{4,5},{5,4},{6,7},{7,6},{8,9},{9,8},{10,11... | collective-permute-start | bytes 577544 | tf_op jit(solution)/shard_map/ppermute | solution.py:386
  22.7 1.4 %collective-permute-start.7 = (f32[47,8,128]{2,1,0:T(8,128)S(1)}, f32[47,8,128]{2,1,0:T(8,128)S(1)}, u32[]{:S(2)}, u32[]{:S(2)}) collective-permute-start(f32[47,8,128]{2,1,0:T(8,128)S(1)} %collective-permute-done.6.hi_a), channel_id=1, source_target_pairs={{0,1},{1,0},{2,3},{3,2},{4,5},{5,4},{6,7},{7,6},{8,9},{9,8},{10,11... | collective-permute-start | bytes 577544 | tf_op jit(solution)/shard_map/ppermute | solution.py:386
  27.0 9.5 %collective-permute-start.8 = (f32[42,8,128]{2,1,0:T(8,128)S(1)}, f32[42,8,128]{2,1,0:T(8,128)S(1)}, u32[]{:S(2)}, u32[]{:S(2)}) collective-permute-start(f32[42,8,128]{2,1,0:T(8,128)S(1)} %get-tuple-element.32), channel_id=1, source_target_pairs={{0,8},{8,24},{24,16},{16,18},{18,26},{26,10},{10,2},{2,4},{4,12},{... | collective-permute-start | bytes 516104 | tf_op jit(solution)/shard_map/ppermute | solution.py:389
  28.5 7.9 %collective-permute-start.10 = (f32[42,8,128]{2,1,0:T(8,128)S(1)}, f32[42,8,128]{2,1,0:T(8,128)S(1)}, u32[]{:S(2)}, u32[]{:S(2)}) collective-permute-start(f32[42,8,128]{2,1,0:T(8,128)S(1)} %get-tuple-element.33), channel_id=1, source_target_pairs={{0,6},{8,0},{24,8},{16,24},{18,16},{26,18},{10,26},{2,10},{4,2},{1... | collective-permute-start | bytes 516104 | tf_op jit(solution)/shard_map/ppermute | solution.py:390
  36.5 1.4 %collective-permute-start.9 = (f32[42,8,128]{2,1,0:T(8,128)S(1)}, f32[42,8,128]{2,1,0:T(8,128)S(1)}, u32[]{:S(2)}, u32[]{:S(2)}) collective-permute-start(f32[42,8,128]{2,1,0:T(8,128)S(1)} %collective-permute-done.8.lo_a), channel_id=1, source_target_pairs={{0,1},{1,0},{2,3},{3,2},{4,5},{5,4},{6,7},{7,6},{8,9},{9,8},{10,11... | collective-permute-start | bytes 516104 | tf_op jit(solution)/shard_map/ppermute | solution.py:386
  36.5 1.6 %collective-permute-start.11 = (f32[42,8,128]{2,1,0:T(8,128)S(1)}, f32[42,8,128]{2,1,0:T(8,128)S(1)}, u32[]{:S(2)}, u32[]{:S(2)}) collective-permute-start(f32[42,8,128]{2,1,0:T(8,128)S(1)} %collective-permute-done.10.hi_a), channel_id=1, source_target_pairs={{0,1},{1,0},{2,3},{3,2},{4,5},{5,4},{6,7},{7,6},{8,9},{9,8},{10,11... | collective-permute-start | bytes 516104 | tf_op jit(solution)/shard_map/ppermute | solution.py:386
  38.1 13.5 %copy-start.1 = (f32[19,2,16,128]{3,2,1,0:T(8,128)S(1)}, f32[19,2,16,128]{3,2,1,0:T(8,128)}, u32[]{:S(2)}) copy-start(f32[19,2,16,128]{3,2,1,0:T(8,128)} %f_ref.3) | copy-start | bytes 933892
  38.1 13.5 %copy-start.4 = (f32[2,16,128]{2,1,0:T(8,128)S(1)}, f32[2,16,128]{2,1,0:T(8,128)}, u32[]{:S(2)}) copy-start(f32[2,16,128]{2,1,0:T(8,128)} %r_ref.3) | copy-start | bytes 49156
  38.1 13.5 %copy-start.6 = (s32[2,16,128]{2,1,0:T(8,128)S(1)}, s32[2,16,128]{2,1,0:T(8,128)}, u32[]{:S(2)}) copy-start(s32[2,16,128]{2,1,0:T(8,128)} %s_ref.3) | copy-start | bytes 49156
  40.3 8.1 %collective-permute-start.12 = (f32[20,8,128]{2,1,0:T(8,128)S(1)}, f32[20,8,128]{2,1,0:T(8,128)S(1)}, u32[]{:S(2)}, u32[]{:S(2)}) collective-permute-start(f32[20,8,128]{2,1,0:T(8,128)S(1)} %get-tuple-element.35), channel_id=1, source_target_pairs={{0,8},{8,0},{16,24},{24,16},{1,9},{9,1},{17,25},{25,17},{2,10},{10... | collective-permute-start | bytes 245768 | tf_op jit(solution)/shard_map/ppermute | solution.py:382
  45.5 6.1 %collective-permute-start.13 = (f32[20,8,128]{2,1,0:T(8,128)S(1)}, f32[20,8,128]{2,1,0:T(8,128)S(1)}, u32[]{:S(2)}, u32[]{:S(2)}) collective-permute-start(f32[20,8,128]{2,1,0:T(8,128)S(1)} %get-tuple-element.36), channel_id=1, source_target_pairs={{0,16},{8,24},{16,0},{24,8},{1,17},{9,25},{17,1},{25,9},{2,18},{10... | collective-permute-start | bytes 245768 | tf_op jit(solution)/shard_map/ppermute | solution.py:382
  45.5 6.1 %collective-permute-start.14 = (f32[20,8,128]{2,1,0:T(8,128)S(1)}, f32[20,8,128]{2,1,0:T(8,128)S(1)}, u32[]{:S(2)}, u32[]{:S(2)}) collective-permute-start(f32[20,8,128]{2,1,0:T(8,128)S(1)} %get-tuple-element.37), channel_id=1, source_target_pairs={{0,24},{8,16},{16,8},{24,0},{1,25},{9,17},{17,9},{25,1},{2,26},{10... | collective-permute-start | bytes 245768 | tf_op jit(solution)/shard_map/ppermute | solution.py:382
where the time goes:
time: 52.9 us; the launch traced here: 52.6 us
  waiting for transfers between devices  24.5 us (46%)
  starting transfers between devices  17.7 us (33%)
  Pallas kernels  6.32 us (12%)
  local copies, waits for them, and re-layouts  3.37 us (6%)
  between operations  0.71 us (1%)
    ppermute x6, waiting for transfers between devices, trade(): lax.ppermute(pieces[k], 'gx', [(i, i ^ k) for i in range(GROUP)])  11.5 us
    ppermute x6, starting transfers between devices, trade(): lax.ppermute(pieces[k], 'gx', [(i, i ^ k) for i in range(GROUP)])  10.3 us
    ppermute x2, waiting for transfers between devices, ring(): lo = lax.ppermute(up, ('gx', 'gy'), ring_pairs(planes, 1))  9.85 us
    pallas_call x5, Pallas kernels, call(): pl.pallas_call(kernel, out_shape=[jax.ShapeDtypeStruct(shape, jnp.float32...  6.32 us
    ppermute x2, starting transfers between devices, ring(): hi = lax.ppermute(down, ('gx', 'gy'), ring_pairs(planes, -1))  4.43 us
    unnamed x14, local copies, waits for them, and re-layouts  3.37 us
    ppermute x5, waiting for transfers between devices, swap(): return lax.ppermute(value, 'gz', [(0, 1), (1, 0)])  2.57 us
    ppermute x2, starting transfers between devices, ring(): lo = lax.ppermute(up, ('gx', 'gy'), ring_pairs(planes, 1))  2.42 us
  transfers between devices with their start and end apart: 15, of which 12 were waited for; matrix products, arithmetic and copies ran while one was open for 0% of the time, Pallas kernels for 0%

commit v1 on v0

--- a/solution.py
+++ b/solution.py
@@ -166,13 +166,17 @@
 
 
 def block_of(number):
-    gray = number ^ (number >> 1)
-    odd = lax.axis_index("gy") % 2
-    return gray + odd * (GROUP - 1 - 2 * gray)
-
-
-def send_kernel(f_ref, r_ref, s_ref, a_ref, *refs):
-    outs, blocks = refs[:GROUP], refs[GROUP]
+    return (lax.axis_index("gy") + GROUP - (number ^ (number >> 1))) % GROUP
+
+
+def send_kernel(*refs):
+    given, outs, blocks, held, sems = refs[:4], refs[4 : 4 + GROUP], refs[4 + GROUP], refs[5 + GROUP : 9 + GROUP], refs[-1]
+    copies = [pltpu.make_async_copy(source, target, sems.at[at]) for at, (source, target) in enumerate(zip(given, held))]
+    for copy in copies:
+        copy.start()
+    for copy in copies:
+        copy.wait()
+    f_ref, r_ref, s_ref, a_ref = held
     for half in range(2):
         rows = pl.ds(8 * half, 8)
         tiles = []
@@ -348,24 +352,24 @@
             sens_ref[layer, rows, :] = tile[Q] + design
 
 
-def call(kernel, outs, scratch, *args):
+def call(kernel, outs, scratch, *args, space=pltpu.VMEM):
     vmem = pl.BlockSpec(memory_space=pltpu.VMEM)
     return pl.pallas_call(
         kernel,
         out_shape=[jax.ShapeDtypeStruct(shape, jnp.float32) for shape in outs],
-        in_specs=[vmem] * len(args),
+        in_specs=[pl.BlockSpec(memory_space=space)] * len(args),
         out_specs=[vmem] * len(outs),
-        scratch_shapes=[pltpu.VMEM(shape, jnp.float32) for shape in scratch],
+        scratch_shapes=[pltpu.VMEM(shape, jnp.float32) if isinstance(shape, tuple) else shape for shape in scratch],
         compiler_params=pltpu.CompilerParams(vmem_limit_bytes=VMEM_LIMIT),
     )(*args)
 
 
 def ring_pairs(planes, step):
-    gray = [number ^ (number >> 1) for number in range(GROUP)]
     order = []
     for plane in range(planes):
-        inside = sorted(range(GROUP), key=lambda number: gray[number])
-        order += [(number, plane) for number in (inside if plane % 2 == 0 else inside[::-1])]
+        for block in range(GROUP):
+            gray = (plane - block) % GROUP
+            order.append((gray ^ (gray >> 1), plane))
     pairs = []
     for at, (number, plane) in enumerate(order):
         other, beyond = order[(at + step) % len(order)]
@@ -390,8 +394,15 @@
         hi = lax.ppermute(down, ("gx", "gy"), ring_pairs(planes, -1))
         return lo, hi
 
+    given = (checkpoint, resistance, solid, adjoint_final)
     pieces = call(
-        send_kernel, [(FIELDS, 8, 128)] * GROUP, [(GROUP, FIELDS, 8, 128)], checkpoint, resistance, solid, adjoint_final
+        send_kernel,
+        [(FIELDS, 8, 128)] * GROUP,
+        [(GROUP, FIELDS, 8, 128)]
+        + [pltpu.VMEM(array.shape, array.dtype) for array in given]
+        + [pltpu.SemaphoreType.DMA((len(given),))],
+        *[pltpu.with_memory_space_constraint(array, pltpu.HBM) for array in given],
+        space=pltpu.HBM,
     )
     pieces = trade(pieces)
     own, up, down = call(

time: 52.9 us -> 47.9 us (0.905)
  the two profiles are of different devices: /device:TPU:18 before, /device:TPU:0 now
where the time goes in v1:
time: 47.9 us; the launch traced here: 47.7 us
  waiting for transfers between devices  22.6 us (47%)
  starting transfers between devices  16.9 us (35%)
  Pallas kernels  7.44 us (16%)
  between operations  0.72 us (2%)
    ppermute x6, waiting for transfers between devices, trade(): lax.ppermute(pieces[k], 'gx', [(i, i ^ k) for i in range(GROUP)])  10.6 us
    ppermute x2, waiting for transfers between devices, ring(): lo = lax.ppermute(up, ('gx', 'gy'), ring_pairs(planes, 1))  9.69 us
    ppermute x6, starting transfers between devices, trade(): lax.ppermute(pieces[k], 'gx', [(i, i ^ k) for i in range(GROUP)])  8.08 us
    pallas_call x5, Pallas kernels, call(): pl.pallas_call(kernel, out_shape=[jax.ShapeDtypeStruct(shape, jnp.float32...  7.44 us
    ppermute x2, starting transfers between devices, ring(): hi = lax.ppermute(down, ('gx', 'gy'), ring_pairs(planes, -1))  6.12 us
    ppermute x5, waiting for transfers between devices, swap(): return lax.ppermute(value, 'gz', [(0, 1), (1, 0)])  2.34 us
    ppermute x2, starting transfers between devices, ring(): lo = lax.ppermute(up, ('gx', 'gy'), ring_pairs(planes, 1))  1.63 us
    ppermute x5, starting transfers between devices, swap(): return lax.ppermute(value, 'gz', [(0, 1), (1, 0)])  1.09 us
  transfers between devices with their start and end apart: 15, of which 10 were waited for; matrix products, arithmetic and copies ran while one was open for 0% of the time, Pallas kernels for 0%

profile of v1, /device:TPU:0, one launch (start us, length us, event | category | flops | bytes accessed | tf_op | source)
XLA Modules:
  0.0 47.7 jit_solution(8161937600616308459)
XLA Ops:
  0.6 1.3 %shard_map.59 = (f32[40,8,128]{2,1,0:T(8,128)S(1)}, f32[40,8,128]{2,1,0:T(8,128)S(1)}, f32[40,8,128]{2,1,0:T(8,128)S(1)}, f32[40,8,128]{2,1,0:T(8,128)S(1)}) custom-call(f32[19,2,16,128]{3,2,1,0:T(8,128)} %f_ref.1, f32[2,16,128]{2,1,0:T(8,128)} %r_ref.1, s32[2,16,128]{2,1,0:T(8,128)} %s_ref.1, f32[19,2,16,128]{3,2,1,0:T(8,128)} %refs_3_.1), custom_call_target="tpu_custom_call" | custom-call | tf_op jit(solution)/shard_map/pallas_call | solution.py:357
  2.0 3.0 %collective-permute-start = (f32[40,8,128]{2,1,0:T(8,128)S(1)}, f32[40,8,128]{2,1,0:T(8,128)S(1)}, u32[]{:S(2)}, u32[]{:S(2)}) collective-permute-start(f32[40,8,128]{2,1,0:T(8,128)S(1)} %get-tuple-element.21), channel_id=1, source_target_pairs={{0,8},{8,0},{16,24},{24,16},{1,9},{9,1},{17,25},{25,17},{2,10},{10... | collective-permute-start | bytes 491528 | tf_op jit(solution)/shard_map/ppermute | solution.py:386
  5.0 1.5 %collective-permute-start.1 = (f32[40,8,128]{2,1,0:T(8,128)S(1)}, f32[40,8,128]{2,1,0:T(8,128)S(1)}, u32[]{:S(2)}, u32[]{:S(2)}) collective-permute-start(f32[40,8,128]{2,1,0:T(8,128)S(1)} %get-tuple-element.22), channel_id=1, source_target_pairs={{0,16},{8,24},{16,0},{24,8},{1,17},{9,25},{17,1},{25,9},{2,18},{10... | collective-permute-start | bytes 491528 | tf_op jit(solution)/shard_map/ppermute | solution.py:386
  6.5 0.0 collective-permute-start.2
  6.5 3.5 %collective-permute-done.refs_1_ = f32[40,8,128]{2,1,0:T(8,128)S(1)} collective-permute-done((f32[40,8,128]{2,1,0:T(8,128)S(1)}, f32[40,8,128]{2,1,0:T(8,128)S(1)}, u32[]{:S(2)}, u32[]{:S(2)}) %collective-permute-start) | collective-permute-done | bytes 163872 | tf_op jit(solution)/shard_map/ppermute | solution.py:386
  10.0 4.1 %collective-permute-done.1.refs_2_ = f32[40,8,128]{2,1,0:T(8,128)S(1)} collective-permute-done((f32[40,8,128]{2,1,0:T(8,128)S(1)}, f32[40,8,128]{2,1,0:T(8,128)S(1)}, u32[]{:S(2)}, u32[]{:S(2)}) %collective-permute-start.1) | collective-permute-done | bytes 163872 | tf_op jit(solution)/shard_map/ppermute | solution.py:386
  14.2 0.0 collective-permute-done.2.refs_3_
  14.2 0.2 shard_map.60
  14.3 0.1 collective-permute-start.3
  14.4 1.6 %collective-permute-start.4 = (f32[47,8,128]{2,1,0:T(8,128)S(1)}, f32[47,8,128]{2,1,0:T(8,128)S(1)}, u32[]{:S(2)}, u32[]{:S(2)}) collective-permute-start(f32[47,8,128]{2,1,0:T(8,128)S(1)} %get-tuple-element.25), channel_id=1, source_target_pairs={{0,16},{16,24},{24,8},{8,10},{10,2},{2,18},{18,26},{26,28},{28,12}... | collective-permute-start | bytes 577544 | tf_op jit(solution)/shard_map/ppermute | solution.py:393
  16.0 2.3 %collective-permute-start.6 = (f32[47,8,128]{2,1,0:T(8,128)S(1)}, f32[47,8,128]{2,1,0:T(8,128)S(1)}, u32[]{:S(2)}, u32[]{:S(2)}) collective-permute-start(f32[47,8,128]{2,1,0:T(8,128)S(1)} %get-tuple-element.26), channel_id=1, source_target_pairs={{0,6},{16,0},{24,16},{8,24},{10,8},{2,10},{18,2},{26,18},{28,26},{... | collective-permute-start | bytes 577544 | tf_op jit(solution)/shard_map/ppermute | solution.py:394
  18.3 5.2 %collective-permute-done.4.lo_a = f32[47,8,128]{2,1,0:T(8,128)S(1)} collective-permute-done((f32[47,8,128]{2,1,0:T(8,128)S(1)}, f32[47,8,128]{2,1,0:T(8,128)S(1)}, u32[]{:S(2)}, u32[]{:S(2)}) %collective-permute-start.4) | collective-permute-done | bytes 192544 | tf_op jit(solution)/shard_map/ppermute | solution.py:393
  23.5 0.0 collective-permute-start.5
  23.5 0.0 collective-permute-done.6.hi_a
  23.5 0.5 %collective-permute-start.7 = (f32[47,8,128]{2,1,0:T(8,128)S(1)}, f32[47,8,128]{2,1,0:T(8,128)S(1)}, u32[]{:S(2)}, u32[]{:S(2)}) collective-permute-start(f32[47,8,128]{2,1,0:T(8,128)S(1)} %collective-permute-done.6.hi_a), channel_id=1, source_target_pairs={{0,1},{1,0},{2,3},{3,2},{4,5},{5,4},{6,7},{7,6},{8,9},{9,8},{10,11... | collective-permute-start | bytes 577544 | tf_op jit(solution)/shard_map/ppermute | solution.py:390
  24.0 0.9 %collective-permute-done.5.lo_b = f32[47,8,128]{2,1,0:T(8,128)S(1)} collective-permute-done((f32[47,8,128]{2,1,0:T(8,128)S(1)}, f32[47,8,128]{2,1,0:T(8,128)S(1)}, u32[]{:S(2)}, u32[]{:S(2)}) %collective-permute-start.5) | collective-permute-done | bytes 192544 | tf_op jit(solution)/shard_map/ppermute | solution.py:390
  24.9 0.3 collective-permute-done.7.hi_b
  25.2 0.0 collective-permute-done.3.own_b
  25.2 2.8 %shard_map.61 = (f32[4,19,8,256]{3,2,1,0:T(8,128)S(1)}, f32[4,8,128]{2,1,0:T(8,128)S(1)}, f32[8,4,8,256]{3,2,1,0:T(8,128)S(1)}, f32[8,4,8,256]{3,2,1,0:T(8,128)S...) custom-call(f32[4,40,8,128]{3,2,1,0:T(8,128)S(1)} %get-tuple-element.24.own_a, ...), custom_call_target="tpu_custom_call" | custom-call | tf_op jit(solution)/shard_map/pallas_call | solution.py:357
  28.1 0.1 collective-permute-start.8
  28.1 3.8 %collective-permute-start.10 = (f32[42,8,128]{2,1,0:T(8,128)S(1)}, f32[42,8,128]{2,1,0:T(8,128)S(1)}, u32[]{:S(2)}, u32[]{:S(2)}) collective-permute-start(f32[42,8,128]{2,1,0:T(8,128)S(1)} %get-tuple-element.33), channel_id=1, source_target_pairs={{0,6},{16,0},{24,16},{8,24},{10,8},{2,10},{18,2},{26,18},{28,26},{... | collective-permute-start | bytes 516104 | tf_op jit(solution)/shard_map/ppermute | solution.py:394
  31.9 4.5 %collective-permute-done.8.lo_a = f32[42,8,128]{2,1,0:T(8,128)S(1)} collective-permute-done((f32[42,8,128]{2,1,0:T(8,128)S(1)}, f32[42,8,128]{2,1,0:T(8,128)S(1)}, u32[]{:S(2)}, u32[]{:S(2)}) %collective-permute-start.8) | collective-permute-done | bytes 172064 | tf_op jit(solution)/shard_map/ppermute | solution.py:393
  36.4 0.0 collective-permute-start.9
  36.4 0.0 collective-permute-done.10.hi_a
  36.4 0.5 %collective-permute-start.11 = (f32[42,8,128]{2,1,0:T(8,128)S(1)}, f32[42,8,128]{2,1,0:T(8,128)S(1)}, u32[]{:S(2)}, u32[]{:S(2)}) collective-permute-start(f32[42,8,128]{2,1,0:T(8,128)S(1)} %collective-permute-done.10.hi_a), channel_id=1, source_target_pairs={{0,1},{1,0},{2,3},{3,2},{4,5},{5,4},{6,7},{7,6},{8,9},{9,8},{10,11... | collective-permute-start | bytes 516104 | tf_op jit(solution)/shard_map/ppermute | solution.py:390
  36.9 0.9 %collective-permute-done.9.lo_b = f32[42,8,128]{2,1,0:T(8,128)S(1)} collective-permute-done((f32[42,8,128]{2,1,0:T(8,128)S(1)}, f32[42,8,128]{2,1,0:T(8,128)S(1)}, u32[]{:S(2)}, u32[]{:S(2)}) %collective-permute-start.9) | collective-permute-done | bytes 172064 | tf_op jit(solution)/shard_map/ppermute | solution.py:390
  37.8 0.2 collective-permute-done.11.hi_b
  38.1 0.0 copy-start
  38.1 0.0 copy-start.1
  38.1 0.0 copy-start.2
  38.1 2.2 %shard_map.62 = (f32[20,8,128]{2,1,0:T(8,128)S(1)}, f32[20,8,128]{2,1,0:T(8,128)S(1)}, f32[20,8,128]{2,1,0:T(8,128)S(1)}, f32[20,8,128]{2,1,0:T(8,128)S(1)}) custom-call(f32[4,19,8,256]{3,2,1,0:T(8,128)S(1)} %get-tuple-element.27.lam_ref, f32[4,8,128]{2,1,0:T(8,128)S(1)} %get-tuple-element.28.sens_ref, f32[8,4,8,256]{3,2,1,0:T(8,128)S(1)} %get-tuple-element.29.mom1, ...), custom_call_target="tpu_custom_call" | custom-call | tf_op jit(solution)/shard_map/pallas_call | solution.py:357
  40.2 0.1 collective-permute-start.12
  40.3 0.1 collective-permute-start.13
  40.4 3.4 %collective-permute-start.14 = (f32[20,8,128]{2,1,0:T(8,128)S(1)}, f32[20,8,128]{2,1,0:T(8,128)S(1)}, u32[]{:S(2)}, u32[]{:S(2)}) collective-permute-start(f32[20,8,128]{2,1,0:T(8,128)S(1)} %get-tuple-element.37), channel_id=1, source_target_pairs={{0,24},{8,16},{16,8},{24,0},{1,25},{9,17},{17,9},{25,1},{2,26},{10... | collective-permute-start | bytes 245768 | tf_op jit(solution)/shard_map/ppermute | solution.py:386
  43.8 1.7 %collective-permute-done.12.refs_1_ = f32[20,8,128]{2,1,0:T(8,128)S(1)} collective-permute-done((f32[20,8,128]{2,1,0:T(8,128)S(1)}, f32[20,8,128]{2,1,0:T(8,128)S(1)}, u32[]{:S(2)}, u32[]{:S(2)}) %collective-permute-start.12) | collective-permute-done | bytes 81952 | tf_op jit(solution)/shard_map/ppermute | solution.py:386
  45.5 1.3 %collective-permute-done.13.refs_2_ = f32[20,8,128]{2,1,0:T(8,128)S(1)} collective-permute-done((f32[20,8,128]{2,1,0:T(8,128)S(1)}, f32[20,8,128]{2,1,0:T(8,128)S(1)}, u32[]{:S(2)}, u32[]{:S(2)}) %collective-permute-start.13) | collective-permute-done | bytes 81952 | tf_op jit(solution)/shard_map/ppermute | solution.py:386
  46.8 0.0 collective-permute-done.14.refs_3_
  46.8 0.0 copy-done
  46.8 0.0 copy-done.1
  46.8 0.0 copy-done.2
  46.8 0.9 %shard_map.63 = (f32[19,2,16,128]{3,2,1,0:T(8,128)}, f32[2,16,128]{2,1,0:T(8,128)}) custom-call(f32[19,2,16,128]{3,2,1,0:T(8,128)S(1)} %copy-done, f32[2,16,128]{2,1,0:T(8,128)S(1)} %copy-done.1, s32[2,16,128]{2,1,0:T(8,128)S(1)} %copy-done.2, f32[20,8,128]{2,1,0:T(8,128)S(1)} %get-tuple-element.34.refs_0_, ...), custom_call_target="tpu_custom_call" | custom-call | tf_op jit(solution)/shard_map/pallas_call | solution.py:357
Async XLA Ops:
  2.0 8.0 %collective-permute-start = (f32[40,8,128]{2,1,0:T(8,128)S(1)}, f32[40,8,128]{2,1,0:T(8,128)S(1)}, u32[]{:S(2)}, u32[]{:S(2)}) collective-permute-start(f32[40,8,128]{2,1,0:T(8,128)S(1)} %get-tuple-element.21), channel_id=1, source_target_pairs={{0,8},{8,0},{16,24},{24,16},{1,9},{9,1},{17,25},{25,17},{2,10},{10... | collective-permute-start | bytes 491528 | tf_op jit(solution)/shard_map/ppermute | solution.py:386
  5.0 9.2 %collective-permute-start.1 = (f32[40,8,128]{2,1,0:T(8,128)S(1)}, f32[40,8,128]{2,1,0:T(8,128)S(1)}, u32[]{:S(2)}, u32[]{:S(2)}) collective-permute-start(f32[40,8,128]{2,1,0:T(8,128)S(1)} %get-tuple-element.22), channel_id=1, source_target_pairs={{0,16},{8,24},{16,0},{24,8},{1,17},{9,25},{17,1},{25,9},{2,18},{10... | collective-permute-start | bytes 491528 | tf_op jit(solution)/shard_map/ppermute | solution.py:386
  6.5 7.7 %collective-permute-start.2 = (f32[40,8,128]{2,1,0:T(8,128)S(1)}, f32[40,8,128]{2,1,0:T(8,128)S(1)}, u32[]{:S(2)}, u32[]{:S(2)}) collective-permute-start(f32[40,8,128]{2,1,0:T(8,128)S(1)} %get-tuple-element.23), channel_id=1, source_target_pairs={{0,24},{8,16},{16,8},{24,0},{1,25},{9,17},{17,9},{25,1},{2,26},{10... | collective-permute-start | bytes 491528 | tf_op jit(solution)/shard_map/ppermute | solution.py:386
  14.3 10.9 %collective-permute-start.3 = (f32[4,40,8,128]{3,2,1,0:T(8,128)S(1)}, f32[4,40,8,128]{3,2,1,0:T(8,128)S(1)}, u32[]{:S(2)}, u32[]{:S(2)}) collective-permute-start(f32[4,40,8,128]{3,2,1,0:T(8,128)S(1)} %get-tuple-element.24.own_a), channel_id=1, source_target_pairs={{0,1},{1,0},{2,3},{3,2},{4,5},{5,4},{6,7},{7,6},{8,9},{9,8},{10,11... | collective-permute-start | bytes 1966088 | tf_op jit(solution)/shard_map/ppermute | solution.py:390
  14.4 9.1 %collective-permute-start.4 = (f32[47,8,128]{2,1,0:T(8,128)S(1)}, f32[47,8,128]{2,1,0:T(8,128)S(1)}, u32[]{:S(2)}, u32[]{:S(2)}) collective-permute-start(f32[47,8,128]{2,1,0:T(8,128)S(1)} %get-tuple-element.25), channel_id=1, source_target_pairs={{0,16},{16,24},{24,8},{8,10},{10,2},{2,18},{18,26},{26,28},{28,12}... | collective-permute-start | bytes 577544 | tf_op jit(solution)/shard_map/ppermute | solution.py:393
  16.0 7.5 %collective-permute-start.6 = (f32[47,8,128]{2,1,0:T(8,128)S(1)}, f32[47,8,128]{2,1,0:T(8,128)S(1)}, u32[]{:S(2)}, u32[]{:S(2)}) collective-permute-start(f32[47,8,128]{2,1,0:T(8,128)S(1)} %get-tuple-element.26), channel_id=1, source_target_pairs={{0,6},{16,0},{24,16},{8,24},{10,8},{2,10},{18,2},{26,18},{28,26},{... | collective-permute-start | bytes 577544 | tf_op jit(solution)/shard_map/ppermute | solution.py:394
  23.5 1.4 %collective-permute-start.5 = (f32[47,8,128]{2,1,0:T(8,128)S(1)}, f32[47,8,128]{2,1,0:T(8,128)S(1)}, u32[]{:S(2)}, u32[]{:S(2)}) collective-permute-start(f32[47,8,128]{2,1,0:T(8,128)S(1)} %collective-permute-done.4.lo_a), channel_id=1, source_target_pairs={{0,1},{1,0},{2,3},{3,2},{4,5},{5,4},{6,7},{7,6},{8,9},{9,8},{10,11... | collective-permute-start | bytes 577544 | tf_op jit(solution)/shard_map/ppermute | solution.py:390
  23.5 1.7 %collective-permute-start.7 = (f32[47,8,128]{2,1,0:T(8,128)S(1)}, f32[47,8,128]{2,1,0:T(8,128)S(1)}, u32[]{:S(2)}, u32[]{:S(2)}) collective-permute-start(f32[47,8,128]{2,1,0:T(8,128)S(1)} %collective-permute-done.6.hi_a), channel_id=1, source_target_pairs={{0,1},{1,0},{2,3},{3,2},{4,5},{5,4},{6,7},{7,6},{8,9},{9,8},{10,11... | collective-permute-start | bytes 577544 | tf_op jit(solution)/shard_map/ppermute | solution.py:390
  28.1 8.4 %collective-permute-start.8 = (f32[42,8,128]{2,1,0:T(8,128)S(1)}, f32[42,8,128]{2,1,0:T(8,128)S(1)}, u32[]{:S(2)}, u32[]{:S(2)}) collective-permute-start(f32[42,8,128]{2,1,0:T(8,128)S(1)} %get-tuple-element.32), channel_id=1, source_target_pairs={{0,16},{16,24},{24,8},{8,10},{10,2},{2,18},{18,26},{26,28},{28,12}... | collective-permute-start | bytes 516104 | tf_op jit(solution)/shard_map/ppermute | solution.py:393
  28.1 8.3 %collective-permute-start.10 = (f32[42,8,128]{2,1,0:T(8,128)S(1)}, f32[42,8,128]{2,1,0:T(8,128)S(1)}, u32[]{:S(2)}, u32[]{:S(2)}) collective-permute-start(f32[42,8,128]{2,1,0:T(8,128)S(1)} %get-tuple-element.33), channel_id=1, source_target_pairs={{0,6},{16,0},{24,16},{8,24},{10,8},{2,10},{18,2},{26,18},{28,26},{... | collective-permute-start | bytes 516104 | tf_op jit(solution)/shard_map/ppermute | solution.py:394
  36.4 1.4 %collective-permute-start.9 = (f32[42,8,128]{2,1,0:T(8,128)S(1)}, f32[42,8,128]{2,1,0:T(8,128)S(1)}, u32[]{:S(2)}, u32[]{:S(2)}) collective-permute-start(f32[42,8,128]{2,1,0:T(8,128)S(1)} %collective-permute-done.8.lo_a), channel_id=1, source_target_pairs={{0,1},{1,0},{2,3},{3,2},{4,5},{5,4},{6,7},{7,6},{8,9},{9,8},{10,11... | collective-permute-start | bytes 516104 | tf_op jit(solution)/shard_map/ppermute | solution.py:390
  36.4 1.6 %collective-permute-start.11 = (f32[42,8,128]{2,1,0:T(8,128)S(1)}, f32[42,8,128]{2,1,0:T(8,128)S(1)}, u32[]{:S(2)}, u32[]{:S(2)}) collective-permute-start(f32[42,8,128]{2,1,0:T(8,128)S(1)} %collective-permute-done.10.hi_a), channel_id=1, source_target_pairs={{0,1},{1,0},{2,3},{3,2},{4,5},{5,4},{6,7},{7,6},{8,9},{9,8},{10,11... | collective-permute-start | bytes 516104 | tf_op jit(solution)/shard_map/ppermute | solution.py:390
  38.1 8.7 %copy-start = (f32[19,2,16,128]{3,2,1,0:T(8,128)S(1)}, f32[19,2,16,128]{3,2,1,0:T(8,128)}, u32[]{:S(2)}) copy-start(f32[19,2,16,128]{3,2,1,0:T(8,128)} %f_ref.1) | copy-start | bytes 933892
  38.1 8.7 %copy-start.1 = (f32[2,16,128]{2,1,0:T(8,128)S(1)}, f32[2,16,128]{2,1,0:T(8,128)}, u32[]{:S(2)}) copy-start(f32[2,16,128]{2,1,0:T(8,128)} %r_ref.1) | copy-start | bytes 49156
  38.1 8.7 %copy-start.2 = (s32[2,16,128]{2,1,0:T(8,128)S(1)}, s32[2,16,128]{2,1,0:T(8,128)}, u32[]{:S(2)}) copy-start(s32[2,16,128]{2,1,0:T(8,128)} %s_ref.1) | copy-start | bytes 49156
  40.2 5.2 %collective-permute-start.12 = (f32[20,8,128]{2,1,0:T(8,128)S(1)}, f32[20,8,128]{2,1,0:T(8,128)S(1)}, u32[]{:S(2)}, u32[]{:S(2)}) collective-permute-start(f32[20,8,128]{2,1,0:T(8,128)S(1)} %get-tuple-element.35), channel_id=1, source_target_pairs={{0,8},{8,0},{16,24},{24,16},{1,9},{9,1},{17,25},{25,17},{2,10},{10... | collective-permute-start | bytes 245768 | tf_op jit(solution)/shard_map/ppermute | solution.py:386
  40.3 6.4 %collective-permute-start.13 = (f32[20,8,128]{2,1,0:T(8,128)S(1)}, f32[20,8,128]{2,1,0:T(8,128)S(1)}, u32[]{:S(2)}, u32[]{:S(2)}) collective-permute-start(f32[20,8,128]{2,1,0:T(8,128)S(1)} %get-tuple-element.36), channel_id=1, source_target_pairs={{0,16},{8,24},{16,0},{24,8},{1,17},{9,25},{17,1},{25,9},{2,18},{10... | collective-permute-start | bytes 245768 | tf_op jit(solution)/shard_map/ppermute | solution.py:386
  40.4 6.4 %collective-permute-start.14 = (f32[20,8,128]{2,1,0:T(8,128)S(1)}, f32[20,8,128]{2,1,0:T(8,128)S(1)}, u32[]{:S(2)}, u32[]{:S(2)}) collective-permute-start(f32[20,8,128]{2,1,0:T(8,128)S(1)} %get-tuple-element.37), channel_id=1, source_target_pairs={{0,24},{8,16},{16,8},{24,0},{1,25},{9,17},{17,9},{25,1},{2,26},{10... | collective-permute-start | bytes 245768 | tf_op jit(solution)/shard_map/ppermute | solution.py:386

commit v2 on v1

--- a/solution.py
+++ b/solution.py
@@ -45,6 +45,8 @@
 ROWS = 4
 LAYERS = 2
 HALO = 3
+WIDTH = 2 * HALO
+SLOTS = 128 // WIDTH
 RES, SOL, ADJ = Q, Q + 1, Q + 2
 FIELDS = Q + 2 + Q
 
@@ -85,6 +87,27 @@
     third = less[2] + ((less[5] - less[6]) + (less[7] - less[8]))
     inverse = 1.0 / density
     return density, first * inverse, second * inverse, third * inverse
+
+
+def strip_count(table):
+    return -(-len(table) // SLOTS)
+
+
+def pack_strips(tiles):
+    lane = lax.broadcasted_iota(jnp.int32, (8, 128), 1)
+    packed = []
+    for number, tile in enumerate(tiles):
+        slot = number % SLOTS
+        moved = pltpu.roll(tile, (WIDTH * slot + HALO) % 128, axis=1)
+        if slot == 0:
+            packed.append(moved)
+        else:
+            packed[-1] = jnp.where(lane >= WIDTH * slot, moved, packed[-1])
+    return packed
+
+
+def unpack_strip(packed, number):
+    return pltpu.roll(packed, (-WIDTH * (number % SLOTS) - HALO) % 128, axis=1)
 
 
 def along(i, x, y, z):
@@ -243,7 +266,7 @@
             p1[row, i] = out[i]
         return 0
 
-    lax.fori_loop(0, ROWS + 4, first, 0)
+    lax.fori_loop(0, ROWS + 4, first, 0, unroll=True)
 
     def second(row, _):
         f = pull(p1, row)
@@ -255,7 +278,7 @@
             p2[row, i] = out[i]
         return 0
 
-    lax.fori_loop(0, ROWS + 2, second, 0)
+    lax.fori_loop(0, ROWS + 2, second, 0, unroll=True)
 
     def third(row, _):
         moment = moments(pull(p2, row))
@@ -266,17 +289,21 @@
         sens_ref[row] = design[:, :128]
         return 0
 
-    lax.fori_loop(0, ROWS, third, 0)
+    lax.fori_loop(0, ROWS, third, 0, unroll=True)
     for table, part in ((BACKWARD_UP, up), (BACKWARD_DOWN, down)):
+        others = []
         for number, (row, field, _) in enumerate(table):
-            source = lam_ref[row, field, :, :128] if field < Q else mom2[row + 2, field - Q, :, :128]
-            part[number] = source
+            source = lam_ref[row, field] if field < Q else mom2[row + 2, field - Q]
+            part[number] = source[:, :128]
+            others.append(source[:, 128:])
+        for number, tile in enumerate(pack_strips(others)):
+            part[len(table) + number] = tile
     for row in (0, ROWS + 3):
         for j in range(4):
             mom2[row, j] = jnp.zeros((8, 256), jnp.float32)
 
 
-def backward_kernel(lam_ref, sens_ref, mom1, mom2, rs_ref, lo_a, lo_b, hi_a, hi_b, *refs):
+def backward_kernel(lam_ref, sens_ref, mom1, mom2, rs_ref, lo, hi, *refs):
     outs, (l3, l2, l1, m2, flat) = refs[:GROUP], refs[GROUP:]
     for row in range(ROWS):
         for i in range(Q):
@@ -284,14 +311,12 @@
     for row in range(ROWS + 4):
         for j in range(4):
             m2[row, j] = mom2[row, j]
-    for side, lo, hi in ((0, lo_a, hi_a), (1, lo_b, hi_b)):
-        lanes = slice(128 * side, 128 * side + 128)
-        for table, part in ((BACKWARD_UP, lo), (BACKWARD_DOWN, hi)):
-            for number, (_, field, row) in enumerate(table):
-                if field < Q:
-                    l3[row + 3, field, :, lanes] = part[number]
-                else:
-                    m2[row + 2, field - Q, :, lanes] = part[number]
+    for table, part in ((BACKWARD_UP, lo), (BACKWARD_DOWN, hi)):
+        packed = [part[len(table) + number] for number in range(strip_count(table))]
+        for number, (_, field, row) in enumerate(table):
+            target = l3.at[row + 3, field] if field < Q else m2.at[row + 2, field - Q]
+            target[:, :128] = part[number]
+            target[:, 128:] = unpack_strip(packed[number // SLOTS], number)
 
     def pull(source, row):
         return [shifted(source[row + 1 + VELOCITIES[i][1], i], i, -1) for i in range(Q)]
@@ -306,7 +331,7 @@
         l1[row, 0] = design
         return 0
 
-    lax.fori_loop(0, ROWS + 4, second, 0)
+    lax.fori_loop(0, ROWS + 4, second, 0, unroll=True)
     total = [sens_ref[row] + l1[row + 2, 0, :, :128] for row in range(ROWS)]
 
     def first(row, _):
@@ -319,7 +344,7 @@
         m2[row, 0] = design
         return 0
 
-    lax.fori_loop(0, ROWS + 2, first, 0)
+    lax.fori_loop(0, ROWS + 2, first, 0, unroll=True)
     for row in range(ROWS):
         designs[pl.ds(row, 8, stride=ROWS), :] = total[row] + m2[row + 1, 0, :, :128]
         mu = pull(l1, row)
@@ -422,8 +447,8 @@
             (ROWS + 4, 4, 8, 256),
             (ROWS + 4, 4, 8, 256),
             (ROWS + 4, 2, 8, 256),
-            (len(BACKWARD_UP), 8, 128),
-            (len(BACKWARD_DOWN), 8, 128),
+            (len(BACKWARD_UP) + strip_count(BACKWARD_UP), 8, 128),
+            (len(BACKWARD_DOWN) + strip_count(BACKWARD_DOWN), 8, 128),
         ],
         [(ROWS + 6, Q, 8, 256), (ROWS + 4, Q, 8, 256), (ROWS + 2, Q, 8, 256), (ROWS + 2, Q, 8, 256)],
         own,
@@ -434,7 +459,6 @@
         hi_b,
     )
     lo, hi = ring(up, down)
-    lo_b, hi_b = swap(lo), swap(hi)
     pieces = call(
         backward_kernel,
         [(Q + 1, 8, 128)] * GROUP,
@@ -451,9 +475,7 @@
         mom2,
         rs,
         lo,
-        lo_b,
         hi,
-        hi_b,
     )
     pieces = trade(pieces)
     return tuple(

time: 47.9 us -> 43.3 us (0.904)
  Pallas kernels: 7.44 us -> 4.86 us
  waiting for transfers between devices: 22.6 us -> 21.1 us
  starting transfers between devices: 16.9 us -> 16.4 us
    pallas_call x5, Pallas kernels: 7.44 us -> 4.86 us  [call(): pl.pallas_call(kernel, out_shape=[jax.ShapeDtypeStruct(shape, jnp.float32...]
    ppermute x5 -> x3, waiting for transfers between devices: 2.34 us -> 1.2 us  [swap(): return lax.ppermute(value, 'gz', [(0, 1), (1, 0)])]
    ppermute x6, waiting for transfers between devices: 10.6 us -> 10 us  [trade(): lax.ppermute(pieces[k], 'gx', [(i, i ^ k) for i in range(GROUP)])]
    ppermute x5 -> x3, starting transfers between devices: 1.09 us -> 0.58 us  [swap(): return lax.ppermute(value, 'gz', [(0, 1), (1, 0)])]
  transfers between devices with their start and end apart: 15 -> 13, of which waited for: 10 -> 8; matrix products, arithmetic and copies ran while one was open for 0% -> 0% of each run, Pallas kernels for 0% -> 0%
where the time goes in v2:
time: 43.3 us; the launch traced here: 43.1 us
  waiting for transfers between devices  21.1 us (49%)
  starting transfers between devices  16.4 us (38%)
  Pallas kernels  4.86 us (11%)
  between operations  0.71 us (2%)
    ppermute x6, waiting for transfers between devices, trade(): lax.ppermute(pieces[k], 'gx', [(i, i ^ k) for i in range(GROUP)])  10 us
    ppermute x2, waiting for transfers between devices, ring(): lo = lax.ppermute(up, ('gx', 'gy'), ring_pairs(planes, 1))  9.86 us
    ppermute x6, starting transfers between devices, trade(): lax.ppermute(pieces[k], 'gx', [(i, i ^ k) for i in range(GROUP)])  8.09 us
    ppermute x2, starting transfers between devices, ring(): hi = lax.ppermute(down, ('gx', 'gy'), ring_pairs(planes, -1))  6.12 us
    pallas_call x5, Pallas kernels, call(): pl.pallas_call(kernel, out_shape=[jax.ShapeDtypeStruct(shape, jnp.float32...  4.86 us
    ppermute x2, starting transfers between devices, ring(): lo = lax.ppermute(up, ('gx', 'gy'), ring_pairs(planes, 1))  1.63 us
    ppermute x3, waiting for transfers between devices, swap(): return lax.ppermute(value, 'gz', [(0, 1), (1, 0)])  1.2 us
  transfers between devices with their start and end apart: 13, of which 8 were waited for; matrix products, arithmetic and copies ran while one was open for 0% of the time, Pallas kernels for 0%

profile of v2, /device:TPU:0, one launch (start us, length us, event | category | flops | bytes accessed | tf_op | source)
XLA Modules:
  0.0 43.1 jit_solution(883942467408286732)
XLA Ops:
  0.6 1.3 %shard_map.59 = (f32[40,8,128]{2,1,0:T(8,128)S(1)}, f32[40,8,128]{2,1,0:T(8,128)S(1)}, f32[40,8,128]{2,1,0:T(8,128)S(1)}, f32[40,8,128]{2,1,0:T(8,128)S(1)}) custom-call(f32[19,2,16,128]{3,2,1,0:T(8,128)} %f_ref.1, f32[2,16,128]{2,1,0:T(8,128)} %r_ref.1, s32[2,16,128]{2,1,0:T(8,128)} %s_ref.1, f32[19,2,16,128]{3,2,1,0:T(8,128)} %refs_3_.1), custom_call_target="tpu_custom_call" | custom-call | tf_op jit(solution)/shard_map/pallas_call | solution.py:382
  2.0 3.0 %collective-permute-start = (f32[40,8,128]{2,1,0:T(8,128)S(1)}, f32[40,8,128]{2,1,0:T(8,128)S(1)}, u32[]{:S(2)}, u32[]{:S(2)}) collective-permute-start(f32[40,8,128]{2,1,0:T(8,128)S(1)} %get-tuple-element.21), channel_id=1, source_target_pairs={{0,8},{8,0},{16,24},{24,16},{1,9},{9,1},{17,25},{25,17},{2,10},{10... | collective-permute-start | bytes 491528 | tf_op jit(solution)/shard_map/ppermute | solution.py:411
  5.0 1.5 %collective-permute-start.1 = (f32[40,8,128]{2,1,0:T(8,128)S(1)}, f32[40,8,128]{2,1,0:T(8,128)S(1)}, u32[]{:S(2)}, u32[]{:S(2)}) collective-permute-start(f32[40,8,128]{2,1,0:T(8,128)S(1)} %get-tuple-element.22), channel_id=1, source_target_pairs={{0,16},{8,24},{16,0},{24,8},{1,17},{9,25},{17,1},{25,9},{2,18},{10... | collective-permute-start | bytes 491528 | tf_op jit(solution)/shard_map/ppermute | solution.py:411
  6.5 0.0 collective-permute-start.2
  6.5 3.5 %collective-permute-done.refs_1_ = f32[40,8,128]{2,1,0:T(8,128)S(1)} collective-permute-done((f32[40,8,128]{2,1,0:T(8,128)S(1)}, f32[40,8,128]{2,1,0:T(8,128)S(1)}, u32[]{:S(2)}, u32[]{:S(2)}) %collective-permute-start) | collective-permute-done | bytes 163872 | tf_op jit(solution)/shard_map/ppermute | solution.py:411
  10.0 4.1 %collective-permute-done.1.refs_2_ = f32[40,8,128]{2,1,0:T(8,128)S(1)} collective-permute-done((f32[40,8,128]{2,1,0:T(8,128)S(1)}, f32[40,8,128]{2,1,0:T(8,128)S(1)}, u32[]{:S(2)}, u32[]{:S(2)}) %collective-permute-start.1) | collective-permute-done | bytes 163872 | tf_op jit(solution)/shard_map/ppermute | solution.py:411
  14.2 0.0 collective-permute-done.2.refs_3_
  14.2 0.2 shard_map.60
  14.3 0.1 collective-permute-start.3
  14.4 1.6 %collective-permute-start.4 = (f32[47,8,128]{2,1,0:T(8,128)S(1)}, f32[47,8,128]{2,1,0:T(8,128)S(1)}, u32[]{:S(2)}, u32[]{:S(2)}) collective-permute-start(f32[47,8,128]{2,1,0:T(8,128)S(1)} %get-tuple-element.25), channel_id=1, source_target_pairs={{0,16},{16,24},{24,8},{8,10},{10,2},{2,18},{18,26},{26,28},{28,12}... | collective-permute-start | bytes 577544 | tf_op jit(solution)/shard_map/ppermute | solution.py:418
  16.0 2.3 %collective-permute-start.6 = (f32[47,8,128]{2,1,0:T(8,128)S(1)}, f32[47,8,128]{2,1,0:T(8,128)S(1)}, u32[]{:S(2)}, u32[]{:S(2)}) collective-permute-start(f32[47,8,128]{2,1,0:T(8,128)S(1)} %get-tuple-element.26), channel_id=1, source_target_pairs={{0,6},{16,0},{24,16},{8,24},{10,8},{2,10},{18,2},{26,18},{28,26},{... | collective-permute-start | bytes 577544 | tf_op jit(solution)/shard_map/ppermute | solution.py:419
  18.3 5.2 %collective-permute-done.4.lo_a = f32[47,8,128]{2,1,0:T(8,128)S(1)} collective-permute-done((f32[47,8,128]{2,1,0:T(8,128)S(1)}, f32[47,8,128]{2,1,0:T(8,128)S(1)}, u32[]{:S(2)}, u32[]{:S(2)}) %collective-permute-start.4) | collective-permute-done | bytes 192544 | tf_op jit(solution)/shard_map/ppermute | solution.py:418
  23.5 0.0 collective-permute-start.5
  23.5 0.0 collective-permute-done.6.hi_a
  23.5 0.5 %collective-permute-start.7 = (f32[47,8,128]{2,1,0:T(8,128)S(1)}, f32[47,8,128]{2,1,0:T(8,128)S(1)}, u32[]{:S(2)}, u32[]{:S(2)}) collective-permute-start(f32[47,8,128]{2,1,0:T(8,128)S(1)} %collective-permute-done.6.hi_a), channel_id=1, source_target_pairs={{0,1},{1,0},{2,3},{3,2},{4,5},{5,4},{6,7},{7,6},{8,9},{9,8},{10,11... | collective-permute-start | bytes 577544 | tf_op jit(solution)/shard_map/ppermute | solution.py:415
  24.0 0.9 %collective-permute-done.5.lo_b = f32[47,8,128]{2,1,0:T(8,128)S(1)} collective-permute-done((f32[47,8,128]{2,1,0:T(8,128)S(1)}, f32[47,8,128]{2,1,0:T(8,128)S(1)}, u32[]{:S(2)}, u32[]{:S(2)}) %collective-permute-start.5) | collective-permute-done | bytes 192544 | tf_op jit(solution)/shard_map/ppermute | solution.py:415
  24.9 0.3 collective-permute-done.7.hi_b
  25.2 0.0 collective-permute-done.3.own_b
  25.2 1.3 %shard_map.61 = (f32[4,19,8,256]{3,2,1,0:T(8,128)S(1)}, f32[4,8,128]{2,1,0:T(8,128)S(1)}, f32[8,4,8,256]{3,2,1,0:T(8,128)S(1)}, f32[8,4,8,256]{3,2,1,0:T(8,128)S...) custom-call(f32[4,40,8,128]{3,2,1,0:T(8,128)S(1)} %get-tuple-element.24.own_a, ...), custom_call_target="tpu_custom_call" | custom-call | tf_op jit(solution)/shard_map/pallas_call | solution.py:382
  26.5 0.1 collective-permute-start.8
  26.6 3.8 %collective-permute-start.9 = (f32[44,8,128]{2,1,0:T(8,128)S(1)}, f32[44,8,128]{2,1,0:T(8,128)S(1)}, u32[]{:S(2)}, u32[]{:S(2)}) collective-permute-start(f32[44,8,128]{2,1,0:T(8,128)S(1)} %get-tuple-element.33), channel_id=1, source_target_pairs={{0,6},{16,0},{24,16},{8,24},{10,8},{2,10},{18,2},{26,18},{28,26},{... | collective-permute-start | bytes 540680 | tf_op jit(solution)/shard_map/ppermute | solution.py:419
  30.4 4.7 %collective-permute-done.8.lo = f32[44,8,128]{2,1,0:T(8,128)S(1)} collective-permute-done((f32[44,8,128]{2,1,0:T(8,128)S(1)}, f32[44,8,128]{2,1,0:T(8,128)S(1)}, u32[]{:S(2)}, u32[]{:S(2)}) %collective-permute-start.8) | collective-permute-done | bytes 180256 | tf_op jit(solution)/shard_map/ppermute | solution.py:418
  35.1 0.0 collective-permute-done.9.hi
  35.1 0.0 copy-start
  35.1 0.0 copy-start.1
  35.1 0.0 copy-start.2
  35.1 1.1 %shard_map.62 = (f32[20,8,128]{2,1,0:T(8,128)S(1)}, f32[20,8,128]{2,1,0:T(8,128)S(1)}, f32[20,8,128]{2,1,0:T(8,128)S(1)}, f32[20,8,128]{2,1,0:T(8,128)S(1)}) custom-call(f32[4,19,8,256]{3,2,1,0:T(8,128)S(1)} %get-tuple-element.27.lam_ref, f32[4,8,128]{2,1,0:T(8,128)S(1)} %get-tuple-element.28.sens_ref, f32[8,4,8,256]{3,2,1,0:T(8,128)S(1)} %get-tuple-element.29.mom1, ...), custom_call_target="tpu_custom_call" | custom-call | tf_op jit(solution)/shard_map/pallas_call | solution.py:382
  36.2 0.1 collective-permute-start.10
  36.3 0.2 collective-permute-start.11
  36.5 3.3 %collective-permute-start.12 = (f32[20,8,128]{2,1,0:T(8,128)S(1)}, f32[20,8,128]{2,1,0:T(8,128)S(1)}, u32[]{:S(2)}, u32[]{:S(2)}) collective-permute-start(f32[20,8,128]{2,1,0:T(8,128)S(1)} %get-tuple-element.37), channel_id=1, source_target_pairs={{0,24},{8,16},{16,8},{24,0},{1,25},{9,17},{17,9},{25,1},{2,26},{10... | collective-permute-start | bytes 245768 | tf_op jit(solution)/shard_map/ppermute | solution.py:411
  39.8 1.5 %collective-permute-done.10.refs_1_ = f32[20,8,128]{2,1,0:T(8,128)S(1)} collective-permute-done((f32[20,8,128]{2,1,0:T(8,128)S(1)}, f32[20,8,128]{2,1,0:T(8,128)S(1)}, u32[]{:S(2)}, u32[]{:S(2)}) %collective-permute-start.10) | collective-permute-done | bytes 81952 | tf_op jit(solution)/shard_map/ppermute | solution.py:411
  41.3 0.0 collective-permute-done.11.refs_2_
  41.3 0.9 %collective-permute-done.12.refs_3_ = f32[20,8,128]{2,1,0:T(8,128)S(1)} collective-permute-done((f32[20,8,128]{2,1,0:T(8,128)S(1)}, f32[20,8,128]{2,1,0:T(8,128)S(1)}, u32[]{:S(2)}, u32[]{:S(2)}) %collective-permute-start.12) | collective-permute-done | bytes 81952 | tf_op jit(solution)/shard_map/ppermute | solution.py:411
  42.2 0.0 copy-done
  42.2 0.0 copy-done.1
  42.2 0.0 copy-done.2
  42.2 0.9 %shard_map.63 = (f32[19,2,16,128]{3,2,1,0:T(8,128)}, f32[2,16,128]{2,1,0:T(8,128)}) custom-call(f32[19,2,16,128]{3,2,1,0:T(8,128)S(1)} %copy-done, f32[2,16,128]{2,1,0:T(8,128)S(1)} %copy-done.1, s32[2,16,128]{2,1,0:T(8,128)S(1)} %copy-done.2, f32[20,8,128]{2,1,0:T(8,128)S(1)} %get-tuple-element.34.refs_0_, ...), custom_call_target="tpu_custom_call" | custom-call | tf_op jit(solution)/shard_map/pallas_call | solution.py:382
Async XLA Ops:
  2.0 8.0 %collective-permute-start = (f32[40,8,128]{2,1,0:T(8,128)S(1)}, f32[40,8,128]{2,1,0:T(8,128)S(1)}, u32[]{:S(2)}, u32[]{:S(2)}) collective-permute-start(f32[40,8,128]{2,1,0:T(8,128)S(1)} %get-tuple-element.21), channel_id=1, source_target_pairs={{0,8},{8,0},{16,24},{24,16},{1,9},{9,1},{17,25},{25,17},{2,10},{10... | collective-permute-start | bytes 491528 | tf_op jit(solution)/shard_map/ppermute | solution.py:411
  5.0 9.2 %collective-permute-start.1 = (f32[40,8,128]{2,1,0:T(8,128)S(1)}, f32[40,8,128]{2,1,0:T(8,128)S(1)}, u32[]{:S(2)}, u32[]{:S(2)}) collective-permute-start(f32[40,8,128]{2,1,0:T(8,128)S(1)} %get-tuple-element.22), channel_id=1, source_target_pairs={{0,16},{8,24},{16,0},{24,8},{1,17},{9,25},{17,1},{25,9},{2,18},{10... | collective-permute-start | bytes 491528 | tf_op jit(solution)/shard_map/ppermute | solution.py:411
  6.5 7.7 %collective-permute-start.2 = (f32[40,8,128]{2,1,0:T(8,128)S(1)}, f32[40,8,128]{2,1,0:T(8,128)S(1)}, u32[]{:S(2)}, u32[]{:S(2)}) collective-permute-start(f32[40,8,128]{2,1,0:T(8,128)S(1)} %get-tuple-element.23), channel_id=1, source_target_pairs={{0,24},{8,16},{16,8},{24,0},{1,25},{9,17},{17,9},{25,1},{2,26},{10... | collective-permute-start | bytes 491528 | tf_op jit(solution)/shard_map/ppermute | solution.py:411
  14.3 10.9 %collective-permute-start.3 = (f32[4,40,8,128]{3,2,1,0:T(8,128)S(1)}, f32[4,40,8,128]{3,2,1,0:T(8,128)S(1)}, u32[]{:S(2)}, u32[]{:S(2)}) collective-permute-start(f32[4,40,8,128]{3,2,1,0:T(8,128)S(1)} %get-tuple-element.24.own_a), channel_id=1, source_target_pairs={{0,1},{1,0},{2,3},{3,2},{4,5},{5,4},{6,7},{7,6},{8,9},{9,8},{10,11... | collective-permute-start | bytes 1966088 | tf_op jit(solution)/shard_map/ppermute | solution.py:415
  14.4 9.1 %collective-permute-start.4 = (f32[47,8,128]{2,1,0:T(8,128)S(1)}, f32[47,8,128]{2,1,0:T(8,128)S(1)}, u32[]{:S(2)}, u32[]{:S(2)}) collective-permute-start(f32[47,8,128]{2,1,0:T(8,128)S(1)} %get-tuple-element.25), channel_id=1, source_target_pairs={{0,16},{16,24},{24,8},{8,10},{10,2},{2,18},{18,26},{26,28},{28,12}... | collective-permute-start | bytes 577544 | tf_op jit(solution)/shard_map/ppermute | solution.py:418
  16.0 7.5 %collective-permute-start.6 = (f32[47,8,128]{2,1,0:T(8,128)S(1)}, f32[47,8,128]{2,1,0:T(8,128)S(1)}, u32[]{:S(2)}, u32[]{:S(2)}) collective-permute-start(f32[47,8,128]{2,1,0:T(8,128)S(1)} %get-tuple-element.26), channel_id=1, source_target_pairs={{0,6},{16,0},{24,16},{8,24},{10,8},{2,10},{18,2},{26,18},{28,26},{... | collective-permute-start | bytes 577544 | tf_op jit(solution)/shard_map/ppermute | solution.py:419
  23.5 1.4 %collective-permute-start.5 = (f32[47,8,128]{2,1,0:T(8,128)S(1)}, f32[47,8,128]{2,1,0:T(8,128)S(1)}, u32[]{:S(2)}, u32[]{:S(2)}) collective-permute-start(f32[47,8,128]{2,1,0:T(8,128)S(1)} %collective-permute-done.4.lo_a), channel_id=1, source_target_pairs={{0,1},{1,0},{2,3},{3,2},{4,5},{5,4},{6,7},{7,6},{8,9},{9,8},{10,11... | collective-permute-start | bytes 577544 | tf_op jit(solution)/shard_map/ppermute | solution.py:415
  23.5 1.7 %collective-permute-start.7 = (f32[47,8,128]{2,1,0:T(8,128)S(1)}, f32[47,8,128]{2,1,0:T(8,128)S(1)}, u32[]{:S(2)}, u32[]{:S(2)}) collective-permute-start(f32[47,8,128]{2,1,0:T(8,128)S(1)} %collective-permute-done.6.hi_a), channel_id=1, source_target_pairs={{0,1},{1,0},{2,3},{3,2},{4,5},{5,4},{6,7},{7,6},{8,9},{9,8},{10,11... | collective-permute-start | bytes 577544 | tf_op jit(solution)/shard_map/ppermute | solution.py:415
  26.5 8.5 %collective-permute-start.8 = (f32[44,8,128]{2,1,0:T(8,128)S(1)}, f32[44,8,128]{2,1,0:T(8,128)S(1)}, u32[]{:S(2)}, u32[]{:S(2)}) collective-permute-start(f32[44,8,128]{2,1,0:T(8,128)S(1)} %get-tuple-element.32), channel_id=1, source_target_pairs={{0,16},{16,24},{24,8},{8,10},{10,2},{2,18},{18,26},{26,28},{28,12}... | collective-permute-start | bytes 540680 | tf_op jit(solution)/shard_map/ppermute | solution.py:418
  26.6 8.5 %collective-permute-start.9 = (f32[44,8,128]{2,1,0:T(8,128)S(1)}, f32[44,8,128]{2,1,0:T(8,128)S(1)}, u32[]{:S(2)}, u32[]{:S(2)}) collective-permute-start(f32[44,8,128]{2,1,0:T(8,128)S(1)} %get-tuple-element.33), channel_id=1, source_target_pairs={{0,6},{16,0},{24,16},{8,24},{10,8},{2,10},{18,2},{26,18},{28,26},{... | collective-permute-start | bytes 540680 | tf_op jit(solution)/shard_map/ppermute | solution.py:419
  35.1 7.1 %copy-start = (f32[19,2,16,128]{3,2,1,0:T(8,128)S(1)}, f32[19,2,16,128]{3,2,1,0:T(8,128)}, u32[]{:S(2)}) copy-start(f32[19,2,16,128]{3,2,1,0:T(8,128)} %f_ref.1) | copy-start | bytes 933892
  35.1 7.1 %copy-start.1 = (f32[2,16,128]{2,1,0:T(8,128)S(1)}, f32[2,16,128]{2,1,0:T(8,128)}, u32[]{:S(2)}) copy-start(f32[2,16,128]{2,1,0:T(8,128)} %r_ref.1) | copy-start | bytes 49156
  35.1 7.1 %copy-start.2 = (s32[2,16,128]{2,1,0:T(8,128)S(1)}, s32[2,16,128]{2,1,0:T(8,128)}, u32[]{:S(2)}) copy-start(s32[2,16,128]{2,1,0:T(8,128)} %s_ref.1) | copy-start | bytes 49156
  36.2 5.1 %collective-permute-start.10 = (f32[20,8,128]{2,1,0:T(8,128)S(1)}, f32[20,8,128]{2,1,0:T(8,128)S(1)}, u32[]{:S(2)}, u32[]{:S(2)}) collective-permute-start(f32[20,8,128]{2,1,0:T(8,128)S(1)} %get-tuple-element.35), channel_id=1, source_target_pairs={{0,8},{8,0},{16,24},{24,16},{1,9},{9,1},{17,25},{25,17},{2,10},{10... | collective-permute-start | bytes 245768 | tf_op jit(solution)/shard_map/ppermute | solution.py:411
  36.3 5.0 %collective-permute-start.11 = (f32[20,8,128]{2,1,0:T(8,128)S(1)}, f32[20,8,128]{2,1,0:T(8,128)S(1)}, u32[]{:S(2)}, u32[]{:S(2)}) collective-permute-start(f32[20,8,128]{2,1,0:T(8,128)S(1)} %get-tuple-element.36), channel_id=1, source_target_pairs={{0,16},{8,24},{16,0},{24,8},{1,17},{9,25},{17,1},{25,9},{2,18},{10... | collective-permute-start | bytes 245768 | tf_op jit(solution)/shard_map/ppermute | solution.py:411
  36.5 5.7 %collective-permute-start.12 = (f32[20,8,128]{2,1,0:T(8,128)S(1)}, f32[20,8,128]{2,1,0:T(8,128)S(1)}, u32[]{:S(2)}, u32[]{:S(2)}) collective-permute-start(f32[20,8,128]{2,1,0:T(8,128)S(1)} %get-tuple-element.37), channel_id=1, source_target_pairs={{0,24},{8,16},{16,8},{24,0},{1,25},{9,17},{17,9},{25,1},{2,26},{10... | collective-permute-start | bytes 245768 | tf_op jit(solution)/shard_map/ppermute | solution.py:411

commit v3 on v2

--- a/solution.py
+++ b/solution.py
@@ -44,11 +44,15 @@
 GROUP = 4
 ROWS = 4
 LAYERS = 2
+TRADES = (1, 3, 2)
 HALO = 3
 WIDTH = 2 * HALO
 SLOTS = 128 // WIDTH
 RES, SOL, ADJ = Q, Q + 1, Q + 2
-FIELDS = Q + 2 + Q
+DOWNWARD = [i for i in range(Q) if VELOCITIES[i][1] > 0]
+UPWARD = [i for i in range(Q) if VELOCITIES[i][1] < 0]
+EDGES = -(-len(UPWARD) // 2)
+FIELDS = ADJ + EDGES
 
 FORWARD_UP = (
     [(3, i, -1) for i in range(Q)]
@@ -120,6 +124,14 @@
         else:
             total = total + part if sign > 0 else total - part
     return total
+
+
+def inward(row, last, sign):
+    if row == 0:
+        return [i for i in range(Q) if sign * VELOCITIES[i][1] > 0]
+    if row == last:
+        return [i for i in range(Q) if sign * VELOCITIES[i][1] < 0]
+    return list(range(Q))
 
 
 def collide_lists(f, density, vx, vy, vz, resistance, solid):
@@ -197,7 +209,7 @@
     copies = [pltpu.make_async_copy(source, target, sems.at[at]) for at, (source, target) in enumerate(zip(given, held))]
     for copy in copies:
         copy.start()
-    for copy in copies:
+    for copy in copies[:3]:
         copy.wait()
     f_ref, r_ref, s_ref, a_ref = held
     for half in range(2):
@@ -207,44 +219,83 @@
             f = [f_ref[i, layer, rows, :] for i in range(Q)]
             resistance, kind = r_ref[layer, rows, :], s_ref[layer, rows, :]
             out = collide_lists(f, *moments(f), resistance, kind == 1)
-            out += [resistance, kind.astype(jnp.float32)]
-            out += [a_ref[i, layer, rows, :] for i in range(Q)]
-            tiles.append(out)
-        for field in range(FIELDS):
+            tiles.append(out + [resistance, kind.astype(jnp.float32)])
+        for field in range(ADJ):
             first, second = tiles[0][field], tiles[1][field]
             blocks[2 * half, field] = jnp.concatenate([first[:4], second[:4]], axis=0)
             blocks[2 * half + 1, field] = jnp.concatenate([first[4:], second[4:]], axis=0)
+    copies[3].wait()
+    for block in range(GROUP):
+        for edge in range(EDGES):
+            rows = []
+            for layer in range(LAYERS):
+                for group, row in ((DOWNWARD, 0), (UPWARD, ROWS - 1)):
+                    for number in (2 * edge, 2 * edge + 1):
+                        i = group[min(number, len(group) - 1)]
+                        rows.append(a_ref[i, layer, pl.ds(ROWS * block + row, 1), :])
+            blocks[block, ADJ + edge] = jnp.concatenate(rows, axis=0)
     here = lax.axis_index("gx")
     for k in range(GROUP):
         outs[k][...] = blocks[block_of(here ^ k)]
 
 
-def turn_kernel(*refs):
-    ins, (own, up, down, flat) = refs[:GROUP], refs[GROUP:]
+def send_adjoint_kernel(a_hbm, *refs):
+    outs, (blocks, a_ref, sem) = refs[:GROUP], refs[GROUP:]
+    copy = pltpu.make_async_copy(a_hbm, a_ref, sem)
+    copy.start()
+    copy.wait()
+    for block in range(GROUP):
+        for i in range(Q):
+            blocks[block, i] = jnp.concatenate([a_ref[i, layer, pl.ds(4 * block, 4), :] for layer in range(LAYERS)], axis=0)
+    here = lax.axis_index("gx")
+    for k in range(GROUP):
+        outs[k][...] = blocks[block_of(here ^ k)]
+
+
+def gather_pieces(ins, flat):
     here = lax.axis_index("gx")
     for k in range(GROUP):
         start = 8 * (here ^ k)
-        for field in range(FIELDS):
+        for field in range(flat.shape[0]):
             flat[field, pl.ds(pl.multiple_of(start, 8), 8), :] = ins[k][field]
-    for field in range(FIELDS):
+
+
+def turn_kernel(*refs):
+    ins, (own, up, down, flat) = refs[:GROUP], refs[GROUP:]
+    gather_pieces(ins, flat)
+    for field in range(ADJ):
         for row in range(ROWS):
             own[row, field] = flat[field, pl.ds(row, 8, stride=ROWS), :]
-    for number, (row, field, _) in enumerate(FORWARD_UP):
-        up[number] = own[row, field]
-    for number, (row, field, _) in enumerate(FORWARD_DOWN):
-        down[number] = own[row, field]
-
-
-def forward_kernel(own_a, own_b, lo_a, lo_b, hi_a, hi_b, lam_ref, sens_ref, mom1, mom2, rs_ref, up, down, p0, p1, p2, a4):
-    for side, own, lo, hi in ((0, own_a, lo_a, hi_a), (1, own_b, lo_b, hi_b)):
+    for table, part in ((FORWARD_UP, up), (FORWARD_DOWN, down)):
+        for number, (row, field, _) in enumerate(table):
+            if field < ADJ:
+                part[number] = own[row, field]
+            else:
+                group, base = (UPWARD, 2) if row else (DOWNWARD, 0)
+                edge, slot = divmod(group.index(field - ADJ), 2)
+                part[number] = flat[ADJ + edge, pl.ds(base + slot, 8, stride=ROWS), :]
+
+
+def turn_adjoint_kernel(*refs):
+    ins, (own, flat) = refs[:GROUP], refs[GROUP:]
+    gather_pieces(ins, flat)
+    for field in range(Q):
+        for row in range(ROWS):
+            own[row, field] = flat[field, pl.ds(row, 8, stride=ROWS), :]
+
+
+def forward_kernel(own_a, own_b, adj_a, adj_b, lo_a, lo_b, hi_a, hi_b, lam_ref, sens_ref, mom1, mom2, rs_ref, up, down, p0, p1, p2, a4):
+    for side, own, adj in ((0, own_a, adj_a), (1, own_b, adj_b)):
         lanes = slice(128 * side, 128 * side + 128)
         for row in range(ROWS):
             for i in range(Q):
                 p0[row + 3, i, :, lanes] = own[row, i]
-                a4[row + 1, i, :, lanes] = own[row, ADJ + i]
+                a4[row + 1, i, :, lanes] = adj[row, i]
             for j in range(2):
                 rs_ref[row + 2, j, :, lanes] = own[row, RES + j]
-        for table, part in ((FORWARD_UP, lo), (FORWARD_DOWN, hi)):
+    for table, parts in ((FORWARD_UP, (lo_a, lo_b)), (FORWARD_DOWN, (hi_a, hi_b))):
+        for side, part in enumerate(parts):
+            lanes = slice(128 * side, 128 * side + 128)
             for number, (_, field, row) in enumerate(table):
                 if field < Q:
                     p0[row + 3, field, :, lanes] = part[number]
@@ -256,40 +307,40 @@
     def pull(source, row):
         return [shifted(source[row + 1 - VELOCITIES[i][1], i], i, 1) for i in range(Q)]
 
-    def first(row, _):
+    def first(row):
         f = pull(p0, row)
         moment = moments(f)
         for j in range(4):
             mom1[row, j] = moment[j]
         out = collide_lists(f, *moment, rs_ref[row, 0], rs_ref[row, 1] == 1.0)
-        for i in range(Q):
+        for i in inward(row, ROWS + 3, 1):
             p1[row, i] = out[i]
-        return 0
-
-    lax.fori_loop(0, ROWS + 4, first, 0, unroll=True)
-
-    def second(row, _):
+
+    for row in range(ROWS + 4):
+        first(row)
+
+    def second(row):
         f = pull(p1, row)
         moment = moments(f)
         for j in range(4):
             mom2[row + 1, j] = moment[j]
         out = collide_lists(f, *moment, rs_ref[row + 1, 0], rs_ref[row + 1, 1] == 1.0)
-        for i in range(Q):
+        for i in inward(row, ROWS + 1, 1):
             p2[row, i] = out[i]
-        return 0
-
-    lax.fori_loop(0, ROWS + 2, second, 0, unroll=True)
-
-    def third(row, _):
+
+    for row in range(ROWS + 2):
+        second(row)
+
+    def third(row):
         moment = moments(pull(p2, row))
         mu = [shifted(a4[row + 1 + VELOCITIES[i][1], i], i, -1) for i in range(Q)]
         out, design = adjoint_lists(mu, *moment, rs_ref[row + 2, 0], rs_ref[row + 2, 1] == 1.0)
         for i in range(Q):
             lam_ref[row, i] = out[i]
         sens_ref[row] = design[:, :128]
-        return 0
-
-    lax.fori_loop(0, ROWS, third, 0, unroll=True)
+
+    for row in range(ROWS):
+        third(row)
     for table, part in ((BACKWARD_UP, up), (BACKWARD_DOWN, down)):
         others = []
         for number, (row, field, _) in enumerate(table):
@@ -321,32 +372,33 @@
     def pull(source, row):
         return [shifted(source[row + 1 + VELOCITIES[i][1], i], i, -1) for i in range(Q)]
 
-    designs = flat.at[Q]
-
-    def second(row, _):
+    designs = {}
+
+    def second(row):
         mu = pull(l3, row)
         out, design = adjoint_lists(mu, *[m2[row, j] for j in range(4)], rs_ref[row, 0], rs_ref[row, 1] == 1.0)
-        for i in range(Q):
+        for i in inward(row, ROWS + 3, -1):
             l2[row, i] = out[i]
-        l1[row, 0] = design
-        return 0
-
-    lax.fori_loop(0, ROWS + 4, second, 0, unroll=True)
-    total = [sens_ref[row] + l1[row + 2, 0, :, :128] for row in range(ROWS)]
-
-    def first(row, _):
+        if 2 <= row < ROWS + 2:
+            designs[row - 2] = design
+
+    for row in range(ROWS + 4):
+        second(row)
+
+    def first(row):
         mu = pull(l2, row)
         out, design = adjoint_lists(
             mu, *[mom1[row + 1, j] for j in range(4)], rs_ref[row + 1, 0], rs_ref[row + 1, 1] == 1.0
         )
-        for i in range(Q):
+        for i in inward(row, ROWS + 1, -1):
             l1[row, i] = out[i]
-        m2[row, 0] = design
-        return 0
-
-    lax.fori_loop(0, ROWS + 2, first, 0, unroll=True)
+        if 1 <= row < ROWS + 1:
+            designs[row - 1] = designs[row - 1] + design
+
+    for row in range(ROWS + 2):
+        first(row)
     for row in range(ROWS):
-        designs[pl.ds(row, 8, stride=ROWS), :] = total[row] + m2[row + 1, 0, :, :128]
+        flat[Q, pl.ds(row, 8, stride=ROWS), :] = sens_ref[row] + designs[row][:, :128]
         mu = pull(l1, row)
         for i in range(Q):
             flat[i, pl.ds(row, 8, stride=ROWS), :] = mu[i][:, :128]
@@ -394,21 +446,17 @@
     for plane in range(planes):
         for block in range(GROUP):
             gray = (plane - block) % GROUP
-            order.append((gray ^ (gray >> 1), plane))
-    pairs = []
-    for at, (number, plane) in enumerate(order):
-        other, beyond = order[(at + step) % len(order)]
-        pairs.append((number * planes + plane, other * planes + beyond))
-    return pairs
+            order.append((gray ^ (gray >> 1)) * planes + plane)
+    return [(here, order[(at + step) % len(order)]) for at, here in enumerate(order)]
 
 
 def fast_body(checkpoint, resistance, solid, adjoint_final):
     planes = lax.axis_size("gy")
 
     def trade(pieces):
-        moved = [pieces[0]]
-        for k in range(1, GROUP):
-            moved.append(lax.ppermute(pieces[k], "gx", [(i, i ^ k) for i in range(GROUP)]))
+        moved = list(pieces)
+        for k in TRADES:
+            moved[k] = lax.ppermute(pieces[k], "gx", [(i, i ^ k) for i in range(GROUP)])
         return moved
 
     def swap(value):
@@ -429,14 +477,24 @@
         *[pltpu.with_memory_space_constraint(array, pltpu.HBM) for array in given],
         space=pltpu.HBM,
     )
-    pieces = trade(pieces)
+    fenced = lax.optimization_barrier((adjoint_final, *pieces))
+    adjoint_pieces = call(
+        send_adjoint_kernel,
+        [(Q, 8, 128)] * GROUP,
+        [(GROUP, Q, 8, 128), pltpu.VMEM(adjoint_final.shape, jnp.float32), pltpu.SemaphoreType.DMA],
+        pltpu.with_memory_space_constraint(fenced[0], pltpu.HBM),
+        space=pltpu.HBM,
+    )
+    pieces = trade(fenced[1:])
     own, up, down = call(
         turn_kernel,
-        [(ROWS, FIELDS, 8, 128), (len(FORWARD_UP), 8, 128), (len(FORWARD_DOWN), 8, 128)],
+        [(ROWS, ADJ, 8, 128), (len(FORWARD_UP), 8, 128), (len(FORWARD_DOWN), 8, 128)],
         [(FIELDS, 8 * ROWS, 128)],
         *pieces,
     )
     own_b = swap(own)
+    (adj,) = call(turn_adjoint_kernel, [(ROWS, Q, 8, 128)], [(Q, 8 * ROWS, 128)], *trade(adjoint_pieces))
+    adj_b = swap(adj)
     lo, hi = ring(up, down)
     lo_b, hi_b = swap(lo), swap(hi)
     lam, sens, mom1, mom2, rs, up, down = call(
@@ -453,6 +511,8 @@
         [(ROWS + 6, Q, 8, 256), (ROWS + 4, Q, 8, 256), (ROWS + 2, Q, 8, 256), (ROWS + 2, Q, 8, 256)],
         own,
         own_b,
+        adj,
+        adj_b,
         lo,
         lo_b,
         hi,

time: 43.3 us -> 39.9 us (0.921)
  waiting for transfers between devices: 21.1 us -> 13.1 us
  starting transfers between devices: 16.4 us -> 20.1 us
  Pallas kernels: 4.86 us -> 5.76 us
    ppermute x6 -> x9, waiting for transfers between devices: 10 us -> 4.34 us  [trade(): moved[k] = lax.ppermute(pieces[k], 'gx', [(i, i ^ k) for i in range(GROUP)])]
    ppermute x6 -> x9, starting transfers between devices: 8.09 us -> 11.8 us  [trade(): moved[k] = lax.ppermute(pieces[k], 'gx', [(i, i ^ k) for i in range(GROUP)])]
    ppermute x2, waiting for transfers between devices: 9.86 us -> 7.52 us  [ring(): lo = lax.ppermute(up, ('gx', 'gy'), ring_pairs(planes, 1))]
    pallas_call x5 -> x7, Pallas kernels: 4.86 us -> 5.76 us  [call(): pl.pallas_call(kernel, out_shape=[jax.ShapeDtypeStruct(shape, jnp.float32...]
    ppermute x2, starting transfers between devices: 6.12 us -> 6.99 us  [ring(): hi = lax.ppermute(down, ('gx', 'gy'), ring_pairs(planes, -1))]
    ppermute x2, starting transfers between devices: 1.63 us -> 0.76 us  [ring(): lo = lax.ppermute(up, ('gx', 'gy'), ring_pairs(planes, 1))]
    ppermute x3 -> x4, waiting for transfers between devices: 1.2 us -> 1.2 us  [swap(): return lax.ppermute(value, 'gz', [(0, 1), (1, 0)])]
  transfers between devices with their start and end apart: 13 -> 17, of which waited for: 8 -> 8; matrix products, arithmetic and copies ran while one was open for 0% -> 0% of each run, Pallas kernels for 0% -> 3%
where the time goes in v3:
time: 39.9 us; the launch traced here: 39.7 us
  starting transfers between devices  20.1 us (50%)
  waiting for transfers between devices  13.1 us (33%)
  Pallas kernels  5.76 us (14%)
  between operations  0.73 us (2%)
    ppermute x9, starting transfers between devices, trade(): moved[k] = lax.ppermute(pieces[k], 'gx', [(i, i ^ k) for i in range(GROUP)])  11.8 us
    ppermute x2, waiting for transfers between devices, ring(): lo = lax.ppermute(up, ('gx', 'gy'), ring_pairs(planes, 1))  7.52 us
    ppermute x2, starting transfers between devices, ring(): hi = lax.ppermute(down, ('gx', 'gy'), ring_pairs(planes, -1))  6.99 us
    pallas_call x7, Pallas kernels, call(): pl.pallas_call(kernel, out_shape=[jax.ShapeDtypeStruct(shape, jnp.float32...  5.76 us
    ppermute x9, waiting for transfers between devices, trade(): moved[k] = lax.ppermute(pieces[k], 'gx', [(i, i ^ k) for i in range(GROUP)])  4.34 us
    ppermute x4, waiting for transfers between devices, swap(): return lax.ppermute(value, 'gz', [(0, 1), (1, 0)])  1.2 us
  transfers between devices with their start and end apart: 17, of which 8 were waited for; matrix products, arithmetic and copies ran while one was open for 0% of the time, Pallas kernels for 3%

profile of v3, /device:TPU:0, one launch (start us, length us, event | category | flops | bytes accessed | tf_op | source)
XLA Modules:
  0.0 39.7 jit_solution(13498600712155643713)
XLA Ops:
  0.6 1.2 %shard_map.59 = (f32[24,8,128]{2,1,0:T(8,128)S(1)}, f32[24,8,128]{2,1,0:T(8,128)S(1)}, f32[24,8,128]{2,1,0:T(8,128)S(1)}, f32[24,8,128]{2,1,0:T(8,128)S(1)}) custom-call(f32[19,2,16,128]{3,2,1,0:T(8,128)} %f_ref.1, f32[2,16,128]{2,1,0:T(8,128)} %r_ref.1, s32[2,16,128]{2,1,0:T(8,128)} %s_ref.1, f32[19,2,16,128]{3,2,1,0:T(8,128)} %a_hbm), custom_call_target="tpu_custom_call" | custom-call | tf_op jit(solution)/shard_map/pallas_call | solution.py:434
  1.9 3.0 %collective-permute-start = (f32[24,8,128]{2,1,0:T(8,128)S(1)}, f32[24,8,128]{2,1,0:T(8,128)S(1)}, u32[]{:S(2)}, u32[]{:S(2)}) collective-permute-start(f32[24,8,128]{2,1,0:T(8,128)S(1)} %get-tuple-element.34), channel_id=1, source_target_pairs={{0,8},{8,0},{16,24},{24,16},{1,9},{9,1},{17,25},{25,17},{2,10},{10... | collective-permute-start | bytes 294920 | tf_op jit(solution)/shard_map/ppermute | solution.py:459
  4.9 1.5 %collective-permute-start.1 = (f32[24,8,128]{2,1,0:T(8,128)S(1)}, f32[24,8,128]{2,1,0:T(8,128)S(1)}, u32[]{:S(2)}, u32[]{:S(2)}) collective-permute-start(f32[24,8,128]{2,1,0:T(8,128)S(1)} %get-tuple-element.35), channel_id=1, source_target_pairs={{0,16},{8,24},{16,0},{24,8},{1,17},{9,25},{17,1},{25,9},{2,18},{10... | collective-permute-start | bytes 294920 | tf_op jit(solution)/shard_map/ppermute | solution.py:459
  6.4 0.0 collective-permute-start.2
  6.4 1.0 %shard_map.61 = (f32[19,8,128]{2,1,0:T(8,128)S(1)}, f32[19,8,128]{2,1,0:T(8,128)S(1)}, f32[19,8,128]{2,1,0:T(8,128)S(1)}, f32[19,8,128]{2,1,0:T(8,128)S(1)}) custom-call(f32[19,2,16,128]{3,2,1,0:T(8,128)} %a_hbm), custom_call_target="tpu_custom_call" | custom-call | tf_op jit(solution)/shard_map/pallas_call | solution.py:434
  7.4 2.0 %collective-permute-start.4 = (f32[19,8,128]{2,1,0:T(8,128)S(1)}, f32[19,8,128]{2,1,0:T(8,128)S(1)}, u32[]{:S(2)}, u32[]{:S(2)}) collective-permute-start(f32[19,8,128]{2,1,0:T(8,128)S(1)} %get-tuple-element.40), channel_id=1, source_target_pairs={{0,8},{8,0},{16,24},{24,16},{1,9},{9,1},{17,25},{25,17},{2,10},{10... | collective-permute-start | bytes 233480 | tf_op jit(solution)/shard_map/ppermute | solution.py:459
  9.5 1.5 %collective-permute-start.5 = (f32[19,8,128]{2,1,0:T(8,128)S(1)}, f32[19,8,128]{2,1,0:T(8,128)S(1)}, u32[]{:S(2)}, u32[]{:S(2)}) collective-permute-start(f32[19,8,128]{2,1,0:T(8,128)S(1)} %get-tuple-element.41), channel_id=1, source_target_pairs={{0,16},{8,24},{16,0},{24,8},{1,17},{9,25},{17,1},{25,9},{2,18},{10... | collective-permute-start | bytes 233480 | tf_op jit(solution)/shard_map/ppermute | solution.py:459
  11.0 0.0 collective-permute-done.refs_1_
  11.0 0.2 collective-permute-start.6
  11.2 0.0 collective-permute-done.1.refs_2_
  11.2 1.3 %collective-permute-done.2.refs_3_ = f32[24,8,128]{2,1,0:T(8,128)S(1)} collective-permute-done((f32[24,8,128]{2,1,0:T(8,128)S(1)}, f32[24,8,128]{2,1,0:T(8,128)S(1)}, u32[]{:S(2)}, u32[]{:S(2)}) %collective-permute-start.2) | collective-permute-done | bytes 98336 | tf_op jit(solution)/shard_map/ppermute | solution.py:459
  12.5 0.1 shard_map.60
  12.6 0.5 %collective-permute-start.8 = (f32[47,8,128]{2,1,0:T(8,128)S(1)}, f32[47,8,128]{2,1,0:T(8,128)S(1)}, u32[]{:S(2)}, u32[]{:S(2)}) collective-permute-start(f32[47,8,128]{2,1,0:T(8,128)S(1)} %get-tuple-element.43), channel_id=1, source_target_pairs={{0,16},{16,24},{24,8},{8,10},{10,2},{2,18},{18,26},{26,28},{28,12}... | collective-permute-start | bytes 577544 | tf_op jit(solution)/shard_map/ppermute | solution.py:466
  13.2 3.3 %collective-permute-start.10 = (f32[47,8,128]{2,1,0:T(8,128)S(1)}, f32[47,8,128]{2,1,0:T(8,128)S(1)}, u32[]{:S(2)}, u32[]{:S(2)}) collective-permute-start(f32[47,8,128]{2,1,0:T(8,128)S(1)} %get-tuple-element.44), channel_id=1, source_target_pairs={{0,6},{16,0},{24,16},{8,24},{10,8},{2,10},{18,2},{26,18},{28,26},{... | collective-permute-start | bytes 577544 | tf_op jit(solution)/shard_map/ppermute | solution.py:467
  16.5 0.0 collective-permute-done.4.refs_1_
  16.5 0.0 collective-permute-start.3
  16.5 0.0 collective-permute-done.5.refs_2_
  16.5 0.6 %collective-permute-done.6.refs_3_ = f32[19,8,128]{2,1,0:T(8,128)S(1)} collective-permute-done((f32[19,8,128]{2,1,0:T(8,128)S(1)}, f32[19,8,128]{2,1,0:T(8,128)S(1)}, u32[]{:S(2)}, u32[]{:S(2)}) %collective-permute-start.6) | collective-permute-done | bytes 77856 | tf_op jit(solution)/shard_map/ppermute | solution.py:459
  17.1 0.1 shard_map.62.adj_a
  17.2 0.1 collective-permute-start.7
  17.2 2.9 %collective-permute-done.8.lo_a = f32[47,8,128]{2,1,0:T(8,128)S(1)} collective-permute-done((f32[47,8,128]{2,1,0:T(8,128)S(1)}, f32[47,8,128]{2,1,0:T(8,128)S(1)}, u32[]{:S(2)}, u32[]{:S(2)}) %collective-permute-start.8) | collective-permute-done | bytes 192544 | tf_op jit(solution)/shard_map/ppermute | solution.py:466
  20.1 0.0 collective-permute-start.9
  20.1 0.0 collective-permute-done.10.hi_a
  20.1 0.5 %collective-permute-start.11 = (f32[47,8,128]{2,1,0:T(8,128)S(1)}, f32[47,8,128]{2,1,0:T(8,128)S(1)}, u32[]{:S(2)}, u32[]{:S(2)}) collective-permute-start(f32[47,8,128]{2,1,0:T(8,128)S(1)} %collective-permute-done.10.hi_a), channel_id=1, source_target_pairs={{0,1},{1,0},{2,3},{3,2},{4,5},{5,4},{6,7},{7,6},{8,9},{9,8},{10,11... | collective-permute-start | bytes 577544 | tf_op jit(solution)/shard_map/ppermute | solution.py:463
  20.6 0.0 collective-permute-done.7.adj_b
  20.6 0.0 collective-permute-done.3.own_b
  20.6 0.9 %collective-permute-done.9.lo_b = f32[47,8,128]{2,1,0:T(8,128)S(1)} collective-permute-done((f32[47,8,128]{2,1,0:T(8,128)S(1)}, f32[47,8,128]{2,1,0:T(8,128)S(1)}, u32[]{:S(2)}, u32[]{:S(2)}) %collective-permute-start.9) | collective-permute-done | bytes 192544 | tf_op jit(solution)/shard_map/ppermute | solution.py:463
  21.5 0.3 collective-permute-done.11.hi_b
  21.8 1.3 %shard_map.63 = (f32[4,19,8,256]{3,2,1,0:T(8,128)S(1)}, f32[4,8,128]{2,1,0:T(8,128)S(1)}, f32[8,4,8,256]{3,2,1,0:T(8,128)S(1)}, f32[8,4,8,256]{3,2,1,0:T(8,128)S...) custom-call(f32[4,21,8,128]{3,2,1,0:T(8,128)S(1)} %get-tuple-element.37.own_a, ...), custom_call_target="tpu_custom_call" | custom-call | tf_op jit(solution)/shard_map/pallas_call | solution.py:434
  23.1 0.2 collective-permute-start.12
  23.4 3.7 %collective-permute-start.13 = (f32[44,8,128]{2,1,0:T(8,128)S(1)}, f32[44,8,128]{2,1,0:T(8,128)S(1)}, u32[]{:S(2)}, u32[]{:S(2)}) collective-permute-start(f32[44,8,128]{2,1,0:T(8,128)S(1)} %get-tuple-element.51), channel_id=1, source_target_pairs={{0,6},{16,0},{24,16},{8,24},{10,8},{2,10},{18,2},{26,18},{28,26},{... | collective-permute-start | bytes 540680 | tf_op jit(solution)/shard_map/ppermute | solution.py:467
  27.0 4.7 %collective-permute-done.12.lo = f32[44,8,128]{2,1,0:T(8,128)S(1)} collective-permute-done((f32[44,8,128]{2,1,0:T(8,128)S(1)}, f32[44,8,128]{2,1,0:T(8,128)S(1)}, u32[]{:S(2)}, u32[]{:S(2)}) %collective-permute-start.12) | collective-permute-done | bytes 180256 | tf_op jit(solution)/shard_map/ppermute | solution.py:466
  31.7 0.0 collective-permute-done.13.hi
  31.7 0.0 copy-start
  31.7 0.0 copy-start.1
  31.7 0.0 copy-start.2
  31.7 1.1 %shard_map.64 = (f32[20,8,128]{2,1,0:T(8,128)S(1)}, f32[20,8,128]{2,1,0:T(8,128)S(1)}, f32[20,8,128]{2,1,0:T(8,128)S(1)}, f32[20,8,128]{2,1,0:T(8,128)S(1)}) custom-call(f32[4,19,8,256]{3,2,1,0:T(8,128)S(1)} %get-tuple-element.45.lam_ref, f32[4,8,128]{2,1,0:T(8,128)S(1)} %get-tuple-element.46.sens_ref, f32[8,4,8,256]{3,2,1,0:T(8,128)S(1)} %get-tuple-element.47.mom1, ...), custom_call_target="tpu_custom_call" | custom-call | tf_op jit(solution)/shard_map/pallas_call | solution.py:434
  32.8 0.1 collective-permute-start.14
  32.9 0.1 collective-permute-start.15
  32.9 3.4 %collective-permute-start.16 = (f32[20,8,128]{2,1,0:T(8,128)S(1)}, f32[20,8,128]{2,1,0:T(8,128)S(1)}, u32[]{:S(2)}, u32[]{:S(2)}) collective-permute-start(f32[20,8,128]{2,1,0:T(8,128)S(1)} %get-tuple-element.55), channel_id=1, source_target_pairs={{0,24},{8,16},{16,8},{24,0},{1,25},{9,17},{17,9},{25,1},{2,26},{10... | collective-permute-start | bytes 245768 | tf_op jit(solution)/shard_map/ppermute | solution.py:459
  36.3 1.5 %collective-permute-done.14.refs_1_ = f32[20,8,128]{2,1,0:T(8,128)S(1)} collective-permute-done((f32[20,8,128]{2,1,0:T(8,128)S(1)}, f32[20,8,128]{2,1,0:T(8,128)S(1)}, u32[]{:S(2)}, u32[]{:S(2)}) %collective-permute-start.14) | collective-permute-done | bytes 81952 | tf_op jit(solution)/shard_map/ppermute | solution.py:459
  37.9 0.0 collective-permute-done.15.refs_2_
  37.9 0.9 %collective-permute-done.16.refs_3_ = f32[20,8,128]{2,1,0:T(8,128)S(1)} collective-permute-done((f32[20,8,128]{2,1,0:T(8,128)S(1)}, f32[20,8,128]{2,1,0:T(8,128)S(1)}, u32[]{:S(2)}, u32[]{:S(2)}) %collective-permute-start.16) | collective-permute-done | bytes 81952 | tf_op jit(solution)/shard_map/ppermute | solution.py:459
  38.8 0.0 copy-done
  38.8 0.0 copy-done.1
  38.8 0.0 copy-done.2
  38.8 0.9 %shard_map.65 = (f32[19,2,16,128]{3,2,1,0:T(8,128)}, f32[2,16,128]{2,1,0:T(8,128)}) custom-call(f32[19,2,16,128]{3,2,1,0:T(8,128)S(1)} %copy-done, f32[2,16,128]{2,1,0:T(8,128)S(1)} %copy-done.1, s32[2,16,128]{2,1,0:T(8,128)S(1)} %copy-done.2, f32[20,8,128]{2,1,0:T(8,128)S(1)} %get-tuple-element.52.refs_0_, ...), custom_call_target="tpu_custom_call" | custom-call | tf_op jit(solution)/shard_map/pallas_call | solution.py:434
Async XLA Ops:
  1.9 9.1 %collective-permute-start = (f32[24,8,128]{2,1,0:T(8,128)S(1)}, f32[24,8,128]{2,1,0:T(8,128)S(1)}, u32[]{:S(2)}, u32[]{:S(2)}) collective-permute-start(f32[24,8,128]{2,1,0:T(8,128)S(1)} %get-tuple-element.34), channel_id=1, source_target_pairs={{0,8},{8,0},{16,24},{24,16},{1,9},{9,1},{17,25},{25,17},{2,10},{10... | collective-permute-start | bytes 294920 | tf_op jit(solution)/shard_map/ppermute | solution.py:459
  4.9 6.3 %collective-permute-start.1 = (f32[24,8,128]{2,1,0:T(8,128)S(1)}, f32[24,8,128]{2,1,0:T(8,128)S(1)}, u32[]{:S(2)}, u32[]{:S(2)}) collective-permute-start(f32[24,8,128]{2,1,0:T(8,128)S(1)} %get-tuple-element.35), channel_id=1, source_target_pairs={{0,16},{8,24},{16,0},{24,8},{1,17},{9,25},{17,1},{25,9},{2,18},{10... | collective-permute-start | bytes 294920 | tf_op jit(solution)/shard_map/ppermute | solution.py:459
  6.4 6.1 %collective-permute-start.2 = (f32[24,8,128]{2,1,0:T(8,128)S(1)}, f32[24,8,128]{2,1,0:T(8,128)S(1)}, u32[]{:S(2)}, u32[]{:S(2)}) collective-permute-start(f32[24,8,128]{2,1,0:T(8,128)S(1)} %get-tuple-element.36), channel_id=1, source_target_pairs={{0,24},{8,16},{16,8},{24,0},{1,25},{9,17},{17,9},{25,1},{2,26},{10... | collective-permute-start | bytes 294920 | tf_op jit(solution)/shard_map/ppermute | solution.py:459
  7.4 9.1 %collective-permute-start.4 = (f32[19,8,128]{2,1,0:T(8,128)S(1)}, f32[19,8,128]{2,1,0:T(8,128)S(1)}, u32[]{:S(2)}, u32[]{:S(2)}) collective-permute-start(f32[19,8,128]{2,1,0:T(8,128)S(1)} %get-tuple-element.40), channel_id=1, source_target_pairs={{0,8},{8,0},{16,24},{24,16},{1,9},{9,1},{17,25},{25,17},{2,10},{10... | collective-permute-start | bytes 233480 | tf_op jit(solution)/shard_map/ppermute | solution.py:459
  9.5 7.0 %collective-permute-start.5 = (f32[19,8,128]{2,1,0:T(8,128)S(1)}, f32[19,8,128]{2,1,0:T(8,128)S(1)}, u32[]{:S(2)}, u32[]{:S(2)}) collective-permute-start(f32[19,8,128]{2,1,0:T(8,128)S(1)} %get-tuple-element.41), channel_id=1, source_target_pairs={{0,16},{8,24},{16,0},{24,8},{1,17},{9,25},{17,1},{25,9},{2,18},{10... | collective-permute-start | bytes 233480 | tf_op jit(solution)/shard_map/ppermute | solution.py:459
  11.0 6.1 %collective-permute-start.6 = (f32[19,8,128]{2,1,0:T(8,128)S(1)}, f32[19,8,128]{2,1,0:T(8,128)S(1)}, u32[]{:S(2)}, u32[]{:S(2)}) collective-permute-start(f32[19,8,128]{2,1,0:T(8,128)S(1)} %get-tuple-element.42), channel_id=1, source_target_pairs={{0,24},{8,16},{16,8},{24,0},{1,25},{9,17},{17,9},{25,1},{2,26},{10... | collective-permute-start | bytes 233480 | tf_op jit(solution)/shard_map/ppermute | solution.py:459
  12.6 7.5 %collective-permute-start.8 = (f32[47,8,128]{2,1,0:T(8,128)S(1)}, f32[47,8,128]{2,1,0:T(8,128)S(1)}, u32[]{:S(2)}, u32[]{:S(2)}) collective-permute-start(f32[47,8,128]{2,1,0:T(8,128)S(1)} %get-tuple-element.43), channel_id=1, source_target_pairs={{0,16},{16,24},{24,8},{8,10},{10,2},{2,18},{18,26},{26,28},{28,12}... | collective-permute-start | bytes 577544 | tf_op jit(solution)/shard_map/ppermute | solution.py:466
  13.2 7.0 %collective-permute-start.10 = (f32[47,8,128]{2,1,0:T(8,128)S(1)}, f32[47,8,128]{2,1,0:T(8,128)S(1)}, u32[]{:S(2)}, u32[]{:S(2)}) collective-permute-start(f32[47,8,128]{2,1,0:T(8,128)S(1)} %get-tuple-element.44), channel_id=1, source_target_pairs={{0,6},{16,0},{24,16},{8,24},{10,8},{2,10},{18,2},{26,18},{28,26},{... | collective-permute-start | bytes 577544 | tf_op jit(solution)/shard_map/ppermute | solution.py:467
  16.5 4.1 %collective-permute-start.3 = (f32[4,21,8,128]{3,2,1,0:T(8,128)S(1)}, f32[4,21,8,128]{3,2,1,0:T(8,128)S(1)}, u32[]{:S(2)}, u32[]{:S(2)}) collective-permute-start(f32[4,21,8,128]{3,2,1,0:T(8,128)S(1)} %get-tuple-element.37.own_a), channel_id=1, source_target_pairs={{0,1},{1,0},{2,3},{3,2},{4,5},{5,4},{6,7},{7,6},{8,9},{9,8},{10,11... | collective-permute-start | bytes 1032200 | tf_op jit(solution)/shard_map/ppermute | solution.py:463
  17.2 3.4 %collective-permute-start.7 = (f32[4,19,8,128]{3,2,1,0:T(8,128)S(1)}, f32[4,19,8,128]{3,2,1,0:T(8,128)S(1)}, u32[]{:S(2)}, u32[]{:S(2)}) collective-permute-start(f32[4,19,8,128]{3,2,1,0:T(8,128)S(1)} %shard_map.62.adj_a), channel_id=1, source_target_pairs={{0,1},{1,0},{2,3},{3,2},{4,5},{5,4},{6,7},{7,6},{8,9},{9,8},{10,11... | collective-permute-start | bytes 933896 | tf_op jit(solution)/shard_map/ppermute | solution.py:463
  20.1 1.4 %collective-permute-start.9 = (f32[47,8,128]{2,1,0:T(8,128)S(1)}, f32[47,8,128]{2,1,0:T(8,128)S(1)}, u32[]{:S(2)}, u32[]{:S(2)}) collective-permute-start(f32[47,8,128]{2,1,0:T(8,128)S(1)} %collective-permute-done.8.lo_a), channel_id=1, source_target_pairs={{0,1},{1,0},{2,3},{3,2},{4,5},{5,4},{6,7},{7,6},{8,9},{9,8},{10,11... | collective-permute-start | bytes 577544 | tf_op jit(solution)/shard_map/ppermute | solution.py:463
  20.1 1.7 %collective-permute-start.11 = (f32[47,8,128]{2,1,0:T(8,128)S(1)}, f32[47,8,128]{2,1,0:T(8,128)S(1)}, u32[]{:S(2)}, u32[]{:S(2)}) collective-permute-start(f32[47,8,128]{2,1,0:T(8,128)S(1)} %collective-permute-done.10.hi_a), channel_id=1, source_target_pairs={{0,1},{1,0},{2,3},{3,2},{4,5},{5,4},{6,7},{7,6},{8,9},{9,8},{10,11... | collective-permute-start | bytes 577544 | tf_op jit(solution)/shard_map/ppermute | solution.py:463
  23.1 8.5 %collective-permute-start.12 = (f32[44,8,128]{2,1,0:T(8,128)S(1)}, f32[44,8,128]{2,1,0:T(8,128)S(1)}, u32[]{:S(2)}, u32[]{:S(2)}) collective-permute-start(f32[44,8,128]{2,1,0:T(8,128)S(1)} %get-tuple-element.50), channel_id=1, source_target_pairs={{0,16},{16,24},{24,8},{8,10},{10,2},{2,18},{18,26},{26,28},{28,12}... | collective-permute-start | bytes 540680 | tf_op jit(solution)/shard_map/ppermute | solution.py:466
  23.4 8.3 %collective-permute-start.13 = (f32[44,8,128]{2,1,0:T(8,128)S(1)}, f32[44,8,128]{2,1,0:T(8,128)S(1)}, u32[]{:S(2)}, u32[]{:S(2)}) collective-permute-start(f32[44,8,128]{2,1,0:T(8,128)S(1)} %get-tuple-element.51), channel_id=1, source_target_pairs={{0,6},{16,0},{24,16},{8,24},{10,8},{2,10},{18,2},{26,18},{28,26},{... | collective-permute-start | bytes 540680 | tf_op jit(solution)/shard_map/ppermute | solution.py:467
  31.7 7.1 %copy-start = (f32[19,2,16,128]{3,2,1,0:T(8,128)S(1)}, f32[19,2,16,128]{3,2,1,0:T(8,128)}, u32[]{:S(2)}) copy-start(f32[19,2,16,128]{3,2,1,0:T(8,128)} %f_ref.1) | copy-start | bytes 933892
  31.7 7.1 %copy-start.1 = (f32[2,16,128]{2,1,0:T(8,128)S(1)}, f32[2,16,128]{2,1,0:T(8,128)}, u32[]{:S(2)}) copy-start(f32[2,16,128]{2,1,0:T(8,128)} %r_ref.1) | copy-start | bytes 49156
  31.7 7.1 %copy-start.2 = (s32[2,16,128]{2,1,0:T(8,128)S(1)}, s32[2,16,128]{2,1,0:T(8,128)}, u32[]{:S(2)}) copy-start(s32[2,16,128]{2,1,0:T(8,128)} %s_ref.1) | copy-start | bytes 49156
  32.8 5.1 %collective-permute-start.14 = (f32[20,8,128]{2,1,0:T(8,128)S(1)}, f32[20,8,128]{2,1,0:T(8,128)S(1)}, u32[]{:S(2)}, u32[]{:S(2)}) collective-permute-start(f32[20,8,128]{2,1,0:T(8,128)S(1)} %get-tuple-element.53), channel_id=1, source_target_pairs={{0,8},{8,0},{16,24},{24,16},{1,9},{9,1},{17,25},{25,17},{2,10},{10... | collective-permute-start | bytes 245768 | tf_op jit(solution)/shard_map/ppermute | solution.py:459
  32.9 5.0 %collective-permute-start.15 = (f32[20,8,128]{2,1,0:T(8,128)S(1)}, f32[20,8,128]{2,1,0:T(8,128)S(1)}, u32[]{:S(2)}, u32[]{:S(2)}) collective-permute-start(f32[20,8,128]{2,1,0:T(8,128)S(1)} %get-tuple-element.54), channel_id=1, source_target_pairs={{0,16},{8,24},{16,0},{24,8},{1,17},{9,25},{17,1},{25,9},{2,18},{10... | collective-permute-start | bytes 245768 | tf_op jit(solution)/shard_map/ppermute | solution.py:459
  32.9 5.8 %collective-permute-start.16 = (f32[20,8,128]{2,1,0:T(8,128)S(1)}, f32[20,8,128]{2,1,0:T(8,128)S(1)}, u32[]{:S(2)}, u32[]{:S(2)}) collective-permute-start(f32[20,8,128]{2,1,0:T(8,128)S(1)} %get-tuple-element.55), channel_id=1, source_target_pairs={{0,24},{8,16},{16,8},{24,0},{1,25},{9,17},{17,9},{25,1},{2,26},{10... | collective-permute-start | bytes 245768 | tf_op jit(solution)/shard_map/ppermute | solution.py:459

commit v4 on v3

--- a/solution.py
+++ b/solution.py
@@ -45,9 +45,7 @@
 ROWS = 4
 LAYERS = 2
 TRADES = (1, 3, 2)
-HALO = 3
-WIDTH = 2 * HALO
-SLOTS = 128 // WIDTH
+FORWARD_REACH, BACKWARD_REACH = 6, 3
 RES, SOL, ADJ = Q, Q + 1, Q + 2
 DOWNWARD = [i for i in range(Q) if VELOCITIES[i][1] > 0]
 UPWARD = [i for i in range(Q) if VELOCITIES[i][1] < 0]
@@ -68,6 +66,8 @@
     + [(0, RES, 4), (0, SOL, 4), (1, RES, 5), (1, SOL, 5)]
     + [(0, ADJ + i, 4) for i in range(Q) if VELOCITIES[i][1] > 0]
 )
+OWN = [(row, field) for row in range(ROWS) for field in range(ADJ)]
+OWN_ADJOINT = [(row, field) for row in range(ROWS) for field in range(Q)]
 BACKWARD_UP = (
     [(3, i, -1) for i in range(Q)]
     + [(2, i, -2) for i in range(Q) if VELOCITIES[i][1] <= 0]
@@ -93,25 +93,30 @@
     return density, first * inverse, second * inverse, third * inverse
 
 
-def strip_count(table):
-    return -(-len(table) // SLOTS)
-
-
-def pack_strips(tiles):
+def slots_of(reach):
+    return 128 // (2 * reach)
+
+
+def strip_count(table, reach):
+    return -(-len(table) // slots_of(reach))
+
+
+def pack_strips(tiles, reach):
     lane = lax.broadcasted_iota(jnp.int32, (8, 128), 1)
     packed = []
     for number, tile in enumerate(tiles):
-        slot = number % SLOTS
-        moved = pltpu.roll(tile, (WIDTH * slot + HALO) % 128, axis=1)
-        if slot == 0:
+        start = 2 * reach * (number % slots_of(reach))
+        moved = pltpu.roll(tile, start + reach, axis=1)
+        if start == 0:
             packed.append(moved)
         else:
-            packed[-1] = jnp.where(lane >= WIDTH * slot, moved, packed[-1])
+            packed[-1] = jnp.where(lane >= start, moved, packed[-1])
     return packed
 
 
-def unpack_strip(packed, number):
-    return pltpu.roll(packed, (-WIDTH * (number % SLOTS) - HALO) % 128, axis=1)
+def unpack_strip(packed, number, reach):
+    start = 2 * reach * (number % slots_of(reach))
+    return pltpu.roll(packed[number // slots_of(reach)], 128 - start - reach, axis=1)
 
 
 def along(i, x, y, z):
@@ -277,129 +282,121 @@
 
 
 def turn_adjoint_kernel(*refs):
-    ins, (own, flat) = refs[:GROUP], refs[GROUP:]
+    ins, (adj, flat) = refs[:GROUP], refs[GROUP:]
     gather_pieces(ins, flat)
     for field in range(Q):
         for row in range(ROWS):
-            own[row, field] = flat[field, pl.ds(row, 8, stride=ROWS), :]
-
-
-def forward_kernel(own_a, own_b, adj_a, adj_b, lo_a, lo_b, hi_a, hi_b, lam_ref, sens_ref, mom1, mom2, rs_ref, up, down, p0, p1, p2, a4):
+            adj[row, field] = flat[field, pl.ds(row, 8, stride=ROWS), :]
+
+
+def stream_pull(source, row, sign):
+    return [shifted(source[row + 1 - sign * VELOCITIES[i][1], i], i, sign) for i in range(Q)]
+
+
+def place(target, own_half, packed, number, reach):
+    target[:, :128] = own_half
+    target[:, 128:] = unpack_strip(packed, number, reach)
+
+
+def forward_kernel(
+    own_a, own_b, adj_a, adj_b, lo_a, lo_b, hi_a, hi_b, lam_ref, sens_ref, mom1, mom2, rs_ref, up, down, p0, p1, p2, a4
+):
+    def target(field, row):
+        if field < Q:
+            return p0.at[row + 3, field]
+        return rs_ref.at[row + 2, field - RES] if field < ADJ else a4.at[row + 1, field - ADJ]
+
     for side, own, adj in ((0, own_a, adj_a), (1, own_b, adj_b)):
         lanes = slice(128 * side, 128 * side + 128)
-        for row in range(ROWS):
-            for i in range(Q):
-                p0[row + 3, i, :, lanes] = own[row, i]
-                a4[row + 1, i, :, lanes] = adj[row, i]
-            for j in range(2):
-                rs_ref[row + 2, j, :, lanes] = own[row, RES + j]
+        for row, field in OWN:
+            target(field, row)[:, lanes] = own[row, field]
+        for row, field in OWN_ADJOINT:
+            target(ADJ + field, row)[:, lanes] = adj[row, field]
     for table, parts in ((FORWARD_UP, (lo_a, lo_b)), (FORWARD_DOWN, (hi_a, hi_b))):
         for side, part in enumerate(parts):
-            lanes = slice(128 * side, 128 * side + 128)
             for number, (_, field, row) in enumerate(table):
-                if field < Q:
-                    p0[row + 3, field, :, lanes] = part[number]
-                elif field < ADJ:
-                    rs_ref[row + 2, field - RES, :, lanes] = part[number]
-                else:
-                    a4[row + 1, field - ADJ, :, lanes] = part[number]
-
-    def pull(source, row):
-        return [shifted(source[row + 1 - VELOCITIES[i][1], i], i, 1) for i in range(Q)]
-
-    def first(row):
-        f = pull(p0, row)
+                target(field, row)[:, slice(128 * side, 128 * side + 128)] = part[number]
+    for row in range(ROWS + 4):
+        f = stream_pull(p0, row, 1)
         moment = moments(f)
         for j in range(4):
             mom1[row, j] = moment[j]
         out = collide_lists(f, *moment, rs_ref[row, 0], rs_ref[row, 1] == 1.0)
         for i in inward(row, ROWS + 3, 1):
             p1[row, i] = out[i]
-
-    for row in range(ROWS + 4):
-        first(row)
-
-    def second(row):
-        f = pull(p1, row)
+    for row in range(ROWS + 2):
+        f = stream_pull(p1, row, 1)
         moment = moments(f)
         for j in range(4):
-            mom2[row + 1, j] = moment[j]
+            mom2[row, j] = moment[j]
         out = collide_lists(f, *moment, rs_ref[row + 1, 0], rs_ref[row + 1, 1] == 1.0)
         for i in inward(row, ROWS + 1, 1):
             p2[row, i] = out[i]
-
-    for row in range(ROWS + 2):
-        second(row)
-
-    def third(row):
-        moment = moments(pull(p2, row))
-        mu = [shifted(a4[row + 1 + VELOCITIES[i][1], i], i, -1) for i in range(Q)]
+    for row in range(ROWS):
+        moment = moments(stream_pull(p2, row, 1))
+        mu = stream_pull(a4, row, -1)
         out, design = adjoint_lists(mu, *moment, rs_ref[row + 2, 0], rs_ref[row + 2, 1] == 1.0)
         for i in range(Q):
             lam_ref[row, i] = out[i]
         sens_ref[row] = design[:, :128]
-
-    for row in range(ROWS):
-        third(row)
     for table, part in ((BACKWARD_UP, up), (BACKWARD_DOWN, down)):
         others = []
         for number, (row, field, _) in enumerate(table):
-            source = lam_ref[row, field] if field < Q else mom2[row + 2, field - Q]
+            source = lam_ref[row, field] if field < Q else mom2[row + 1, field - Q]
             part[number] = source[:, :128]
             others.append(source[:, 128:])
-        for number, tile in enumerate(pack_strips(others)):
+        for number, tile in enumerate(pack_strips(others, BACKWARD_REACH)):
             part[len(table) + number] = tile
-    for row in (0, ROWS + 3):
-        for j in range(4):
-            mom2[row, j] = jnp.zeros((8, 256), jnp.float32)
-
-
-def backward_kernel(lam_ref, sens_ref, mom1, mom2, rs_ref, lo, hi, *refs):
+
+
+def inner_backward_kernel(lam_ref, sens_ref, mom2, rs_ref, l2, sens_out):
+    for row in (0, ROWS - 1):
+        sens_out[row] = sens_ref[row]
+    for row in range(ROWS - 2):
+        mu = stream_pull(lam_ref, row, -1)
+        moment = [mom2[row + 2, j] for j in range(4)]
+        out, design = adjoint_lists(mu, *moment, rs_ref[row + 3, 0], rs_ref[row + 3, 1] == 1.0)
+        for i in range(Q):
+            l2[row, i] = out[i]
+        sens_out[row + 1] = sens_ref[row + 1] + design[:, :128]
+
+
+def backward_kernel(lam_ref, sens_ref, mom1, mom2, rs_ref, l2_inner, lo, hi, *refs):
     outs, (l3, l2, l1, m2, flat) = refs[:GROUP], refs[GROUP:]
     for row in range(ROWS):
         for i in range(Q):
             l3[row + 3, i] = lam_ref[row, i]
-    for row in range(ROWS + 4):
+    for row in range(ROWS + 2):
         for j in range(4):
-            m2[row, j] = mom2[row, j]
+            m2[row + 1, j] = mom2[row, j]
     for table, part in ((BACKWARD_UP, lo), (BACKWARD_DOWN, hi)):
-        packed = [part[len(table) + number] for number in range(strip_count(table))]
+        packed = [part[len(table) + number] for number in range(strip_count(table, BACKWARD_REACH))]
         for number, (_, field, row) in enumerate(table):
             target = l3.at[row + 3, field] if field < Q else m2.at[row + 2, field - Q]
-            target[:, :128] = part[number]
-            target[:, 128:] = unpack_strip(packed[number // SLOTS], number)
-
-    def pull(source, row):
-        return [shifted(source[row + 1 + VELOCITIES[i][1], i], i, -1) for i in range(Q)]
-
-    designs = {}
-
-    def second(row):
-        mu = pull(l3, row)
+            place(target, part[number], packed, number, BACKWARD_REACH)
+    designs = [sens_ref[row] for row in range(ROWS)]
+    for row in range(ROWS + 4):
+        if 3 <= row < ROWS + 1:
+            for i in range(Q):
+                l2[row, i] = l2_inner[row - 3, i]
+            continue
+        mu = stream_pull(l3, row, -1)
         out, design = adjoint_lists(mu, *[m2[row, j] for j in range(4)], rs_ref[row, 0], rs_ref[row, 1] == 1.0)
         for i in inward(row, ROWS + 3, -1):
             l2[row, i] = out[i]
         if 2 <= row < ROWS + 2:
-            designs[row - 2] = design
-
-    for row in range(ROWS + 4):
-        second(row)
-
-    def first(row):
-        mu = pull(l2, row)
-        out, design = adjoint_lists(
-            mu, *[mom1[row + 1, j] for j in range(4)], rs_ref[row + 1, 0], rs_ref[row + 1, 1] == 1.0
-        )
+            designs[row - 2] = designs[row - 2] + design[:, :128]
+    for row in range(ROWS + 2):
+        mu = stream_pull(l2, row, -1)
+        moment = [mom1[row + 1, j] for j in range(4)]
+        out, design = adjoint_lists(mu, *moment, rs_ref[row + 1, 0], rs_ref[row + 1, 1] == 1.0)
         for i in inward(row, ROWS + 1, -1):
             l1[row, i] = out[i]
         if 1 <= row < ROWS + 1:
-            designs[row - 1] = designs[row - 1] + design
-
-    for row in range(ROWS + 2):
-        first(row)
+            designs[row - 1] = designs[row - 1] + design[:, :128]
     for row in range(ROWS):
-        flat[Q, pl.ds(row, 8, stride=ROWS), :] = sens_ref[row] + designs[row][:, :128]
-        mu = pull(l1, row)
+        flat[Q, pl.ds(row, 8, stride=ROWS), :] = designs[row]
+        mu = stream_pull(l1, row, -1)
         for i in range(Q):
             flat[i, pl.ds(row, 8, stride=ROWS), :] = mu[i][:, :128]
     here = lax.axis_index("gx")
@@ -503,39 +500,27 @@
             (ROWS, Q, 8, 256),
             (ROWS, 8, 128),
             (ROWS + 4, 4, 8, 256),
-            (ROWS + 4, 4, 8, 256),
+            (ROWS + 2, 4, 8, 256),
             (ROWS + 4, 2, 8, 256),
-            (len(BACKWARD_UP) + strip_count(BACKWARD_UP), 8, 128),
-            (len(BACKWARD_DOWN) + strip_count(BACKWARD_DOWN), 8, 128),
+            (len(BACKWARD_UP) + strip_count(BACKWARD_UP, BACKWARD_REACH), 8, 128),
+            (len(BACKWARD_DOWN) + strip_count(BACKWARD_DOWN, BACKWARD_REACH), 8, 128),
         ],
         [(ROWS + 6, Q, 8, 256), (ROWS + 4, Q, 8, 256), (ROWS + 2, Q, 8, 256), (ROWS + 2, Q, 8, 256)],
-        own,
-        own_b,
-        adj,
-        adj_b,
-        lo,
-        lo_b,
-        hi,
-        hi_b,
+        *(own, own_b, adj, adj_b, lo, lo_b, hi, hi_b),
     )
     lo, hi = ring(up, down)
+    l2_inner, sens = call(inner_backward_kernel, [(2, Q, 8, 256), (ROWS, 8, 128)], [], lam, sens, mom2, rs)
     pieces = call(
         backward_kernel,
         [(Q + 1, 8, 128)] * GROUP,
         [
             (ROWS + 6, Q, 8, 256),
             (ROWS + 4, Q, 8, 256),
-            (ROWS + 4, Q, 8, 256),
+            (ROWS + 2, Q, 8, 256),
             (ROWS + 4, 4, 8, 256),
             (Q + 1, 8 * ROWS, 128),
         ],
-        lam,
-        sens,
-        mom1,
-        mom2,
-        rs,
-        lo,
-        hi,
+        *(lam, sens, mom1, mom2, rs, l2_inner, lo, hi),
     )
     pieces = trade(pieces)
     return tuple(

time: 39.9 us -> 39.8 us (level)
    pallas_call x7 -> x8, Pallas kernels: 5.76 us -> 5.82 us  [call(): pl.pallas_call(kernel, out_shape=[jax.ShapeDtypeStruct(shape, jnp.float32...]
  transfers between devices with their start and end apart: 17 -> 17, of which waited for: 8 -> 8; matrix products, arithmetic and copies ran while one was open for 0% -> 0% of each run, Pallas kernels for 3% -> 4%
where the time goes in v4:
time: 39.8 us; the launch traced here: 39.6 us
  starting transfers between devices  20.1 us (51%)
  waiting for transfers between devices  12.9 us (32%)
  Pallas kernels  5.82 us (15%)
  between operations  0.74 us (2%)
    ppermute x9, starting transfers between devices, trade(): moved[k] = lax.ppermute(pieces[k], 'gx', [(i, i ^ k) for i in range(GROUP)])  11.8 us
    ppermute x2, waiting for transfers between devices, ring(): lo = lax.ppermute(up, ('gx', 'gy'), ring_pairs(planes, 1))  7.33 us
    ppermute x2, starting transfers between devices, ring(): hi = lax.ppermute(down, ('gx', 'gy'), ring_pairs(planes, -1))  6.99 us
    pallas_call x8, Pallas kernels, call(): pl.pallas_call(kernel, out_shape=[jax.ShapeDtypeStruct(shape, jnp.float32...  5.82 us
    ppermute x9, waiting for transfers between devices, trade(): moved[k] = lax.ppermute(pieces[k], 'gx', [(i, i ^ k) for i in range(GROUP)])  4.34 us
    ppermute x4, waiting for transfers between devices, swap(): return lax.ppermute(value, 'gz', [(0, 1), (1, 0)])  1.2 us
  transfers between devices with their start and end apart: 17, of which 8 were waited for; matrix products, arithmetic and copies ran while one was open for 0% of the time, Pallas kernels for 4%

profile of v4, /device:TPU:0, one launch (start us, length us, event | category | flops | bytes accessed | tf_op | source)
XLA Modules:
  0.0 39.6 jit_solution(15653378527897273746)
XLA Ops:
  0.6 1.2 %shard_map.59 = (f32[24,8,128]{2,1,0:T(8,128)S(1)}, f32[24,8,128]{2,1,0:T(8,128)S(1)}, f32[24,8,128]{2,1,0:T(8,128)S(1)}, f32[24,8,128]{2,1,0:T(8,128)S(1)}) custom-call(f32[19,2,16,128]{3,2,1,0:T(8,128)} %f_ref.1, f32[2,16,128]{2,1,0:T(8,128)} %r_ref.1, s32[2,16,128]{2,1,0:T(8,128)} %s_ref.1, f32[19,2,16,128]{3,2,1,0:T(8,128)} %a_hbm), custom_call_target="tpu_custom_call" | custom-call | tf_op jit(solution)/shard_map/pallas_call | solution.py:431
  1.9 3.0 %collective-permute-start = (f32[24,8,128]{2,1,0:T(8,128)S(1)}, f32[24,8,128]{2,1,0:T(8,128)S(1)}, u32[]{:S(2)}, u32[]{:S(2)}) collective-permute-start(f32[24,8,128]{2,1,0:T(8,128)S(1)} %get-tuple-element.36), channel_id=1, source_target_pairs={{0,8},{8,0},{16,24},{24,16},{1,9},{9,1},{17,25},{25,17},{2,10},{10... | collective-permute-start | bytes 294920 | tf_op jit(solution)/shard_map/ppermute | solution.py:456
  4.9 1.5 %collective-permute-start.1 = (f32[24,8,128]{2,1,0:T(8,128)S(1)}, f32[24,8,128]{2,1,0:T(8,128)S(1)}, u32[]{:S(2)}, u32[]{:S(2)}) collective-permute-start(f32[24,8,128]{2,1,0:T(8,128)S(1)} %get-tuple-element.37), channel_id=1, source_target_pairs={{0,16},{8,24},{16,0},{24,8},{1,17},{9,25},{17,1},{25,9},{2,18},{10... | collective-permute-start | bytes 294920 | tf_op jit(solution)/shard_map/ppermute | solution.py:456
  6.4 0.0 collective-permute-start.2
  6.4 1.0 %shard_map.61 = (f32[19,8,128]{2,1,0:T(8,128)S(1)}, f32[19,8,128]{2,1,0:T(8,128)S(1)}, f32[19,8,128]{2,1,0:T(8,128)S(1)}, f32[19,8,128]{2,1,0:T(8,128)S(1)}) custom-call(f32[19,2,16,128]{3,2,1,0:T(8,128)} %a_hbm), custom_call_target="tpu_custom_call" | custom-call | tf_op jit(solution)/shard_map/pallas_call | solution.py:431
  7.4 2.0 %collective-permute-start.4 = (f32[19,8,128]{2,1,0:T(8,128)S(1)}, f32[19,8,128]{2,1,0:T(8,128)S(1)}, u32[]{:S(2)}, u32[]{:S(2)}) collective-permute-start(f32[19,8,128]{2,1,0:T(8,128)S(1)} %get-tuple-element.42), channel_id=1, source_target_pairs={{0,8},{8,0},{16,24},{24,16},{1,9},{9,1},{17,25},{25,17},{2,10},{10... | collective-permute-start | bytes 233480 | tf_op jit(solution)/shard_map/ppermute | solution.py:456
  9.5 1.5 %collective-permute-start.5 = (f32[19,8,128]{2,1,0:T(8,128)S(1)}, f32[19,8,128]{2,1,0:T(8,128)S(1)}, u32[]{:S(2)}, u32[]{:S(2)}) collective-permute-start(f32[19,8,128]{2,1,0:T(8,128)S(1)} %get-tuple-element.43), channel_id=1, source_target_pairs={{0,16},{8,24},{16,0},{24,8},{1,17},{9,25},{17,1},{25,9},{2,18},{10... | collective-permute-start | bytes 233480 | tf_op jit(solution)/shard_map/ppermute | solution.py:456
  11.0 0.0 collective-permute-done.refs_1_
  11.0 0.2 collective-permute-start.6
  11.2 0.0 collective-permute-done.1.refs_2_
  11.2 1.3 %collective-permute-done.2.refs_3_ = f32[24,8,128]{2,1,0:T(8,128)S(1)} collective-permute-done((f32[24,8,128]{2,1,0:T(8,128)S(1)}, f32[24,8,128]{2,1,0:T(8,128)S(1)}, u32[]{:S(2)}, u32[]{:S(2)}) %collective-permute-start.2) | collective-permute-done | bytes 98336 | tf_op jit(solution)/shard_map/ppermute | solution.py:456
  12.5 0.1 shard_map.60
  12.6 0.5 %collective-permute-start.8 = (f32[47,8,128]{2,1,0:T(8,128)S(1)}, f32[47,8,128]{2,1,0:T(8,128)S(1)}, u32[]{:S(2)}, u32[]{:S(2)}) collective-permute-start(f32[47,8,128]{2,1,0:T(8,128)S(1)} %get-tuple-element.45), channel_id=1, source_target_pairs={{0,16},{16,24},{24,8},{8,10},{10,2},{2,18},{18,26},{26,28},{28,12}... | collective-permute-start | bytes 577544 | tf_op jit(solution)/shard_map/ppermute | solution.py:463
  13.2 3.3 %collective-permute-start.10 = (f32[47,8,128]{2,1,0:T(8,128)S(1)}, f32[47,8,128]{2,1,0:T(8,128)S(1)}, u32[]{:S(2)}, u32[]{:S(2)}) collective-permute-start(f32[47,8,128]{2,1,0:T(8,128)S(1)} %get-tuple-element.46), channel_id=1, source_target_pairs={{0,6},{16,0},{24,16},{8,24},{10,8},{2,10},{18,2},{26,18},{28,26},{... | collective-permute-start | bytes 577544 | tf_op jit(solution)/shard_map/ppermute | solution.py:464
  16.5 0.0 collective-permute-done.4.refs_1_
  16.5 0.0 collective-permute-start.3
  16.5 0.0 collective-permute-done.5.refs_2_
  16.5 0.6 %collective-permute-done.6.refs_3_ = f32[19,8,128]{2,1,0:T(8,128)S(1)} collective-permute-done((f32[19,8,128]{2,1,0:T(8,128)S(1)}, f32[19,8,128]{2,1,0:T(8,128)S(1)}, u32[]{:S(2)}, u32[]{:S(2)}) %collective-permute-start.6) | collective-permute-done | bytes 77856 | tf_op jit(solution)/shard_map/ppermute | solution.py:456
  17.1 0.1 shard_map.62.adj_a
  17.2 0.1 collective-permute-start.7
  17.2 2.9 %collective-permute-done.8.lo_a = f32[47,8,128]{2,1,0:T(8,128)S(1)} collective-permute-done((f32[47,8,128]{2,1,0:T(8,128)S(1)}, f32[47,8,128]{2,1,0:T(8,128)S(1)}, u32[]{:S(2)}, u32[]{:S(2)}) %collective-permute-start.8) | collective-permute-done | bytes 192544 | tf_op jit(solution)/shard_map/ppermute | solution.py:463
  20.1 0.0 collective-permute-start.9
  20.1 0.0 collective-permute-done.10.hi_a
  20.1 0.5 %collective-permute-start.11 = (f32[47,8,128]{2,1,0:T(8,128)S(1)}, f32[47,8,128]{2,1,0:T(8,128)S(1)}, u32[]{:S(2)}, u32[]{:S(2)}) collective-permute-start(f32[47,8,128]{2,1,0:T(8,128)S(1)} %collective-permute-done.10.hi_a), channel_id=1, source_target_pairs={{0,1},{1,0},{2,3},{3,2},{4,5},{5,4},{6,7},{7,6},{8,9},{9,8},{10,11... | collective-permute-start | bytes 577544 | tf_op jit(solution)/shard_map/ppermute | solution.py:460
  20.6 0.0 collective-permute-done.7.adj_b
  20.6 0.0 collective-permute-done.3.own_b
  20.6 0.9 %collective-permute-done.9.lo_b = f32[47,8,128]{2,1,0:T(8,128)S(1)} collective-permute-done((f32[47,8,128]{2,1,0:T(8,128)S(1)}, f32[47,8,128]{2,1,0:T(8,128)S(1)}, u32[]{:S(2)}, u32[]{:S(2)}) %collective-permute-start.9) | collective-permute-done | bytes 192544 | tf_op jit(solution)/shard_map/ppermute | solution.py:460
  21.5 0.3 collective-permute-done.11.hi_b
  21.8 1.3 %shard_map.63 = (f32[4,19,8,256]{3,2,1,0:T(8,128)S(1)}, f32[4,8,128]{2,1,0:T(8,128)S(1)}, f32[8,4,8,256]{3,2,1,0:T(8,128)S(1)}, f32[6,4,8,256]{3,2,1,0:T(8,128)S...) custom-call(f32[4,21,8,128]{3,2,1,0:T(8,128)S(1)} %get-tuple-element.39.own_a, ...), custom_call_target="tpu_custom_call" | custom-call | tf_op jit(solution)/shard_map/pallas_call | solution.py:431
  23.1 0.2 collective-permute-start.12
  23.4 3.7 %collective-permute-start.13 = (f32[44,8,128]{2,1,0:T(8,128)S(1)}, f32[44,8,128]{2,1,0:T(8,128)S(1)}, u32[]{:S(2)}, u32[]{:S(2)}) collective-permute-start(f32[44,8,128]{2,1,0:T(8,128)S(1)} %get-tuple-element.55), channel_id=1, source_target_pairs={{0,6},{16,0},{24,16},{8,24},{10,8},{2,10},{18,2},{26,18},{28,26},{... | collective-permute-start | bytes 540680 | tf_op jit(solution)/shard_map/ppermute | solution.py:464
  27.0 0.2 shard_map.64
  27.2 4.5 %collective-permute-done.12.lo = f32[44,8,128]{2,1,0:T(8,128)S(1)} collective-permute-done((f32[44,8,128]{2,1,0:T(8,128)S(1)}, f32[44,8,128]{2,1,0:T(8,128)S(1)}, u32[]{:S(2)}, u32[]{:S(2)}) %collective-permute-start.12) | collective-permute-done | bytes 180256 | tf_op jit(solution)/shard_map/ppermute | solution.py:463
  31.7 0.0 collective-permute-done.13.hi
  31.7 0.0 copy-start
  31.7 0.0 copy-start.1
  31.7 0.0 copy-start.2
  31.7 1.0 %shard_map.65 = (f32[20,8,128]{2,1,0:T(8,128)S(1)}, f32[20,8,128]{2,1,0:T(8,128)S(1)}, f32[20,8,128]{2,1,0:T(8,128)S(1)}, f32[20,8,128]{2,1,0:T(8,128)S(1)}) custom-call(f32[4,19,8,256]{3,2,1,0:T(8,128)S(1)} %get-tuple-element.47.lam_ref, f32[4,8,128]{2,1,0:T(8,128)S(1)} %get-tuple-element.51.sens_ref, f32[8,4,8,256]{3,2,1,0:T(8,128)S(1)} %get-tuple-element.52.mom1, ...), custom_call_target="tpu_custom_call" | custom-call | tf_op jit(solution)/shard_map/pallas_call | solution.py:431
  32.7 0.1 collective-permute-start.14
  32.7 0.1 collective-permute-start.15
  32.8 3.4 %collective-permute-start.16 = (f32[20,8,128]{2,1,0:T(8,128)S(1)}, f32[20,8,128]{2,1,0:T(8,128)S(1)}, u32[]{:S(2)}, u32[]{:S(2)}) collective-permute-start(f32[20,8,128]{2,1,0:T(8,128)S(1)} %get-tuple-element.59), channel_id=1, source_target_pairs={{0,24},{8,16},{16,8},{24,0},{1,25},{9,17},{17,9},{25,1},{2,26},{10... | collective-permute-start | bytes 245768 | tf_op jit(solution)/shard_map/ppermute | solution.py:456
  36.2 1.5 %collective-permute-done.14.refs_1_ = f32[20,8,128]{2,1,0:T(8,128)S(1)} collective-permute-done((f32[20,8,128]{2,1,0:T(8,128)S(1)}, f32[20,8,128]{2,1,0:T(8,128)S(1)}, u32[]{:S(2)}, u32[]{:S(2)}) %collective-permute-start.14) | collective-permute-done | bytes 81952 | tf_op jit(solution)/shard_map/ppermute | solution.py:456
  37.8 0.0 collective-permute-done.15.refs_2_
  37.8 0.9 %collective-permute-done.16.refs_3_ = f32[20,8,128]{2,1,0:T(8,128)S(1)} collective-permute-done((f32[20,8,128]{2,1,0:T(8,128)S(1)}, f32[20,8,128]{2,1,0:T(8,128)S(1)}, u32[]{:S(2)}, u32[]{:S(2)}) %collective-permute-start.16) | collective-permute-done | bytes 81952 | tf_op jit(solution)/shard_map/ppermute | solution.py:456
  38.6 0.0 copy-done
  38.6 0.0 copy-done.1
  38.6 0.0 copy-done.2
  38.6 0.9 %shard_map.66 = (f32[19,2,16,128]{3,2,1,0:T(8,128)}, f32[2,16,128]{2,1,0:T(8,128)}) custom-call(f32[19,2,16,128]{3,2,1,0:T(8,128)S(1)} %copy-done, f32[2,16,128]{2,1,0:T(8,128)S(1)} %copy-done.1, s32[2,16,128]{2,1,0:T(8,128)S(1)} %copy-done.2, f32[20,8,128]{2,1,0:T(8,128)S(1)} %get-tuple-element.56.refs_0_, ...), custom_call_target="tpu_custom_call" | custom-call | tf_op jit(solution)/shard_map/pallas_call | solution.py:431
Async XLA Ops:
  1.9 9.1 %collective-permute-start = (f32[24,8,128]{2,1,0:T(8,128)S(1)}, f32[24,8,128]{2,1,0:T(8,128)S(1)}, u32[]{:S(2)}, u32[]{:S(2)}) collective-permute-start(f32[24,8,128]{2,1,0:T(8,128)S(1)} %get-tuple-element.36), channel_id=1, source_target_pairs={{0,8},{8,0},{16,24},{24,16},{1,9},{9,1},{17,25},{25,17},{2,10},{10... | collective-permute-start | bytes 294920 | tf_op jit(solution)/shard_map/ppermute | solution.py:456
  4.9 6.3 %collective-permute-start.1 = (f32[24,8,128]{2,1,0:T(8,128)S(1)}, f32[24,8,128]{2,1,0:T(8,128)S(1)}, u32[]{:S(2)}, u32[]{:S(2)}) collective-permute-start(f32[24,8,128]{2,1,0:T(8,128)S(1)} %get-tuple-element.37), channel_id=1, source_target_pairs={{0,16},{8,24},{16,0},{24,8},{1,17},{9,25},{17,1},{25,9},{2,18},{10... | collective-permute-start | bytes 294920 | tf_op jit(solution)/shard_map/ppermute | solution.py:456
  6.4 6.1 %collective-permute-start.2 = (f32[24,8,128]{2,1,0:T(8,128)S(1)}, f32[24,8,128]{2,1,0:T(8,128)S(1)}, u32[]{:S(2)}, u32[]{:S(2)}) collective-permute-start(f32[24,8,128]{2,1,0:T(8,128)S(1)} %get-tuple-element.38), channel_id=1, source_target_pairs={{0,24},{8,16},{16,8},{24,0},{1,25},{9,17},{17,9},{25,1},{2,26},{10... | collective-permute-start | bytes 294920 | tf_op jit(solution)/shard_map/ppermute | solution.py:456
  7.4 9.1 %collective-permute-start.4 = (f32[19,8,128]{2,1,0:T(8,128)S(1)}, f32[19,8,128]{2,1,0:T(8,128)S(1)}, u32[]{:S(2)}, u32[]{:S(2)}) collective-permute-start(f32[19,8,128]{2,1,0:T(8,128)S(1)} %get-tuple-element.42), channel_id=1, source_target_pairs={{0,8},{8,0},{16,24},{24,16},{1,9},{9,1},{17,25},{25,17},{2,10},{10... | collective-permute-start | bytes 233480 | tf_op jit(solution)/shard_map/ppermute | solution.py:456
  9.5 7.0 %collective-permute-start.5 = (f32[19,8,128]{2,1,0:T(8,128)S(1)}, f32[19,8,128]{2,1,0:T(8,128)S(1)}, u32[]{:S(2)}, u32[]{:S(2)}) collective-permute-start(f32[19,8,128]{2,1,0:T(8,128)S(1)} %get-tuple-element.43), channel_id=1, source_target_pairs={{0,16},{8,24},{16,0},{24,8},{1,17},{9,25},{17,1},{25,9},{2,18},{10... | collective-permute-start | bytes 233480 | tf_op jit(solution)/shard_map/ppermute | solution.py:456
  11.0 6.1 %collective-permute-start.6 = (f32[19,8,128]{2,1,0:T(8,128)S(1)}, f32[19,8,128]{2,1,0:T(8,128)S(1)}, u32[]{:S(2)}, u32[]{:S(2)}) collective-permute-start(f32[19,8,128]{2,1,0:T(8,128)S(1)} %get-tuple-element.44), channel_id=1, source_target_pairs={{0,24},{8,16},{16,8},{24,0},{1,25},{9,17},{17,9},{25,1},{2,26},{10... | collective-permute-start | bytes 233480 | tf_op jit(solution)/shard_map/ppermute | solution.py:456
  12.6 7.5 %collective-permute-start.8 = (f32[47,8,128]{2,1,0:T(8,128)S(1)}, f32[47,8,128]{2,1,0:T(8,128)S(1)}, u32[]{:S(2)}, u32[]{:S(2)}) collective-permute-start(f32[47,8,128]{2,1,0:T(8,128)S(1)} %get-tuple-element.45), channel_id=1, source_target_pairs={{0,16},{16,24},{24,8},{8,10},{10,2},{2,18},{18,26},{26,28},{28,12}... | collective-permute-start | bytes 577544 | tf_op jit(solution)/shard_map/ppermute | solution.py:463
  13.2 7.0 %collective-permute-start.10 = (f32[47,8,128]{2,1,0:T(8,128)S(1)}, f32[47,8,128]{2,1,0:T(8,128)S(1)}, u32[]{:S(2)}, u32[]{:S(2)}) collective-permute-start(f32[47,8,128]{2,1,0:T(8,128)S(1)} %get-tuple-element.46), channel_id=1, source_target_pairs={{0,6},{16,0},{24,16},{8,24},{10,8},{2,10},{18,2},{26,18},{28,26},{... | collective-permute-start | bytes 577544 | tf_op jit(solution)/shard_map/ppermute | solution.py:464
  16.5 4.1 %collective-permute-start.3 = (f32[4,21,8,128]{3,2,1,0:T(8,128)S(1)}, f32[4,21,8,128]{3,2,1,0:T(8,128)S(1)}, u32[]{:S(2)}, u32[]{:S(2)}) collective-permute-start(f32[4,21,8,128]{3,2,1,0:T(8,128)S(1)} %get-tuple-element.39.own_a), channel_id=1, source_target_pairs={{0,1},{1,0},{2,3},{3,2},{4,5},{5,4},{6,7},{7,6},{8,9},{9,8},{10,11... | collective-permute-start | bytes 1032200 | tf_op jit(solution)/shard_map/ppermute | solution.py:460
  17.2 3.4 %collective-permute-start.7 = (f32[4,19,8,128]{3,2,1,0:T(8,128)S(1)}, f32[4,19,8,128]{3,2,1,0:T(8,128)S(1)}, u32[]{:S(2)}, u32[]{:S(2)}) collective-permute-start(f32[4,19,8,128]{3,2,1,0:T(8,128)S(1)} %shard_map.62.adj_a), channel_id=1, source_target_pairs={{0,1},{1,0},{2,3},{3,2},{4,5},{5,4},{6,7},{7,6},{8,9},{9,8},{10,11... | collective-permute-start | bytes 933896 | tf_op jit(solution)/shard_map/ppermute | solution.py:460
  20.1 1.4 %collective-permute-start.9 = (f32[47,8,128]{2,1,0:T(8,128)S(1)}, f32[47,8,128]{2,1,0:T(8,128)S(1)}, u32[]{:S(2)}, u32[]{:S(2)}) collective-permute-start(f32[47,8,128]{2,1,0:T(8,128)S(1)} %collective-permute-done.8.lo_a), channel_id=1, source_target_pairs={{0,1},{1,0},{2,3},{3,2},{4,5},{5,4},{6,7},{7,6},{8,9},{9,8},{10,11... | collective-permute-start | bytes 577544 | tf_op jit(solution)/shard_map/ppermute | solution.py:460
  20.1 1.7 %collective-permute-start.11 = (f32[47,8,128]{2,1,0:T(8,128)S(1)}, f32[47,8,128]{2,1,0:T(8,128)S(1)}, u32[]{:S(2)}, u32[]{:S(2)}) collective-permute-start(f32[47,8,128]{2,1,0:T(8,128)S(1)} %collective-permute-done.10.hi_a), channel_id=1, source_target_pairs={{0,1},{1,0},{2,3},{3,2},{4,5},{5,4},{6,7},{7,6},{8,9},{9,8},{10,11... | collective-permute-start | bytes 577544 | tf_op jit(solution)/shard_map/ppermute | solution.py:460
  23.1 8.5 %collective-permute-start.12 = (f32[44,8,128]{2,1,0:T(8,128)S(1)}, f32[44,8,128]{2,1,0:T(8,128)S(1)}, u32[]{:S(2)}, u32[]{:S(2)}) collective-permute-start(f32[44,8,128]{2,1,0:T(8,128)S(1)} %get-tuple-element.54), channel_id=1, source_target_pairs={{0,16},{16,24},{24,8},{8,10},{10,2},{2,18},{18,26},{26,28},{28,12}... | collective-permute-start | bytes 540680 | tf_op jit(solution)/shard_map/ppermute | solution.py:463
  23.4 8.3 %collective-permute-start.13 = (f32[44,8,128]{2,1,0:T(8,128)S(1)}, f32[44,8,128]{2,1,0:T(8,128)S(1)}, u32[]{:S(2)}, u32[]{:S(2)}) collective-permute-start(f32[44,8,128]{2,1,0:T(8,128)S(1)} %get-tuple-element.55), channel_id=1, source_target_pairs={{0,6},{16,0},{24,16},{8,24},{10,8},{2,10},{18,2},{26,18},{28,26},{... | collective-permute-start | bytes 540680 | tf_op jit(solution)/shard_map/ppermute | solution.py:464
  31.7 6.9 %copy-start = (f32[19,2,16,128]{3,2,1,0:T(8,128)S(1)}, f32[19,2,16,128]{3,2,1,0:T(8,128)}, u32[]{:S(2)}) copy-start(f32[19,2,16,128]{3,2,1,0:T(8,128)} %f_ref.1) | copy-start | bytes 933892
  31.7 6.9 %copy-start.1 = (f32[2,16,128]{2,1,0:T(8,128)S(1)}, f32[2,16,128]{2,1,0:T(8,128)}, u32[]{:S(2)}) copy-start(f32[2,16,128]{2,1,0:T(8,128)} %r_ref.1) | copy-start | bytes 49156
  31.7 6.9 %copy-start.2 = (s32[2,16,128]{2,1,0:T(8,128)S(1)}, s32[2,16,128]{2,1,0:T(8,128)}, u32[]{:S(2)}) copy-start(s32[2,16,128]{2,1,0:T(8,128)} %s_ref.1) | copy-start | bytes 49156
  32.7 5.1 %collective-permute-start.14 = (f32[20,8,128]{2,1,0:T(8,128)S(1)}, f32[20,8,128]{2,1,0:T(8,128)S(1)}, u32[]{:S(2)}, u32[]{:S(2)}) collective-permute-start(f32[20,8,128]{2,1,0:T(8,128)S(1)} %get-tuple-element.57), channel_id=1, source_target_pairs={{0,8},{8,0},{16,24},{24,16},{1,9},{9,1},{17,25},{25,17},{2,10},{10... | collective-permute-start | bytes 245768 | tf_op jit(solution)/shard_map/ppermute | solution.py:456
  32.7 5.0 %collective-permute-start.15 = (f32[20,8,128]{2,1,0:T(8,128)S(1)}, f32[20,8,128]{2,1,0:T(8,128)S(1)}, u32[]{:S(2)}, u32[]{:S(2)}) collective-permute-start(f32[20,8,128]{2,1,0:T(8,128)S(1)} %get-tuple-element.58), channel_id=1, source_target_pairs={{0,16},{8,24},{16,0},{24,8},{1,17},{9,25},{17,1},{25,9},{2,18},{10... | collective-permute-start | bytes 245768 | tf_op jit(solution)/shard_map/ppermute | solution.py:456
  32.8 5.8 %collective-permute-start.16 = (f32[20,8,128]{2,1,0:T(8,128)S(1)}, f32[20,8,128]{2,1,0:T(8,128)S(1)}, u32[]{:S(2)}, u32[]{:S(2)}) collective-permute-start(f32[20,8,128]{2,1,0:T(8,128)S(1)} %get-tuple-element.59), channel_id=1, source_target_pairs={{0,24},{8,16},{16,8},{24,0},{1,25},{9,17},{17,9},{25,1},{2,26},{10... | collective-permute-start | bytes 245768 | tf_op jit(solution)/shard_map/ppermute | solution.py:456

commit v5 on v4

--- a/solution.py
+++ b/solution.py
@@ -44,7 +44,7 @@
 GROUP = 4
 ROWS = 4
 LAYERS = 2
-TRADES = (1, 3, 2)
+TRADES = (0, 3, 2, 1)
 FORWARD_REACH, BACKWARD_REACH = 6, 3
 RES, SOL, ADJ = Q, Q + 1, Q + 2
 DOWNWARD = [i for i in range(Q) if VELOCITIES[i][1] > 0]
@@ -240,8 +240,8 @@
                         rows.append(a_ref[i, layer, pl.ds(ROWS * block + row, 1), :])
             blocks[block, ADJ + edge] = jnp.concatenate(rows, axis=0)
     here = lax.axis_index("gx")
-    for k in range(GROUP):
-        outs[k][...] = blocks[block_of(here ^ k)]
+    for k, out in zip(TRADES, outs):
+        out[...] = blocks[block_of(here ^ k)]
 
 
 def send_adjoint_kernel(a_hbm, *refs):
@@ -253,16 +253,16 @@
         for i in range(Q):
             blocks[block, i] = jnp.concatenate([a_ref[i, layer, pl.ds(4 * block, 4), :] for layer in range(LAYERS)], axis=0)
     here = lax.axis_index("gx")
-    for k in range(GROUP):
-        outs[k][...] = blocks[block_of(here ^ k)]
+    for k, out in zip(TRADES, outs):
+        out[...] = blocks[block_of(here ^ k)]
 
 
 def gather_pieces(ins, flat):
     here = lax.axis_index("gx")
-    for k in range(GROUP):
+    for k, piece in zip(TRADES, ins):
         start = 8 * (here ^ k)
         for field in range(flat.shape[0]):
-            flat[field, pl.ds(pl.multiple_of(start, 8), 8), :] = ins[k][field]
+            flat[field, pl.ds(pl.multiple_of(start, 8), 8), :] = piece[field]
 
 
 def turn_kernel(*refs):
@@ -400,17 +400,17 @@
         for i in range(Q):
             flat[i, pl.ds(row, 8, stride=ROWS), :] = mu[i][:, :128]
     here = lax.axis_index("gx")
-    for k in range(GROUP):
+    for k, out in zip(TRADES, outs):
         start = 8 * (here ^ k)
         for i in range(Q + 1):
-            outs[k][i] = flat[i, pl.ds(pl.multiple_of(start, 8), 8), :]
+            out[i] = flat[i, pl.ds(pl.multiple_of(start, 8), 8), :]
 
 
 def finish_kernel(f_ref, r_ref, s_ref, *refs):
     ins, (lam_ref, sens_ref, blocks) = refs[:GROUP], refs[GROUP:]
     here = lax.axis_index("gx")
-    for k in range(GROUP):
-        blocks[block_of(here ^ k)] = ins[k][...]
+    for k, piece in zip(TRADES, ins):
+        blocks[block_of(here ^ k)] = piece[...]
     for half in range(2):
         rows = pl.ds(8 * half, 8)
         for layer in range(LAYERS):
@@ -451,9 +451,9 @@
     planes = lax.axis_size("gy")
 
     def trade(pieces):
-        moved = list(pieces)
-        for k in TRADES:
-            moved[k] = lax.ppermute(pieces[k], "gx", [(i, i ^ k) for i in range(GROUP)])
+        moved = [pieces[0]]
+        for number, k in enumerate(TRADES[1:], 1):
+            moved.append(lax.ppermute(pieces[number], "gx", [(i, i ^ k) for i in range(GROUP)]))
         return moved
 
     def swap(value):

time: 39.8 us -> 39 us (0.980)
  waiting for transfers between devices: 12.9 us -> 11.6 us
  starting transfers between devices: 20.1 us -> 20.7 us
    ppermute x2, starting transfers between devices: 0.76 us -> 2.81 us  [ring(): lo = lax.ppermute(up, ('gx', 'gy'), ring_pairs(planes, 1))]
    ppermute x2, starting transfers between devices: 6.99 us -> 4.97 us  [ring(): hi = lax.ppermute(down, ('gx', 'gy'), ring_pairs(planes, -1))]
    ppermute x9, waiting for transfers between devices: 4.34 us -> 2.89 us  [trade(): lax.ppermute(pieces[number], 'gx', [(i, i ^ k) for i in range(GROUP)])]
    ppermute x4, starting transfers between devices: 0.58 us -> 1.08 us  [swap(): return lax.ppermute(value, 'gz', [(0, 1), (1, 0)])]
where the time goes in v5:
time: 39 us; the launch traced here: 38.8 us
  starting transfers between devices  20.7 us (53%)
  waiting for transfers between devices  11.6 us (30%)
  Pallas kernels  5.82 us (15%)
  between operations  0.72 us (2%)
    ppermute x9, starting transfers between devices, trade(): lax.ppermute(pieces[number], 'gx', [(i, i ^ k) for i in range(GROUP)])  11.8 us
    ppermute x2, waiting for transfers between devices, ring(): lo = lax.ppermute(up, ('gx', 'gy'), ring_pairs(planes, 1))  7.47 us
    pallas_call x8, Pallas kernels, call(): pl.pallas_call(kernel, out_shape=[jax.ShapeDtypeStruct(shape, jnp.float32...  5.82 us
    ppermute x2, starting transfers between devices, ring(): hi = lax.ppermute(down, ('gx', 'gy'), ring_pairs(planes, -1))  4.97 us
    ppermute x9, waiting for transfers between devices, trade(): lax.ppermute(pieces[number], 'gx', [(i, i ^ k) for i in range(GROUP)])  2.89 us
    ppermute x2, starting transfers between devices, ring(): lo = lax.ppermute(up, ('gx', 'gy'), ring_pairs(planes, 1))  2.81 us
    ppermute x4, waiting for transfers between devices, swap(): return lax.ppermute(value, 'gz', [(0, 1), (1, 0)])  1.2 us
    ppermute x4, starting transfers between devices, swap(): return lax.ppermute(value, 'gz', [(0, 1), (1, 0)])  1.08 us
  transfers between devices with their start and end apart: 17, of which 8 were waited for; matrix products, arithmetic and copies ran while one was open for 0% of the time, Pallas kernels for 4%

profile of v5, /device:TPU:0, one launch (start us, length us, event | category | flops | bytes accessed | tf_op | source)
XLA Modules:
  0.0 38.8 jit_solution(9701473312715609885)
XLA Ops:
  0.6 1.2 %shard_map.59 = (f32[24,8,128]{2,1,0:T(8,128)S(1)}, f32[24,8,128]{2,1,0:T(8,128)S(1)}, f32[24,8,128]{2,1,0:T(8,128)S(1)}, f32[24,8,128]{2,1,0:T(8,128)S(1)}) custom-call(f32[19,2,16,128]{3,2,1,0:T(8,128)} %f_ref.1, f32[2,16,128]{2,1,0:T(8,128)} %r_ref.1, s32[2,16,128]{2,1,0:T(8,128)} %s_ref.1, f32[19,2,16,128]{3,2,1,0:T(8,128)} %a_hbm), custom_call_target="tpu_custom_call" | custom-call | tf_op jit(solution)/shard_map/pallas_call | solution.py:431
  1.9 4.0 %collective-permute-start = (f32[24,8,128]{2,1,0:T(8,128)S(1)}, f32[24,8,128]{2,1,0:T(8,128)S(1)}, u32[]{:S(2)}, u32[]{:S(2)}) collective-permute-start(f32[24,8,128]{2,1,0:T(8,128)S(1)} %get-tuple-element.36), channel_id=1, source_target_pairs={{0,24},{8,16},{16,8},{24,0},{1,25},{9,17},{17,9},{25,1},{2,26},{10... | collective-permute-start | bytes 294920 | tf_op jit(solution)/shard_map/ppermute | solution.py:456
  5.8 0.5 %collective-permute-start.1 = (f32[24,8,128]{2,1,0:T(8,128)S(1)}, f32[24,8,128]{2,1,0:T(8,128)S(1)}, u32[]{:S(2)}, u32[]{:S(2)}) collective-permute-start(f32[24,8,128]{2,1,0:T(8,128)S(1)} %get-tuple-element.37), channel_id=1, source_target_pairs={{0,16},{8,24},{16,0},{24,8},{1,17},{9,25},{17,1},{25,9},{2,18},{10... | collective-permute-start | bytes 294920 | tf_op jit(solution)/shard_map/ppermute | solution.py:456
  6.3 0.1 collective-permute-start.2
  6.5 1.0 %shard_map.61 = (f32[19,8,128]{2,1,0:T(8,128)S(1)}, f32[19,8,128]{2,1,0:T(8,128)S(1)}, f32[19,8,128]{2,1,0:T(8,128)S(1)}, f32[19,8,128]{2,1,0:T(8,128)S(1)}) custom-call(f32[19,2,16,128]{3,2,1,0:T(8,128)} %a_hbm), custom_call_target="tpu_custom_call" | custom-call | tf_op jit(solution)/shard_map/pallas_call | solution.py:431
  7.5 2.9 %collective-permute-start.4 = (f32[19,8,128]{2,1,0:T(8,128)S(1)}, f32[19,8,128]{2,1,0:T(8,128)S(1)}, u32[]{:S(2)}, u32[]{:S(2)}) collective-permute-start(f32[19,8,128]{2,1,0:T(8,128)S(1)} %get-tuple-element.42), channel_id=1, source_target_pairs={{0,24},{8,16},{16,8},{24,0},{1,25},{9,17},{17,9},{25,1},{2,26},{10... | collective-permute-start | bytes 233480 | tf_op jit(solution)/shard_map/ppermute | solution.py:456
  10.4 0.5 %collective-permute-start.5 = (f32[19,8,128]{2,1,0:T(8,128)S(1)}, f32[19,8,128]{2,1,0:T(8,128)S(1)}, u32[]{:S(2)}, u32[]{:S(2)}) collective-permute-start(f32[19,8,128]{2,1,0:T(8,128)S(1)} %get-tuple-element.43), channel_id=1, source_target_pairs={{0,16},{8,24},{16,0},{24,8},{1,17},{9,25},{17,1},{25,9},{2,18},{10... | collective-permute-start | bytes 233480 | tf_op jit(solution)/shard_map/ppermute | solution.py:456
  10.9 0.0 collective-permute-done.refs_1_
  10.9 0.2 collective-permute-start.6
  11.2 0.4 collective-permute-done.1.refs_2_
  11.5 0.1 collective-permute-done.2.refs_3_
  11.6 0.1 shard_map.60
  11.7 1.9 %collective-permute-start.8 = (f32[47,8,128]{2,1,0:T(8,128)S(1)}, f32[47,8,128]{2,1,0:T(8,128)S(1)}, u32[]{:S(2)}, u32[]{:S(2)}) collective-permute-start(f32[47,8,128]{2,1,0:T(8,128)S(1)} %get-tuple-element.45), channel_id=1, source_target_pairs={{0,16},{16,24},{24,8},{8,10},{10,2},{2,18},{18,26},{26,28},{28,12}... | collective-permute-start | bytes 577544 | tf_op jit(solution)/shard_map/ppermute | solution.py:463
  13.6 2.0 %collective-permute-start.10 = (f32[47,8,128]{2,1,0:T(8,128)S(1)}, f32[47,8,128]{2,1,0:T(8,128)S(1)}, u32[]{:S(2)}, u32[]{:S(2)}) collective-permute-start(f32[47,8,128]{2,1,0:T(8,128)S(1)} %get-tuple-element.46), channel_id=1, source_target_pairs={{0,6},{16,0},{24,16},{8,24},{10,8},{2,10},{18,2},{26,18},{28,26},{... | collective-permute-start | bytes 577544 | tf_op jit(solution)/shard_map/ppermute | solution.py:464
  15.6 0.0 collective-permute-done.4.refs_1_
  15.6 0.0 collective-permute-start.3
  15.6 0.0 collective-permute-done.5.refs_2_
  15.7 0.0 collective-permute-done.6.refs_3_
  15.7 0.1 shard_map.62.adj_a
  15.7 0.6 %collective-permute-start.7 = (f32[4,19,8,128]{3,2,1,0:T(8,128)S(1)}, f32[4,19,8,128]{3,2,1,0:T(8,128)S(1)}, u32[]{:S(2)}, u32[]{:S(2)}) collective-permute-start(f32[4,19,8,128]{3,2,1,0:T(8,128)S(1)} %shard_map.62.adj_a), channel_id=1, source_target_pairs={{0,1},{1,0},{2,3},{3,2},{4,5},{5,4},{6,7},{7,6},{8,9},{9,8},{10,11... | collective-permute-start | bytes 933896 | tf_op jit(solution)/shard_map/ppermute | solution.py:460
  16.3 3.0 %collective-permute-done.8.lo_a = f32[47,8,128]{2,1,0:T(8,128)S(1)} collective-permute-done((f32[47,8,128]{2,1,0:T(8,128)S(1)}, f32[47,8,128]{2,1,0:T(8,128)S(1)}, u32[]{:S(2)}, u32[]{:S(2)}) %collective-permute-start.8) | collective-permute-done | bytes 192544 | tf_op jit(solution)/shard_map/ppermute | solution.py:463
  19.3 0.0 collective-permute-start.9
  19.3 0.0 collective-permute-done.10.hi_a
  19.3 0.5 %collective-permute-start.11 = (f32[47,8,128]{2,1,0:T(8,128)S(1)}, f32[47,8,128]{2,1,0:T(8,128)S(1)}, u32[]{:S(2)}, u32[]{:S(2)}) collective-permute-start(f32[47,8,128]{2,1,0:T(8,128)S(1)} %collective-permute-done.10.hi_a), channel_id=1, source_target_pairs={{0,1},{1,0},{2,3},{3,2},{4,5},{5,4},{6,7},{7,6},{8,9},{9,8},{10,11... | collective-permute-start | bytes 577544 | tf_op jit(solution)/shard_map/ppermute | solution.py:460
  19.8 0.0 collective-permute-done.7.adj_b
  19.8 0.0 collective-permute-done.3.own_b
  19.8 0.9 %collective-permute-done.9.lo_b = f32[47,8,128]{2,1,0:T(8,128)S(1)} collective-permute-done((f32[47,8,128]{2,1,0:T(8,128)S(1)}, f32[47,8,128]{2,1,0:T(8,128)S(1)}, u32[]{:S(2)}, u32[]{:S(2)}) %collective-permute-start.9) | collective-permute-done | bytes 192544 | tf_op jit(solution)/shard_map/ppermute | solution.py:460
  20.7 0.3 collective-permute-done.11.hi_b
  21.0 1.3 %shard_map.63 = (f32[4,19,8,256]{3,2,1,0:T(8,128)S(1)}, f32[4,8,128]{2,1,0:T(8,128)S(1)}, f32[8,4,8,256]{3,2,1,0:T(8,128)S(1)}, f32[6,4,8,256]{3,2,1,0:T(8,128)S...) custom-call(f32[4,21,8,128]{3,2,1,0:T(8,128)S(1)} %get-tuple-element.39.own_a, ...), custom_call_target="tpu_custom_call" | custom-call | tf_op jit(solution)/shard_map/pallas_call | solution.py:431
  22.3 0.9 %collective-permute-start.12 = (f32[44,8,128]{2,1,0:T(8,128)S(1)}, f32[44,8,128]{2,1,0:T(8,128)S(1)}, u32[]{:S(2)}, u32[]{:S(2)}) collective-permute-start(f32[44,8,128]{2,1,0:T(8,128)S(1)} %get-tuple-element.54), channel_id=1, source_target_pairs={{0,16},{16,24},{24,8},{8,10},{10,2},{2,18},{18,26},{26,28},{28,12}... | collective-permute-start | bytes 540680 | tf_op jit(solution)/shard_map/ppermute | solution.py:463
  23.3 3.0 %collective-permute-start.13 = (f32[44,8,128]{2,1,0:T(8,128)S(1)}, f32[44,8,128]{2,1,0:T(8,128)S(1)}, u32[]{:S(2)}, u32[]{:S(2)}) collective-permute-start(f32[44,8,128]{2,1,0:T(8,128)S(1)} %get-tuple-element.55), channel_id=1, source_target_pairs={{0,6},{16,0},{24,16},{8,24},{10,8},{2,10},{18,2},{26,18},{28,26},{... | collective-permute-start | bytes 540680 | tf_op jit(solution)/shard_map/ppermute | solution.py:464
  26.2 0.2 shard_map.64
  26.4 4.5 %collective-permute-done.12.lo = f32[44,8,128]{2,1,0:T(8,128)S(1)} collective-permute-done((f32[44,8,128]{2,1,0:T(8,128)S(1)}, f32[44,8,128]{2,1,0:T(8,128)S(1)}, u32[]{:S(2)}, u32[]{:S(2)}) %collective-permute-start.12) | collective-permute-done | bytes 180256 | tf_op jit(solution)/shard_map/ppermute | solution.py:463
  30.9 0.0 collective-permute-done.13.hi
  30.9 0.0 copy-start
  30.9 0.0 copy-start.1
  30.9 0.0 copy-start.2
  30.9 1.0 %shard_map.65 = (f32[20,8,128]{2,1,0:T(8,128)S(1)}, f32[20,8,128]{2,1,0:T(8,128)S(1)}, f32[20,8,128]{2,1,0:T(8,128)S(1)}, f32[20,8,128]{2,1,0:T(8,128)S(1)}) custom-call(f32[4,19,8,256]{3,2,1,0:T(8,128)S(1)} %get-tuple-element.47.lam_ref, f32[4,8,128]{2,1,0:T(8,128)S(1)} %get-tuple-element.51.sens_ref, f32[8,4,8,256]{3,2,1,0:T(8,128)S(1)} %get-tuple-element.52.mom1, ...), custom_call_target="tpu_custom_call" | custom-call | tf_op jit(solution)/shard_map/pallas_call | solution.py:431
  31.9 0.6 %collective-permute-start.14 = (f32[20,8,128]{2,1,0:T(8,128)S(1)}, f32[20,8,128]{2,1,0:T(8,128)S(1)}, u32[]{:S(2)}, u32[]{:S(2)}) collective-permute-start(f32[20,8,128]{2,1,0:T(8,128)S(1)} %get-tuple-element.57), channel_id=1, source_target_pairs={{0,24},{8,16},{16,8},{24,0},{1,25},{9,17},{17,9},{25,1},{2,26},{10... | collective-permute-start | bytes 245768 | tf_op jit(solution)/shard_map/ppermute | solution.py:456
  32.5 0.7 %collective-permute-start.15 = (f32[20,8,128]{2,1,0:T(8,128)S(1)}, f32[20,8,128]{2,1,0:T(8,128)S(1)}, u32[]{:S(2)}, u32[]{:S(2)}) collective-permute-start(f32[20,8,128]{2,1,0:T(8,128)S(1)} %get-tuple-element.58), channel_id=1, source_target_pairs={{0,16},{8,24},{16,0},{24,8},{1,17},{9,25},{17,1},{25,9},{2,18},{10... | collective-permute-start | bytes 245768 | tf_op jit(solution)/shard_map/ppermute | solution.py:456
  33.2 2.2 %collective-permute-start.16 = (f32[20,8,128]{2,1,0:T(8,128)S(1)}, f32[20,8,128]{2,1,0:T(8,128)S(1)}, u32[]{:S(2)}, u32[]{:S(2)}) collective-permute-start(f32[20,8,128]{2,1,0:T(8,128)S(1)} %get-tuple-element.59), channel_id=1, source_target_pairs={{0,8},{8,0},{16,24},{24,16},{1,9},{9,1},{17,25},{25,17},{2,10},{10... | collective-permute-start | bytes 245768 | tf_op jit(solution)/shard_map/ppermute | solution.py:456
  35.4 2.2 %collective-permute-done.14.refs_1_ = f32[20,8,128]{2,1,0:T(8,128)S(1)} collective-permute-done((f32[20,8,128]{2,1,0:T(8,128)S(1)}, f32[20,8,128]{2,1,0:T(8,128)S(1)}, u32[]{:S(2)}, u32[]{:S(2)}) %collective-permute-start.14) | collective-permute-done | bytes 81952 | tf_op jit(solution)/shard_map/ppermute | solution.py:456
  37.6 0.2 collective-permute-done.15.refs_2_
  37.8 0.0 collective-permute-done.16.refs_3_
  37.8 0.0 copy-done
  37.8 0.0 copy-done.1
  37.8 0.0 copy-done.2
  37.8 0.9 %shard_map.66 = (f32[19,2,16,128]{3,2,1,0:T(8,128)}, f32[2,16,128]{2,1,0:T(8,128)}) custom-call(f32[19,2,16,128]{3,2,1,0:T(8,128)S(1)} %copy-done, f32[2,16,128]{2,1,0:T(8,128)S(1)} %copy-done.1, s32[2,16,128]{2,1,0:T(8,128)S(1)} %copy-done.2, f32[20,8,128]{2,1,0:T(8,128)S(1)} %get-tuple-element.56.refs_0_, ...), custom_call_target="tpu_custom_call" | custom-call | tf_op jit(solution)/shard_map/pallas_call | solution.py:431
Async XLA Ops:
  1.9 9.1 %collective-permute-start = (f32[24,8,128]{2,1,0:T(8,128)S(1)}, f32[24,8,128]{2,1,0:T(8,128)S(1)}, u32[]{:S(2)}, u32[]{:S(2)}) collective-permute-start(f32[24,8,128]{2,1,0:T(8,128)S(1)} %get-tuple-element.36), channel_id=1, source_target_pairs={{0,24},{8,16},{16,8},{24,0},{1,25},{9,17},{17,9},{25,1},{2,26},{10... | collective-permute-start | bytes 294920 | tf_op jit(solution)/shard_map/ppermute | solution.py:456
  5.8 5.7 %collective-permute-start.1 = (f32[24,8,128]{2,1,0:T(8,128)S(1)}, f32[24,8,128]{2,1,0:T(8,128)S(1)}, u32[]{:S(2)}, u32[]{:S(2)}) collective-permute-start(f32[24,8,128]{2,1,0:T(8,128)S(1)} %get-tuple-element.37), channel_id=1, source_target_pairs={{0,16},{8,24},{16,0},{24,8},{1,17},{9,25},{17,1},{25,9},{2,18},{10... | collective-permute-start | bytes 294920 | tf_op jit(solution)/shard_map/ppermute | solution.py:456
  6.3 5.3 %collective-permute-start.2 = (f32[24,8,128]{2,1,0:T(8,128)S(1)}, f32[24,8,128]{2,1,0:T(8,128)S(1)}, u32[]{:S(2)}, u32[]{:S(2)}) collective-permute-start(f32[24,8,128]{2,1,0:T(8,128)S(1)} %get-tuple-element.38), channel_id=1, source_target_pairs={{0,8},{8,0},{16,24},{24,16},{1,9},{9,1},{17,25},{25,17},{2,10},{10... | collective-permute-start | bytes 294920 | tf_op jit(solution)/shard_map/ppermute | solution.py:456
  7.5 8.1 %collective-permute-start.4 = (f32[19,8,128]{2,1,0:T(8,128)S(1)}, f32[19,8,128]{2,1,0:T(8,128)S(1)}, u32[]{:S(2)}, u32[]{:S(2)}) collective-permute-start(f32[19,8,128]{2,1,0:T(8,128)S(1)} %get-tuple-element.42), channel_id=1, source_target_pairs={{0,24},{8,16},{16,8},{24,0},{1,25},{9,17},{17,9},{25,1},{2,26},{10... | collective-permute-start | bytes 233480 | tf_op jit(solution)/shard_map/ppermute | solution.py:456
  10.4 5.2 %collective-permute-start.5 = (f32[19,8,128]{2,1,0:T(8,128)S(1)}, f32[19,8,128]{2,1,0:T(8,128)S(1)}, u32[]{:S(2)}, u32[]{:S(2)}) collective-permute-start(f32[19,8,128]{2,1,0:T(8,128)S(1)} %get-tuple-element.43), channel_id=1, source_target_pairs={{0,16},{8,24},{16,0},{24,8},{1,17},{9,25},{17,1},{25,9},{2,18},{10... | collective-permute-start | bytes 233480 | tf_op jit(solution)/shard_map/ppermute | solution.py:456
  10.9 4.7 %collective-permute-start.6 = (f32[19,8,128]{2,1,0:T(8,128)S(1)}, f32[19,8,128]{2,1,0:T(8,128)S(1)}, u32[]{:S(2)}, u32[]{:S(2)}) collective-permute-start(f32[19,8,128]{2,1,0:T(8,128)S(1)} %get-tuple-element.44), channel_id=1, source_target_pairs={{0,8},{8,0},{16,24},{24,16},{1,9},{9,1},{17,25},{25,17},{2,10},{10... | collective-permute-start | bytes 233480 | tf_op jit(solution)/shard_map/ppermute | solution.py:456
  11.7 7.6 %collective-permute-start.8 = (f32[47,8,128]{2,1,0:T(8,128)S(1)}, f32[47,8,128]{2,1,0:T(8,128)S(1)}, u32[]{:S(2)}, u32[]{:S(2)}) collective-permute-start(f32[47,8,128]{2,1,0:T(8,128)S(1)} %get-tuple-element.45), channel_id=1, source_target_pairs={{0,16},{16,24},{24,8},{8,10},{10,2},{2,18},{18,26},{26,28},{28,12}... | collective-permute-start | bytes 577544 | tf_op jit(solution)/shard_map/ppermute | solution.py:463
  13.6 5.7 %collective-permute-start.10 = (f32[47,8,128]{2,1,0:T(8,128)S(1)}, f32[47,8,128]{2,1,0:T(8,128)S(1)}, u32[]{:S(2)}, u32[]{:S(2)}) collective-permute-start(f32[47,8,128]{2,1,0:T(8,128)S(1)} %get-tuple-element.46), channel_id=1, source_target_pairs={{0,6},{16,0},{24,16},{8,24},{10,8},{2,10},{18,2},{26,18},{28,26},{... | collective-permute-start | bytes 577544 | tf_op jit(solution)/shard_map/ppermute | solution.py:464
  15.6 4.2 %collective-permute-start.3 = (f32[4,21,8,128]{3,2,1,0:T(8,128)S(1)}, f32[4,21,8,128]{3,2,1,0:T(8,128)S(1)}, u32[]{:S(2)}, u32[]{:S(2)}) collective-permute-start(f32[4,21,8,128]{3,2,1,0:T(8,128)S(1)} %get-tuple-element.39.own_a), channel_id=1, source_target_pairs={{0,1},{1,0},{2,3},{3,2},{4,5},{5,4},{6,7},{7,6},{8,9},{9,8},{10,11... | collective-permute-start | bytes 1032200 | tf_op jit(solution)/shard_map/ppermute | solution.py:460
  15.7 4.1 %collective-permute-start.7 = (f32[4,19,8,128]{3,2,1,0:T(8,128)S(1)}, f32[4,19,8,128]{3,2,1,0:T(8,128)S(1)}, u32[]{:S(2)}, u32[]{:S(2)}) collective-permute-start(f32[4,19,8,128]{3,2,1,0:T(8,128)S(1)} %shard_map.62.adj_a), channel_id=1, source_target_pairs={{0,1},{1,0},{2,3},{3,2},{4,5},{5,4},{6,7},{7,6},{8,9},{9,8},{10,11... | collective-permute-start | bytes 933896 | tf_op jit(solution)/shard_map/ppermute | solution.py:460
  19.3 1.4 %collective-permute-start.9 = (f32[47,8,128]{2,1,0:T(8,128)S(1)}, f32[47,8,128]{2,1,0:T(8,128)S(1)}, u32[]{:S(2)}, u32[]{:S(2)}) collective-permute-start(f32[47,8,128]{2,1,0:T(8,128)S(1)} %collective-permute-done.8.lo_a), channel_id=1, source_target_pairs={{0,1},{1,0},{2,3},{3,2},{4,5},{5,4},{6,7},{7,6},{8,9},{9,8},{10,11... | collective-permute-start | bytes 577544 | tf_op jit(solution)/shard_map/ppermute | solution.py:460
  19.3 1.7 %collective-permute-start.11 = (f32[47,8,128]{2,1,0:T(8,128)S(1)}, f32[47,8,128]{2,1,0:T(8,128)S(1)}, u32[]{:S(2)}, u32[]{:S(2)}) collective-permute-start(f32[47,8,128]{2,1,0:T(8,128)S(1)} %collective-permute-done.10.hi_a), channel_id=1, source_target_pairs={{0,1},{1,0},{2,3},{3,2},{4,5},{5,4},{6,7},{7,6},{8,9},{9,8},{10,11... | collective-permute-start | bytes 577544 | tf_op jit(solution)/shard_map/ppermute | solution.py:460
  22.3 8.5 %collective-permute-start.12 = (f32[44,8,128]{2,1,0:T(8,128)S(1)}, f32[44,8,128]{2,1,0:T(8,128)S(1)}, u32[]{:S(2)}, u32[]{:S(2)}) collective-permute-start(f32[44,8,128]{2,1,0:T(8,128)S(1)} %get-tuple-element.54), channel_id=1, source_target_pairs={{0,16},{16,24},{24,8},{8,10},{10,2},{2,18},{18,26},{26,28},{28,12}... | collective-permute-start | bytes 540680 | tf_op jit(solution)/shard_map/ppermute | solution.py:463
  23.3 7.6 %collective-permute-start.13 = (f32[44,8,128]{2,1,0:T(8,128)S(1)}, f32[44,8,128]{2,1,0:T(8,128)S(1)}, u32[]{:S(2)}, u32[]{:S(2)}) collective-permute-start(f32[44,8,128]{2,1,0:T(8,128)S(1)} %get-tuple-element.55), channel_id=1, source_target_pairs={{0,6},{16,0},{24,16},{8,24},{10,8},{2,10},{18,2},{26,18},{28,26},{... | collective-permute-start | bytes 540680 | tf_op jit(solution)/shard_map/ppermute | solution.py:464
  30.9 6.9 %copy-start = (f32[19,2,16,128]{3,2,1,0:T(8,128)S(1)}, f32[19,2,16,128]{3,2,1,0:T(8,128)}, u32[]{:S(2)}) copy-start(f32[19,2,16,128]{3,2,1,0:T(8,128)} %f_ref.1) | copy-start | bytes 933892
  30.9 6.9 %copy-start.1 = (f32[2,16,128]{2,1,0:T(8,128)S(1)}, f32[2,16,128]{2,1,0:T(8,128)}, u32[]{:S(2)}) copy-start(f32[2,16,128]{2,1,0:T(8,128)} %r_ref.1) | copy-start | bytes 49156
  30.9 6.9 %copy-start.2 = (s32[2,16,128]{2,1,0:T(8,128)S(1)}, s32[2,16,128]{2,1,0:T(8,128)}, u32[]{:S(2)}) copy-start(s32[2,16,128]{2,1,0:T(8,128)} %s_ref.1) | copy-start | bytes 49156
  31.9 5.7 %collective-permute-start.14 = (f32[20,8,128]{2,1,0:T(8,128)S(1)}, f32[20,8,128]{2,1,0:T(8,128)S(1)}, u32[]{:S(2)}, u32[]{:S(2)}) collective-permute-start(f32[20,8,128]{2,1,0:T(8,128)S(1)} %get-tuple-element.57), channel_id=1, source_target_pairs={{0,24},{8,16},{16,8},{24,0},{1,25},{9,17},{17,9},{25,1},{2,26},{10... | collective-permute-start | bytes 245768 | tf_op jit(solution)/shard_map/ppermute | solution.py:456
  32.5 5.3 %collective-permute-start.15 = (f32[20,8,128]{2,1,0:T(8,128)S(1)}, f32[20,8,128]{2,1,0:T(8,128)S(1)}, u32[]{:S(2)}, u32[]{:S(2)}) collective-permute-start(f32[20,8,128]{2,1,0:T(8,128)S(1)} %get-tuple-element.58), channel_id=1, source_target_pairs={{0,16},{8,24},{16,0},{24,8},{1,17},{9,25},{17,1},{25,9},{2,18},{10... | collective-permute-start | bytes 245768 | tf_op jit(solution)/shard_map/ppermute | solution.py:456
  33.2 4.6 %collective-permute-start.16 = (f32[20,8,128]{2,1,0:T(8,128)S(1)}, f32[20,8,128]{2,1,0:T(8,128)S(1)}, u32[]{:S(2)}, u32[]{:S(2)}) collective-permute-start(f32[20,8,128]{2,1,0:T(8,128)S(1)} %get-tuple-element.59), channel_id=1, source_target_pairs={{0,8},{8,0},{16,24},{24,16},{1,9},{9,1},{17,25},{25,17},{2,10},{10... | collective-permute-start | bytes 245768 | tf_op jit(solution)/shard_map/ppermute | solution.py:456

commit v6 on v5

--- a/solution.py
+++ b/solution.py
@@ -72,13 +72,13 @@
     [(3, i, -1) for i in range(Q)]
     + [(2, i, -2) for i in range(Q) if VELOCITIES[i][1] <= 0]
     + [(1, i, -3) for i in range(Q) if VELOCITIES[i][1] < 0]
-    + [(2, Q + j, -2) for j in range(4)]
+    + [(2, Q + j, -2) for j in range(1, 4)]
 )
 BACKWARD_DOWN = (
     [(0, i, 4) for i in range(Q)]
     + [(1, i, 5) for i in range(Q) if VELOCITIES[i][1] >= 0]
     + [(2, i, 6) for i in range(Q) if VELOCITIES[i][1] > 0]
-    + [(1, Q + j, 5) for j in range(4)]
+    + [(1, Q + j, 5) for j in range(1, 4)]
 )
 
 

time: 39 us -> 38.9 us (level)
  no operation moved by 1% of the time
where the time goes in v6:
time: 38.9 us; the launch traced here: 38.7 us
  starting transfers between devices  20.7 us (53%)
  waiting for transfers between devices  11.5 us (30%)
  Pallas kernels  5.83 us (15%)
  between operations  0.72 us (2%)
    ppermute x9, starting transfers between devices, trade(): lax.ppermute(pieces[number], 'gx', [(i, i ^ k) for i in range(GROUP)])  11.8 us
    ppermute x2, waiting for transfers between devices, ring(): lo = lax.ppermute(up, ('gx', 'gy'), ring_pairs(planes, 1))  7.38 us
    pallas_call x8, Pallas kernels, call(): pl.pallas_call(kernel, out_shape=[jax.ShapeDtypeStruct(shape, jnp.float32...  5.83 us
    ppermute x2, starting transfers between devices, ring(): hi = lax.ppermute(down, ('gx', 'gy'), ring_pairs(planes, -1))  4.97 us
    ppermute x9, waiting for transfers between devices, trade(): lax.ppermute(pieces[number], 'gx', [(i, i ^ k) for i in range(GROUP)])  2.89 us
    ppermute x2, starting transfers between devices, ring(): lo = lax.ppermute(up, ('gx', 'gy'), ring_pairs(planes, 1))  2.81 us
    ppermute x4, waiting for transfers between devices, swap(): return lax.ppermute(value, 'gz', [(0, 1), (1, 0)])  1.2 us
    ppermute x4, starting transfers between devices, swap(): return lax.ppermute(value, 'gz', [(0, 1), (1, 0)])  1.08 us
  transfers between devices with their start and end apart: 17, of which 8 were waited for; matrix products, arithmetic and copies ran while one was open for 0% of the time, Pallas kernels for 4%

profile of v6, /device:TPU:0, one launch (start us, length us, event | category | flops | bytes accessed | tf_op | source)
XLA Modules:
  0.0 38.7 jit_solution(3845566820750888480)
XLA Ops:
  0.6 1.2 %shard_map.59 = (f32[24,8,128]{2,1,0:T(8,128)S(1)}, f32[24,8,128]{2,1,0:T(8,128)S(1)}, f32[24,8,128]{2,1,0:T(8,128)S(1)}, f32[24,8,128]{2,1,0:T(8,128)S(1)}) custom-call(f32[19,2,16,128]{3,2,1,0:T(8,128)} %f_ref.1, f32[2,16,128]{2,1,0:T(8,128)} %r_ref.1, s32[2,16,128]{2,1,0:T(8,128)} %s_ref.1, f32[19,2,16,128]{3,2,1,0:T(8,128)} %a_hbm), custom_call_target="tpu_custom_call" | custom-call | tf_op jit(solution)/shard_map/pallas_call | solution.py:431
  1.9 4.0 %collective-permute-start = (f32[24,8,128]{2,1,0:T(8,128)S(1)}, f32[24,8,128]{2,1,0:T(8,128)S(1)}, u32[]{:S(2)}, u32[]{:S(2)}) collective-permute-start(f32[24,8,128]{2,1,0:T(8,128)S(1)} %get-tuple-element.36), channel_id=1, source_target_pairs={{0,24},{8,16},{16,8},{24,0},{1,25},{9,17},{17,9},{25,1},{2,26},{10... | collective-permute-start | bytes 294920 | tf_op jit(solution)/shard_map/ppermute | solution.py:456
  5.8 0.5 %collective-permute-start.1 = (f32[24,8,128]{2,1,0:T(8,128)S(1)}, f32[24,8,128]{2,1,0:T(8,128)S(1)}, u32[]{:S(2)}, u32[]{:S(2)}) collective-permute-start(f32[24,8,128]{2,1,0:T(8,128)S(1)} %get-tuple-element.37), channel_id=1, source_target_pairs={{0,16},{8,24},{16,0},{24,8},{1,17},{9,25},{17,1},{25,9},{2,18},{10... | collective-permute-start | bytes 294920 | tf_op jit(solution)/shard_map/ppermute | solution.py:456
  6.3 0.1 collective-permute-start.2
  6.5 1.0 %shard_map.61 = (f32[19,8,128]{2,1,0:T(8,128)S(1)}, f32[19,8,128]{2,1,0:T(8,128)S(1)}, f32[19,8,128]{2,1,0:T(8,128)S(1)}, f32[19,8,128]{2,1,0:T(8,128)S(1)}) custom-call(f32[19,2,16,128]{3,2,1,0:T(8,128)} %a_hbm), custom_call_target="tpu_custom_call" | custom-call | tf_op jit(solution)/shard_map/pallas_call | solution.py:431
  7.5 2.9 %collective-permute-start.4 = (f32[19,8,128]{2,1,0:T(8,128)S(1)}, f32[19,8,128]{2,1,0:T(8,128)S(1)}, u32[]{:S(2)}, u32[]{:S(2)}) collective-permute-start(f32[19,8,128]{2,1,0:T(8,128)S(1)} %get-tuple-element.42), channel_id=1, source_target_pairs={{0,24},{8,16},{16,8},{24,0},{1,25},{9,17},{17,9},{25,1},{2,26},{10... | collective-permute-start | bytes 233480 | tf_op jit(solution)/shard_map/ppermute | solution.py:456
  10.4 0.5 %collective-permute-start.5 = (f32[19,8,128]{2,1,0:T(8,128)S(1)}, f32[19,8,128]{2,1,0:T(8,128)S(1)}, u32[]{:S(2)}, u32[]{:S(2)}) collective-permute-start(f32[19,8,128]{2,1,0:T(8,128)S(1)} %get-tuple-element.43), channel_id=1, source_target_pairs={{0,16},{8,24},{16,0},{24,8},{1,17},{9,25},{17,1},{25,9},{2,18},{10... | collective-permute-start | bytes 233480 | tf_op jit(solution)/shard_map/ppermute | solution.py:456
  10.9 0.0 collective-permute-done.refs_1_
  10.9 0.2 collective-permute-start.6
  11.2 0.4 collective-permute-done.1.refs_2_
  11.5 0.1 collective-permute-done.2.refs_3_
  11.6 0.1 shard_map.60
  11.7 1.9 %collective-permute-start.8 = (f32[47,8,128]{2,1,0:T(8,128)S(1)}, f32[47,8,128]{2,1,0:T(8,128)S(1)}, u32[]{:S(2)}, u32[]{:S(2)}) collective-permute-start(f32[47,8,128]{2,1,0:T(8,128)S(1)} %get-tuple-element.45), channel_id=1, source_target_pairs={{0,16},{16,24},{24,8},{8,10},{10,2},{2,18},{18,26},{26,28},{28,12}... | collective-permute-start | bytes 577544 | tf_op jit(solution)/shard_map/ppermute | solution.py:463
  13.6 2.0 %collective-permute-start.10 = (f32[47,8,128]{2,1,0:T(8,128)S(1)}, f32[47,8,128]{2,1,0:T(8,128)S(1)}, u32[]{:S(2)}, u32[]{:S(2)}) collective-permute-start(f32[47,8,128]{2,1,0:T(8,128)S(1)} %get-tuple-element.46), channel_id=1, source_target_pairs={{0,6},{16,0},{24,16},{8,24},{10,8},{2,10},{18,2},{26,18},{28,26},{... | collective-permute-start | bytes 577544 | tf_op jit(solution)/shard_map/ppermute | solution.py:464
  15.6 0.0 collective-permute-done.4.refs_1_
  15.6 0.0 collective-permute-start.3
  15.6 0.0 collective-permute-done.5.refs_2_
  15.7 0.0 collective-permute-done.6.refs_3_
  15.7 0.1 shard_map.62.adj_a
  15.7 0.6 %collective-permute-start.7 = (f32[4,19,8,128]{3,2,1,0:T(8,128)S(1)}, f32[4,19,8,128]{3,2,1,0:T(8,128)S(1)}, u32[]{:S(2)}, u32[]{:S(2)}) collective-permute-start(f32[4,19,8,128]{3,2,1,0:T(8,128)S(1)} %shard_map.62.adj_a), channel_id=1, source_target_pairs={{0,1},{1,0},{2,3},{3,2},{4,5},{5,4},{6,7},{7,6},{8,9},{9,8},{10,11... | collective-permute-start | bytes 933896 | tf_op jit(solution)/shard_map/ppermute | solution.py:460
  16.3 3.0 %collective-permute-done.8.lo_a = f32[47,8,128]{2,1,0:T(8,128)S(1)} collective-permute-done((f32[47,8,128]{2,1,0:T(8,128)S(1)}, f32[47,8,128]{2,1,0:T(8,128)S(1)}, u32[]{:S(2)}, u32[]{:S(2)}) %collective-permute-start.8) | collective-permute-done | bytes 192544 | tf_op jit(solution)/shard_map/ppermute | solution.py:463
  19.3 0.0 collective-permute-start.9
  19.3 0.0 collective-permute-done.10.hi_a
  19.3 0.5 %collective-permute-start.11 = (f32[47,8,128]{2,1,0:T(8,128)S(1)}, f32[47,8,128]{2,1,0:T(8,128)S(1)}, u32[]{:S(2)}, u32[]{:S(2)}) collective-permute-start(f32[47,8,128]{2,1,0:T(8,128)S(1)} %collective-permute-done.10.hi_a), channel_id=1, source_target_pairs={{0,1},{1,0},{2,3},{3,2},{4,5},{5,4},{6,7},{7,6},{8,9},{9,8},{10,11... | collective-permute-start | bytes 577544 | tf_op jit(solution)/shard_map/ppermute | solution.py:460
  19.8 0.0 collective-permute-done.7.adj_b
  19.8 0.0 collective-permute-done.3.own_b
  19.8 0.9 %collective-permute-done.9.lo_b = f32[47,8,128]{2,1,0:T(8,128)S(1)} collective-permute-done((f32[47,8,128]{2,1,0:T(8,128)S(1)}, f32[47,8,128]{2,1,0:T(8,128)S(1)}, u32[]{:S(2)}, u32[]{:S(2)}) %collective-permute-start.9) | collective-permute-done | bytes 192544 | tf_op jit(solution)/shard_map/ppermute | solution.py:460
  20.7 0.3 collective-permute-done.11.hi_b
  21.0 1.3 %shard_map.63 = (f32[4,19,8,256]{3,2,1,0:T(8,128)S(1)}, f32[4,8,128]{2,1,0:T(8,128)S(1)}, f32[8,4,8,256]{3,2,1,0:T(8,128)S(1)}, f32[6,4,8,256]{3,2,1,0:T(8,128)S...) custom-call(f32[4,21,8,128]{3,2,1,0:T(8,128)S(1)} %get-tuple-element.39.own_a, ...), custom_call_target="tpu_custom_call" | custom-call | tf_op jit(solution)/shard_map/pallas_call | solution.py:431
  22.3 0.9 %collective-permute-start.12 = (f32[43,8,128]{2,1,0:T(8,128)S(1)}, f32[43,8,128]{2,1,0:T(8,128)S(1)}, u32[]{:S(2)}, u32[]{:S(2)}) collective-permute-start(f32[43,8,128]{2,1,0:T(8,128)S(1)} %get-tuple-element.54), channel_id=1, source_target_pairs={{0,16},{16,24},{24,8},{8,10},{10,2},{2,18},{18,26},{26,28},{28,12}... | collective-permute-start | bytes 528392 | tf_op jit(solution)/shard_map/ppermute | solution.py:463
  23.3 3.0 %collective-permute-start.13 = (f32[43,8,128]{2,1,0:T(8,128)S(1)}, f32[43,8,128]{2,1,0:T(8,128)S(1)}, u32[]{:S(2)}, u32[]{:S(2)}) collective-permute-start(f32[43,8,128]{2,1,0:T(8,128)S(1)} %get-tuple-element.55), channel_id=1, source_target_pairs={{0,6},{16,0},{24,16},{8,24},{10,8},{2,10},{18,2},{26,18},{28,26},{... | collective-permute-start | bytes 528392 | tf_op jit(solution)/shard_map/ppermute | solution.py:464
  26.2 0.2 shard_map.64
  26.4 4.4 %collective-permute-done.12.lo = f32[43,8,128]{2,1,0:T(8,128)S(1)} collective-permute-done((f32[43,8,128]{2,1,0:T(8,128)S(1)}, f32[43,8,128]{2,1,0:T(8,128)S(1)}, u32[]{:S(2)}, u32[]{:S(2)}) %collective-permute-start.12) | collective-permute-done | bytes 176160 | tf_op jit(solution)/shard_map/ppermute | solution.py:463
  30.8 0.0 collective-permute-done.13.hi
  30.8 0.0 copy-start
  30.8 0.0 copy-start.1
  30.8 0.0 copy-start.2
  30.8 1.0 %shard_map.65 = (f32[20,8,128]{2,1,0:T(8,128)S(1)}, f32[20,8,128]{2,1,0:T(8,128)S(1)}, f32[20,8,128]{2,1,0:T(8,128)S(1)}, f32[20,8,128]{2,1,0:T(8,128)S(1)}) custom-call(f32[4,19,8,256]{3,2,1,0:T(8,128)S(1)} %get-tuple-element.47.lam_ref, f32[4,8,128]{2,1,0:T(8,128)S(1)} %get-tuple-element.51.sens_ref, f32[8,4,8,256]{3,2,1,0:T(8,128)S(1)} %get-tuple-element.52.mom1, ...), custom_call_target="tpu_custom_call" | custom-call | tf_op jit(solution)/shard_map/pallas_call | solution.py:431
  31.8 0.6 %collective-permute-start.14 = (f32[20,8,128]{2,1,0:T(8,128)S(1)}, f32[20,8,128]{2,1,0:T(8,128)S(1)}, u32[]{:S(2)}, u32[]{:S(2)}) collective-permute-start(f32[20,8,128]{2,1,0:T(8,128)S(1)} %get-tuple-element.57), channel_id=1, source_target_pairs={{0,24},{8,16},{16,8},{24,0},{1,25},{9,17},{17,9},{25,1},{2,26},{10... | collective-permute-start | bytes 245768 | tf_op jit(solution)/shard_map/ppermute | solution.py:456
  32.4 0.7 %collective-permute-start.15 = (f32[20,8,128]{2,1,0:T(8,128)S(1)}, f32[20,8,128]{2,1,0:T(8,128)S(1)}, u32[]{:S(2)}, u32[]{:S(2)}) collective-permute-start(f32[20,8,128]{2,1,0:T(8,128)S(1)} %get-tuple-element.58), channel_id=1, source_target_pairs={{0,16},{8,24},{16,0},{24,8},{1,17},{9,25},{17,1},{25,9},{2,18},{10... | collective-permute-start | bytes 245768 | tf_op jit(solution)/shard_map/ppermute | solution.py:456
  33.1 2.2 %collective-permute-start.16 = (f32[20,8,128]{2,1,0:T(8,128)S(1)}, f32[20,8,128]{2,1,0:T(8,128)S(1)}, u32[]{:S(2)}, u32[]{:S(2)}) collective-permute-start(f32[20,8,128]{2,1,0:T(8,128)S(1)} %get-tuple-element.59), channel_id=1, source_target_pairs={{0,8},{8,0},{16,24},{24,16},{1,9},{9,1},{17,25},{25,17},{2,10},{10... | collective-permute-start | bytes 245768 | tf_op jit(solution)/shard_map/ppermute | solution.py:456
  35.3 2.2 %collective-permute-done.14.refs_1_ = f32[20,8,128]{2,1,0:T(8,128)S(1)} collective-permute-done((f32[20,8,128]{2,1,0:T(8,128)S(1)}, f32[20,8,128]{2,1,0:T(8,128)S(1)}, u32[]{:S(2)}, u32[]{:S(2)}) %collective-permute-start.14) | collective-permute-done | bytes 81952 | tf_op jit(solution)/shard_map/ppermute | solution.py:456
  37.5 0.2 collective-permute-done.15.refs_2_
  37.7 0.0 collective-permute-done.16.refs_3_
  37.8 0.0 copy-done
  37.8 0.0 copy-done.1
  37.8 0.0 copy-done.2
  37.8 0.9 %shard_map.66 = (f32[19,2,16,128]{3,2,1,0:T(8,128)}, f32[2,16,128]{2,1,0:T(8,128)}) custom-call(f32[19,2,16,128]{3,2,1,0:T(8,128)S(1)} %copy-done, f32[2,16,128]{2,1,0:T(8,128)S(1)} %copy-done.1, s32[2,16,128]{2,1,0:T(8,128)S(1)} %copy-done.2, f32[20,8,128]{2,1,0:T(8,128)S(1)} %get-tuple-element.56.refs_0_, ...), custom_call_target="tpu_custom_call" | custom-call | tf_op jit(solution)/shard_map/pallas_call | solution.py:431
Async XLA Ops:
  1.9 9.1 %collective-permute-start = (f32[24,8,128]{2,1,0:T(8,128)S(1)}, f32[24,8,128]{2,1,0:T(8,128)S(1)}, u32[]{:S(2)}, u32[]{:S(2)}) collective-permute-start(f32[24,8,128]{2,1,0:T(8,128)S(1)} %get-tuple-element.36), channel_id=1, source_target_pairs={{0,24},{8,16},{16,8},{24,0},{1,25},{9,17},{17,9},{25,1},{2,26},{10... | collective-permute-start | bytes 294920 | tf_op jit(solution)/shard_map/ppermute | solution.py:456
  5.8 5.7 %collective-permute-start.1 = (f32[24,8,128]{2,1,0:T(8,128)S(1)}, f32[24,8,128]{2,1,0:T(8,128)S(1)}, u32[]{:S(2)}, u32[]{:S(2)}) collective-permute-start(f32[24,8,128]{2,1,0:T(8,128)S(1)} %get-tuple-element.37), channel_id=1, source_target_pairs={{0,16},{8,24},{16,0},{24,8},{1,17},{9,25},{17,1},{25,9},{2,18},{10... | collective-permute-start | bytes 294920 | tf_op jit(solution)/shard_map/ppermute | solution.py:456
  6.3 5.3 %collective-permute-start.2 = (f32[24,8,128]{2,1,0:T(8,128)S(1)}, f32[24,8,128]{2,1,0:T(8,128)S(1)}, u32[]{:S(2)}, u32[]{:S(2)}) collective-permute-start(f32[24,8,128]{2,1,0:T(8,128)S(1)} %get-tuple-element.38), channel_id=1, source_target_pairs={{0,8},{8,0},{16,24},{24,16},{1,9},{9,1},{17,25},{25,17},{2,10},{10... | collective-permute-start | bytes 294920 | tf_op jit(solution)/shard_map/ppermute | solution.py:456
  7.5 8.1 %collective-permute-start.4 = (f32[19,8,128]{2,1,0:T(8,128)S(1)}, f32[19,8,128]{2,1,0:T(8,128)S(1)}, u32[]{:S(2)}, u32[]{:S(2)}) collective-permute-start(f32[19,8,128]{2,1,0:T(8,128)S(1)} %get-tuple-element.42), channel_id=1, source_target_pairs={{0,24},{8,16},{16,8},{24,0},{1,25},{9,17},{17,9},{25,1},{2,26},{10... | collective-permute-start | bytes 233480 | tf_op jit(solution)/shard_map/ppermute | solution.py:456
  10.4 5.2 %collective-permute-start.5 = (f32[19,8,128]{2,1,0:T(8,128)S(1)}, f32[19,8,128]{2,1,0:T(8,128)S(1)}, u32[]{:S(2)}, u32[]{:S(2)}) collective-permute-start(f32[19,8,128]{2,1,0:T(8,128)S(1)} %get-tuple-element.43), channel_id=1, source_target_pairs={{0,16},{8,24},{16,0},{24,8},{1,17},{9,25},{17,1},{25,9},{2,18},{10... | collective-permute-start | bytes 233480 | tf_op jit(solution)/shard_map/ppermute | solution.py:456
  10.9 4.7 %collective-permute-start.6 = (f32[19,8,128]{2,1,0:T(8,128)S(1)}, f32[19,8,128]{2,1,0:T(8,128)S(1)}, u32[]{:S(2)}, u32[]{:S(2)}) collective-permute-start(f32[19,8,128]{2,1,0:T(8,128)S(1)} %get-tuple-element.44), channel_id=1, source_target_pairs={{0,8},{8,0},{16,24},{24,16},{1,9},{9,1},{17,25},{25,17},{2,10},{10... | collective-permute-start | bytes 233480 | tf_op jit(solution)/shard_map/ppermute | solution.py:456
  11.7 7.6 %collective-permute-start.8 = (f32[47,8,128]{2,1,0:T(8,128)S(1)}, f32[47,8,128]{2,1,0:T(8,128)S(1)}, u32[]{:S(2)}, u32[]{:S(2)}) collective-permute-start(f32[47,8,128]{2,1,0:T(8,128)S(1)} %get-tuple-element.45), channel_id=1, source_target_pairs={{0,16},{16,24},{24,8},{8,10},{10,2},{2,18},{18,26},{26,28},{28,12}... | collective-permute-start | bytes 577544 | tf_op jit(solution)/shard_map/ppermute | solution.py:463
  13.6 5.7 %collective-permute-start.10 = (f32[47,8,128]{2,1,0:T(8,128)S(1)}, f32[47,8,128]{2,1,0:T(8,128)S(1)}, u32[]{:S(2)}, u32[]{:S(2)}) collective-permute-start(f32[47,8,128]{2,1,0:T(8,128)S(1)} %get-tuple-element.46), channel_id=1, source_target_pairs={{0,6},{16,0},{24,16},{8,24},{10,8},{2,10},{18,2},{26,18},{28,26},{... | collective-permute-start | bytes 577544 | tf_op jit(solution)/shard_map/ppermute | solution.py:464
  15.6 4.2 %collective-permute-start.3 = (f32[4,21,8,128]{3,2,1,0:T(8,128)S(1)}, f32[4,21,8,128]{3,2,1,0:T(8,128)S(1)}, u32[]{:S(2)}, u32[]{:S(2)}) collective-permute-start(f32[4,21,8,128]{3,2,1,0:T(8,128)S(1)} %get-tuple-element.39.own_a), channel_id=1, source_target_pairs={{0,1},{1,0},{2,3},{3,2},{4,5},{5,4},{6,7},{7,6},{8,9},{9,8},{10,11... | collective-permute-start | bytes 1032200 | tf_op jit(solution)/shard_map/ppermute | solution.py:460
  15.7 4.1 %collective-permute-start.7 = (f32[4,19,8,128]{3,2,1,0:T(8,128)S(1)}, f32[4,19,8,128]{3,2,1,0:T(8,128)S(1)}, u32[]{:S(2)}, u32[]{:S(2)}) collective-permute-start(f32[4,19,8,128]{3,2,1,0:T(8,128)S(1)} %shard_map.62.adj_a), channel_id=1, source_target_pairs={{0,1},{1,0},{2,3},{3,2},{4,5},{5,4},{6,7},{7,6},{8,9},{9,8},{10,11... | collective-permute-start | bytes 933896 | tf_op jit(solution)/shard_map/ppermute | solution.py:460
  19.3 1.4 %collective-permute-start.9 = (f32[47,8,128]{2,1,0:T(8,128)S(1)}, f32[47,8,128]{2,1,0:T(8,128)S(1)}, u32[]{:S(2)}, u32[]{:S(2)}) collective-permute-start(f32[47,8,128]{2,1,0:T(8,128)S(1)} %collective-permute-done.8.lo_a), channel_id=1, source_target_pairs={{0,1},{1,0},{2,3},{3,2},{4,5},{5,4},{6,7},{7,6},{8,9},{9,8},{10,11... | collective-permute-start | bytes 577544 | tf_op jit(solution)/shard_map/ppermute | solution.py:460
  19.3 1.7 %collective-permute-start.11 = (f32[47,8,128]{2,1,0:T(8,128)S(1)}, f32[47,8,128]{2,1,0:T(8,128)S(1)}, u32[]{:S(2)}, u32[]{:S(2)}) collective-permute-start(f32[47,8,128]{2,1,0:T(8,128)S(1)} %collective-permute-done.10.hi_a), channel_id=1, source_target_pairs={{0,1},{1,0},{2,3},{3,2},{4,5},{5,4},{6,7},{7,6},{8,9},{9,8},{10,11... | collective-permute-start | bytes 577544 | tf_op jit(solution)/shard_map/ppermute | solution.py:460
  22.3 8.5 %collective-permute-start.12 = (f32[43,8,128]{2,1,0:T(8,128)S(1)}, f32[43,8,128]{2,1,0:T(8,128)S(1)}, u32[]{:S(2)}, u32[]{:S(2)}) collective-permute-start(f32[43,8,128]{2,1,0:T(8,128)S(1)} %get-tuple-element.54), channel_id=1, source_target_pairs={{0,16},{16,24},{24,8},{8,10},{10,2},{2,18},{18,26},{26,28},{28,12}... | collective-permute-start | bytes 528392 | tf_op jit(solution)/shard_map/ppermute | solution.py:463
  23.3 7.5 %collective-permute-start.13 = (f32[43,8,128]{2,1,0:T(8,128)S(1)}, f32[43,8,128]{2,1,0:T(8,128)S(1)}, u32[]{:S(2)}, u32[]{:S(2)}) collective-permute-start(f32[43,8,128]{2,1,0:T(8,128)S(1)} %get-tuple-element.55), channel_id=1, source_target_pairs={{0,6},{16,0},{24,16},{8,24},{10,8},{2,10},{18,2},{26,18},{28,26},{... | collective-permute-start | bytes 528392 | tf_op jit(solution)/shard_map/ppermute | solution.py:464
  30.8 7.0 %copy-start = (f32[19,2,16,128]{3,2,1,0:T(8,128)S(1)}, f32[19,2,16,128]{3,2,1,0:T(8,128)}, u32[]{:S(2)}) copy-start(f32[19,2,16,128]{3,2,1,0:T(8,128)} %f_ref.1) | copy-start | bytes 933892
  30.8 7.0 %copy-start.1 = (f32[2,16,128]{2,1,0:T(8,128)S(1)}, f32[2,16,128]{2,1,0:T(8,128)}, u32[]{:S(2)}) copy-start(f32[2,16,128]{2,1,0:T(8,128)} %r_ref.1) | copy-start | bytes 49156
  30.8 7.0 %copy-start.2 = (s32[2,16,128]{2,1,0:T(8,128)S(1)}, s32[2,16,128]{2,1,0:T(8,128)}, u32[]{:S(2)}) copy-start(s32[2,16,128]{2,1,0:T(8,128)} %s_ref.1) | copy-start | bytes 49156
  31.8 5.7 %collective-permute-start.14 = (f32[20,8,128]{2,1,0:T(8,128)S(1)}, f32[20,8,128]{2,1,0:T(8,128)S(1)}, u32[]{:S(2)}, u32[]{:S(2)}) collective-permute-start(f32[20,8,128]{2,1,0:T(8,128)S(1)} %get-tuple-element.57), channel_id=1, source_target_pairs={{0,24},{8,16},{16,8},{24,0},{1,25},{9,17},{17,9},{25,1},{2,26},{10... | collective-permute-start | bytes 245768 | tf_op jit(solution)/shard_map/ppermute | solution.py:456
  32.4 5.3 %collective-permute-start.15 = (f32[20,8,128]{2,1,0:T(8,128)S(1)}, f32[20,8,128]{2,1,0:T(8,128)S(1)}, u32[]{:S(2)}, u32[]{:S(2)}) collective-permute-start(f32[20,8,128]{2,1,0:T(8,128)S(1)} %get-tuple-element.58), channel_id=1, source_target_pairs={{0,16},{8,24},{16,0},{24,8},{1,17},{9,25},{17,1},{25,9},{2,18},{10... | collective-permute-start | bytes 245768 | tf_op jit(solution)/shard_map/ppermute | solution.py:456
  33.1 4.6 %collective-permute-start.16 = (f32[20,8,128]{2,1,0:T(8,128)S(1)}, f32[20,8,128]{2,1,0:T(8,128)S(1)}, u32[]{:S(2)}, u32[]{:S(2)}) collective-permute-start(f32[20,8,128]{2,1,0:T(8,128)S(1)} %get-tuple-element.59), channel_id=1, source_target_pairs={{0,8},{8,0},{16,24},{24,16},{1,9},{9,1},{17,25},{25,17},{2,10},{10... | collective-permute-start | bytes 245768 | tf_op jit(solution)/shard_map/ppermute | solution.py:456
